TPU v7x, 256 devices: a whole 4x4x8 slice. The times are simulated.
256 devices in a mesh: seq: 32 (over x, z), head: 8 (over y, core).
Axes of the slice: x: 4, y: 4, z: 8, core: 2. Of those that a mesh axis runs over, the one named last changes fastest.
Arguments:
- points: bfloat16 [65536, 512], P(('seq', 'head')), may hold values from -6 to 6
- gain_attn: float32 [512], replicated, may hold values from 0.1 to 1.9
- w_qkv: bfloat16 [512, 1536], replicated
- w_out: bfloat16 [512, 512], replicated, may hold values from -1.1953125 to 1.1953125
- gain_mlp: float32 [512], replicated, may hold values from 0.1 to 1.9
- w_fc1: bfloat16 [512, 2048], P(None, 'head'), may hold values from -0.25 to 0.25
- w_fc2: bfloat16 [2048, 512], P('head'), may hold values from -0.125 to 0.125
- contact_route: int32 [8, 128, 1], P('head'), may hold values from 0 to 7; in each aligned block of 4 rows (0 to 3, 4 to 7, ..., all dimensions but the last counted through in order) at most 2 rows name the same one
- contact_patch: int32 [8, 128], P('head'), may hold values from 0 to 1
- counts: int32 [256], replicated, may hold values from 64 to 256, as said below
Outputs:
- block_out: bfloat16 [65536, 512], P(('seq', 'head'))
Inputs may be any that keep to these rules, and one draw needn't show every extreme that they name: `contact_route`: in each head group, among the 4 contacts of the patches of one seq index, no route value appears more than 2 times. `counts`: some shard is full in every draw.
All inputs are finite; a program needn't handle non-finite values.
Results may differ from a plain program's by a relative error of at most 0.03.
Values may be sent and summed in bfloat16 or wider, within the bound.
A program may use at most 128 MiB of HBM per device.

v0:
```python
import jax
import jax.numpy as jnp
from jax import lax
from jax.sharding import PartitionSpec as P

D = 512
HEADS = 32
HEAD_DIM = 16
PATCH = 1024
CB = 2


def passed_along(value, axis, steps):
    count = lax.axis_size(axis)
    pairs = [(source, (source + steps) % count) for source in range(count)]
    return lax.ppermute(value, axis, pairs)


def layer_norm(values, gain):
    values = values.astype(jnp.float32)
    centred = values - jnp.mean(values, axis=-1, keepdims=True)
    spread = jnp.mean(centred * centred, axis=-1, keepdims=True)
    return centred * lax.rsqrt(spread + 1e-05) * gain


def point_valid(first_points, tok_rows, counts):
    positions = first_points[:, None] + jnp.arange(PATCH, dtype=jnp.int32)[None, :]
    return positions % tok_rows < jnp.take(counts, positions // tok_rows)


def attend_patch(packed):
    queries, own_kv, far_kv, own_valid, far_valid = packed
    keys_all = jnp.concatenate([own_kv[None], far_kv], axis=0)
    keys_all = keys_all.reshape(-1, keys_all.shape[2], keys_all.shape[3])
    key_valid = jnp.concatenate([own_valid[None], far_valid], axis=0).reshape(-1)
    scores = jnp.einsum(
        "qhd,khd->hqk", queries, keys_all[..., :HEAD_DIM], preferred_element_type=jnp.float32
    ) * HEAD_DIM ** (-0.5)
    masked = jnp.where(key_valid[None, None, :], scores, -jnp.inf)
    row_max = jnp.max(masked, axis=-1, keepdims=True)
    weights = jnp.exp(masked - row_max)
    denominator = jnp.sum(weights, axis=-1)
    rounded = weights.astype(jnp.bfloat16)
    attended = jnp.einsum(
        "hqk,khd->qhd", rounded, keys_all[..., HEAD_DIM:], preferred_element_type=jnp.float32
    )
    attended = attended / jnp.transpose(denominator)[:, :, None]
    return attended.astype(jnp.bfloat16)


def per_device(
    points, gain_attn, w_qkv, w_out, gain_mlp, w_fc1, w_fc2, contact_route, contact_patch, counts
):
    tok_rows = points.shape[0]
    head_groups = lax.axis_size("head")
    seq_count = lax.axis_size("seq")
    seq_index = lax.axis_index("seq")
    group_rows = head_groups * tok_rows
    patch_count = group_rows // PATCH
    reach_span = min(4, seq_count // 4)
    offsets = [
        route_slot - reach_span + (1 if route_slot >= reach_span else 0)
        for route_slot in range(2 * reach_span)
    ]
    per_group = HEADS // head_groups
    normed = layer_norm(points, gain_attn).astype(jnp.bfloat16)
    projected = jnp.dot(normed, w_qkv, preferred_element_type=jnp.float32).astype(jnp.bfloat16)
    projected = projected.reshape(tok_rows, head_groups, per_group, 3 * HEAD_DIM)
    routes_all = contact_route.reshape(seq_count, patch_count * CB)
    local_all = contact_patch.reshape(seq_count, patch_count * CB)
    my_routes = jnp.take(routes_all, seq_index, axis=0)
    my_local = jnp.take(local_all, seq_index, axis=0)
    my_offsets = my_routes - reach_span + (my_routes >= reach_span).astype(jnp.int32)
    far_first = ((seq_index + my_offsets) % seq_count * patch_count + my_local) * PATCH
    far_valid = point_valid(far_first, tok_rows, counts).reshape(patch_count, CB, PATCH)
    own_first = seq_index * group_rows + jnp.arange(patch_count, dtype=jnp.int32) * PATCH
    own_valid = point_valid(own_first, tok_rows, counts)
    head_items = lax.all_to_all(projected, "head", split_axis=1, concat_axis=0, tiled=True)
    item_width = head_items.shape[2]
    blocks = head_items.reshape(patch_count, PATCH, item_width, 3 * HEAD_DIM)
    queries = blocks[..., :HEAD_DIM]
    key_values = blocks[..., HEAD_DIM:]
    arrived = [passed_along(key_values, "seq", -offset) for offset in offsets]
    stacked = jnp.stack(arrived).reshape(
        2 * reach_span * patch_count, PATCH, item_width, 2 * HEAD_DIM
    )
    far_kv = jnp.take(stacked, my_routes * patch_count + my_local, axis=0)
    far_kv = far_kv.reshape(patch_count, CB, PATCH, item_width, 2 * HEAD_DIM)
    attended = lax.map(attend_patch, (queries, key_values, far_kv, own_valid, far_valid))
    attended = attended.reshape(group_rows, 1, item_width, HEAD_DIM)
    returned = lax.all_to_all(
        attended.reshape(group_rows, 1, per_group * HEAD_DIM),
        "head",
        split_axis=0,
        concat_axis=1,
        tiled=True,
    )
    returned = returned.reshape(tok_rows, D)
    updated = (
        points.astype(jnp.float32) + jnp.dot(returned, w_out, preferred_element_type=jnp.float32)
    ).astype(jnp.bfloat16)
    normed_mlp = layer_norm(updated, gain_mlp).astype(jnp.bfloat16)
    gathered = lax.all_gather(normed_mlp, "head", axis=0, tiled=True)
    hidden = jax.nn.gelu(
        jnp.dot(gathered, w_fc1, preferred_element_type=jnp.float32), approximate=False
    ).astype(jnp.bfloat16)
    summed = lax.psum_scatter(
        jnp.dot(hidden, w_fc2, preferred_element_type=jnp.float32).astype(jnp.bfloat16),
        "head",
        scatter_dimension=0,
        tiled=True,
    ).astype(jnp.float32)
    return (updated.astype(jnp.float32) + summed).astype(jnp.bfloat16)


def solution(mesh):
    return jax.shard_map(
        per_device,
        mesh=mesh,
        in_specs=(
            P(("seq", "head"), None),
            P(),
            P(),
            P(),
            P(),
            P(None, "head"),
            P("head", None),
            P("head", None, None),
            P("head", None),
            P(),
        ),
        out_specs=P(("seq", "head"), None),
        check_vma=False,
    )
```

profile of v0, /device:TPU:25, one launch (start us, length us, event | category | flops | bytes accessed | tf_op | source)
XLA Modules:
  0.0 396.7 jit_solution(1403485950938228957)
XLA Ops:
  6.5 1.2 convert_reduce_fusion
  7.7 1.2 fusion.74
  8.9 1.6 convolution_convert_fusion.1
  10.5 1.2 copy.25
  11.7 5.8 %all-to-all-start = ((bf16[256,8,4,48]{0,3,2,1:T(8,128)(2,1)}), bf16[256,8,4,48]{0,3,2,1:T(8,128)(2,1)S(1)}, u32[]{:S(2)}, u32[]{:S(2)}) async-start(bf16[256,8,4,48]{0,3,2,1:T(8,128)(2,1)} %bitcast.6), calls=%async_computation | async-start | bytes 1572864 | tf_op jit(solution)/shard_map/all_to_all | solution.py:78
  18.0 0.7 reduce.7
  18.8 0.7 reduce.6
  19.8 25.7 %gather_fusion.2 = s32[4096]{0:T(1024)S(1)} fusion(s32[256]{0:T(256)S(1)} %copy-done.2, s32[4096]{0:T(1024)S(1)} %bitcast_clamp_fusion), kind=kCustom, calls=%fused_computation.2 | custom fusion | bytes 49152 | tf_op jit(solution)/shard_map/jit(_take)/gather | solution.py:28
  46.9 6.2 %collective-permute-start = (bf16[2,1024,4,32]{1,0,3,2:T(2,128)(2,1)S(1)}, bf16[2,1024,4,32]{1,0,3,2:T(2,128)(2,1)S(1)}, u32[]{:S(2)}, u32[]{:S(2)}) collective-permute-start(bf16[2,1024,4,32]{1,0,3,2:T(2,128)(2,1)S(1)} %slice.29), channel_id=1, source_target_pairs={{0,32},{8,40},{16,48},{24,56},{32,64},{40,72},{48,80},{56,88},{64,... | collective-permute-start | bytes 1572872 | tf_op jit(solution)/shard_map/ppermute | solution.py:16
  53.2 13.1 %gather_fusion.1 = s32[2048]{0:T(1024)S(1)} fusion(s32[256]{0:T(256)S(1)} %copy-done.2, s32[2048]{0:T(1024)S(1)} %bitcast_clamp_fusion.1), kind=kCustom, calls=%fused_computation.1 | custom fusion | bytes 24576 | tf_op jit(solution)/shard_map/jit(_take)/gather | solution.py:28
  66.3 1.7 collective-permute-start.1
  68.4 1.0 collective-permute-start.3
  69.4 3.8 collective-permute-start.4
  73.4 10.6 %collective-permute-start.5 = (bf16[2,1024,4,32]{1,0,3,2:T(2,128)(2,1)S(1)}, bf16[2,1024,4,32]{1,0,3,2:T(2,128)(2,1)S(1)}, u32[]{:S(2)}, u32[]{:S(2)}) collective-permute-start(bf16[2,1024,4,32]{1,0,3,2:T(2,128)(2,1)S(1)} %slice.29), channel_id=1, source_target_pairs={{0,240},{8,248},{16,0},{24,8},{32,16},{40,24},{48,32},{56,40},{64,... | collective-permute-start | bytes 1572872 | tf_op jit(solution)/shard_map/ppermute | solution.py:16
  84.4 32.5 %collective-permute-done.1 = bf16[2,1024,4,32]{1,0,3,2:T(2,128)(2,1)S(1)} collective-permute-done((bf16[2,1024,4,32]{1,0,3,2:T(2,128)(2,1)S(1)}, bf16[2,1024,4,32]{1,0,3,2:T(2,128)(2,1)S(1)}, u32[]{:S(2)}, u32[]{:S(2)}) %collective-permute-start.1) | collective-permute-done | bytes 524320 | tf_op jit(solution)/shard_map/ppermute | solution.py:16
  117.0 0.6 collective-permute-start.6
  117.9 6.2 %collective-permute-done.2 = bf16[2,1024,4,32]{1,0,3,2:T(2,128)(2,1)S(1)} collective-permute-done((bf16[2,1024,4,32]{1,0,3,2:T(2,128)(2,1)S(1)}, bf16[2,1024,4,32]{1,0,3,2:T(2,128)(2,1)S(1)}, u32[]{:S(2)}, u32[]{:S(2)}) %collective-permute-start.2) | collective-permute-done | bytes 524320 | tf_op jit(solution)/shard_map/ppermute | solution.py:16
  124.1 5.7 %collective-permute-start.7 = (bf16[2,1024,4,32]{1,0,3,2:T(2,128)(2,1)S(1)}, bf16[2,1024,4,32]{1,0,3,2:T(2,128)(2,1)S(1)}, u32[]{:S(2)}, u32[]{:S(2)}) collective-permute-start(bf16[2,1024,4,32]{1,0,3,2:T(2,128)(2,1)S(1)} %slice.29), channel_id=1, source_target_pairs={{0,224},{8,232},{16,240},{24,248},{32,0},{40,8},{48,16},{56,24},{6... | collective-permute-start | bytes 1572872 | tf_op jit(solution)/shard_map/ppermute | solution.py:16
  130.3 15.6 %collective-permute-done.3 = bf16[2,1024,4,32]{1,0,3,2:T(2,128)(2,1)S(1)} collective-permute-done((bf16[2,1024,4,32]{1,0,3,2:T(2,128)(2,1)S(1)}, bf16[2,1024,4,32]{1,0,3,2:T(2,128)(2,1)S(1)}, u32[]{:S(2)}, u32[]{:S(2)}) %collective-permute-start.3) | collective-permute-done | bytes 524320 | tf_op jit(solution)/shard_map/ppermute | solution.py:16
  147.0 2.0 collective-permute-done.6
  149.5 18.8 %collective-permute-done.7 = bf16[2,1024,4,32]{1,0,3,2:T(2,128)(2,1)S(1)} collective-permute-done((bf16[2,1024,4,32]{1,0,3,2:T(2,128)(2,1)S(1)}, bf16[2,1024,4,32]{1,0,3,2:T(2,128)(2,1)S(1)}, u32[]{:S(2)}, u32[]{:S(2)}) %collective-permute-start.7) | collective-permute-done | bytes 524320 | tf_op jit(solution)/shard_map/ppermute | solution.py:16
  168.7 3.3 copy.27
  172.0 2.8 gather_fusion
  174.9 0.8 copy-done.7
  175.7 123.0 %while.11 = (s32[]{:T(128)}, bf16[2,1024,4,16]{1,3,2,0:T(8,128)(2,1)S(1)}, bf16[2,1024,4,32]{1,0,3,2:T(2,128)(2,1)S(1)}, bf16[2,2,1024,4,32]{2,4,3,1,0:T(8,128)(...) while((s32[]{:T(128)}, ...), condition=%wide.region_5.7_spmd, body=%wide.region_2.6_spmd.sunk | while | flops 945417216 | bytes 166309040 | solution.py:89
  175.9 0.5 copy.44
  176.7 0.5 constant_dynamic-slice_fusion.8
  177.2 1.1 pad_maximum_fusion.2
  178.3 1.1 reshape.382
  179.4 18.4 %fusion.142 = (f32[4,1024]{1,0:T(4,128)S(1)}, f32[4,1024,3072]{2,1,0:T(8,128)}) fusion(pred[3072]{0:T(1024)(128)(4,1)S(1)} %broadcast_in_dim.123, bf16[3072,4,32]{0,2,1:T(8,128)(2,1)S(1)} %reshape.382, bf16[2,1024,4,16]{1,3,2,0:T(8,128)(2,1)S(1)} %get-tuple-element.172, s32[]{:T(128)} %get-tuple-element.158), kind=kOutput, calls=%fused_computation.5.clone.1 | convolution fusion | flops 440397824 | bytes 50875396 | tf_op jit(solution)/shard_map/while/body/eval_jaxpr/qhd,khd->hqk/dot_general | solution.py:36
  197.8 21.3 %fusion.143 = f32[4,1024]{1,0:T(4,128)S(1)} fusion(f32[4,1024,3072]{2,1,0:T(8,128)} %get-tuple-element.148, f32[4,1024]{1,0:T(4,128)S(1)} %get-tuple-element.149, pred[3072]{0:T(1024)(128)(4,1)S(1)} %broadcast_in_dim.123), kind=kLoop, calls=%fused_computation.6.clone.1 | loop fusion | flops 50327552 | bytes 50367488 | tf_op jit(solution)/shard_map/while/body/eval_jaxpr/reduce_sum | solution.py:42
  219.1 18.1 %fusion.144 = bf16[2,1024,4,16]{1,3,2,0:T(8,128)(2,1)S(1)} fusion(bf16[2,1024,4,16]{1,3,2,0:T(8,128)(2,1)S(1)} %get-tuple-element.159, s32[]{:T(128)} %get-tuple-element.158, f32[4,1024,3072]{2,1,0:T(8,128)} %get-tuple-element.148, f32[4,1024]{1,0:T(4,128)S(1)} %get-tuple-element.149, pred[3072]{0:T(1024)(128)(4,1)S(1)} %broadcast_in_dim.123, ...), kind=kOutput, calls=%fused_computation.14.clone.1 | convolution fusion | flops 453115904 | bytes 50891780 | tf_op jit(solution)/shard_map/while/body/eval_jaxpr/hqk,khd->qhd/dot_general | solution.py:44
  237.4 0.5 copy.44
  238.2 0.5 constant_dynamic-slice_fusion.8
  238.8 1.1 pad_maximum_fusion.2
  239.9 1.1 reshape.382
  241.0 18.4 %fusion.142 = (f32[4,1024]{1,0:T(4,128)S(1)}, f32[4,1024,3072]{2,1,0:T(8,128)}) fusion(pred[3072]{0:T(1024)(128)(4,1)S(1)} %broadcast_in_dim.123, bf16[3072,4,32]{0,2,1:T(8,128)(2,1)S(1)} %reshape.382, bf16[2,1024,4,16]{1,3,2,0:T(8,128)(2,1)S(1)} %get-tuple-element.172, s32[]{:T(128)} %get-tuple-element.158), kind=kOutput, calls=%fused_computation.5.clone.1 | convolution fusion | flops 440397824 | bytes 50875396 | tf_op jit(solution)/shard_map/while/body/eval_jaxpr/qhd,khd->hqk/dot_general | solution.py:36
  259.3 21.3 %fusion.143 = f32[4,1024]{1,0:T(4,128)S(1)} fusion(f32[4,1024,3072]{2,1,0:T(8,128)} %get-tuple-element.148, f32[4,1024]{1,0:T(4,128)S(1)} %get-tuple-element.149, pred[3072]{0:T(1024)(128)(4,1)S(1)} %broadcast_in_dim.123), kind=kLoop, calls=%fused_computation.6.clone.1 | loop fusion | flops 50327552 | bytes 50367488 | tf_op jit(solution)/shard_map/while/body/eval_jaxpr/reduce_sum | solution.py:42
  280.6 18.1 %fusion.144 = bf16[2,1024,4,16]{1,3,2,0:T(8,128)(2,1)S(1)} fusion(bf16[2,1024,4,16]{1,3,2,0:T(8,128)(2,1)S(1)} %get-tuple-element.159, s32[]{:T(128)} %get-tuple-element.158, f32[4,1024,3072]{2,1,0:T(8,128)} %get-tuple-element.148, f32[4,1024]{1,0:T(4,128)S(1)} %get-tuple-element.149, pred[3072]{0:T(1024)(128)(4,1)S(1)} %broadcast_in_dim.123, ...), kind=kOutput, calls=%fused_computation.14.clone.1 | convolution fusion | flops 453115904 | bytes 50891780 | tf_op jit(solution)/shard_map/while/body/eval_jaxpr/hqk,khd->qhd/dot_general | solution.py:44
  299.7 0.8 reduce.8
  301.2 11.9 %all_to_all.30 = bf16[8,2,8192]{2,1,0:T(2,128)(2,1)S(1)} all-to-all(bf16[8,2,8192]{2,1,0:T(2,128)(2,1)S(1)} %reshape.379), channel_id=1, replica_groups=mesh['seq'=32,'head'=8] {'head'}, dimensions={0} | all-to-all | bytes 524288 | tf_op jit(solution)/shard_map/all_to_all | solution.py:91
  313.1 0.6 reshape.380
  313.7 0.6 copy.32
  315.1 0.9 multiply_convert_fusion
  316.1 27.4 %all-gather.2.cloned.1.call-done = bf16[2048,512]{1,0:T(8,128)(2,1)} async-done(((bf16[256,512]{1,0:T(8,128)(2,1)}), bf16[2048,512]{1,0:T(8,128)(2,1)}) %all-gather.2.cloned.1.call-update) | async-done | bytes 2097168 | tf_op jit(solution)/shard_map/all_gather | solution.py:103
  343.5 9.0 %convolution_convert_fusion = bf16[2048,512]{1,0:T(8,128)(2,1)} fusion(bf16[256,512]{1,0:T(8,128)(2,1)S(1)} %copy-done.9, bf16[2048,512]{1,0:T(8,128)(2,1)} %all-gather.2.cloned.1.call-done, bf16[512,256]{1,0:T(8,128)(2,1)S(1)} %copy-done.10), kind=kOutput, calls=%fused_computation.31 | convolution fusion | flops 1108869120 | bytes 4718592 | tf_op jit(solution)/shard_map/dot_general | solution.py:108
  352.5 35.7 %reduce-scatter.2.cloned.1.call-done = bf16[256,512]{1,0:T(8,128)(2,1)} async-done(((bf16[2048,512]{1,0:T(8,128)(2,1)}), bf16[256,512]{1,0:T(8,128)(2,1)}) %reduce-scatter.2.cloned.1.call-update) | async-done | bytes 262160 | tf_op jit(solution)/shard_map/reduce_scatter | solution.py:107
  388.1 1.7 add_convert_fusion
  (93 shorter events, 9.4 us)
Async XLA Ops:
  6.5 2.4 copy-start
  10.5 7.5 %copy-start.11 = (s32[1,128,1]{1,2,0:T(1,128)S(1)}, s32[1,128,1]{1,2,0:T(1,128)}, u32[]{:S(2)}) copy-start(s32[1,128,1]{1,2,0:T(1,128)} %param.21) | copy-start | bytes 1540
  10.5 8.2 %copy-start.12 = (s32[1,128]{1,0:T(1,128)S(1)}, s32[1,128]{1,0:T(1,128)}, u32[]{:S(2)}) copy-start(s32[1,128]{1,0:T(1,128)} %param.22) | copy-start | bytes 1540
  10.5 9.2 %copy-start.2 = (s32[256]{0:T(256)S(1)}, s32[256]{0:T(256)}, u32[]{:S(2)}) copy-start(s32[256]{0:T(256)} %param.23) | copy-start | bytes 3076
  11.7 34.1 %all-to-all-start = ((bf16[256,8,4,48]{0,3,2,1:T(8,128)(2,1)}), bf16[256,8,4,48]{0,3,2,1:T(8,128)(2,1)S(1)}, u32[]{:S(2)}, u32[]{:S(2)}) async-start(bf16[256,8,4,48]{0,3,2,1:T(8,128)(2,1)} %bitcast.6), calls=%async_computation | async-start | bytes 1572864 | tf_op jit(solution)/shard_map/all_to_all | solution.py:78
  17.5 326.0 %all-gather.2.cloned.1.call-start = ((), (), s32[]{:S(2)}) async-start(), calls=%async_computation.3 | async-start | bytes 2359296 | tf_op jit(solution)/shard_map/all_gather | solution.py:103
  46.9 26.5 %collective-permute-start = (bf16[2,1024,4,32]{1,0,3,2:T(2,128)(2,1)S(1)}, bf16[2,1024,4,32]{1,0,3,2:T(2,128)(2,1)S(1)}, u32[]{:S(2)}, u32[]{:S(2)}) collective-permute-start(bf16[2,1024,4,32]{1,0,3,2:T(2,128)(2,1)S(1)} %slice.29), channel_id=1, source_target_pairs={{0,32},{8,40},{16,48},{24,56},{32,64},{40,72},{48,80},{56,88},{64,... | collective-permute-start | bytes 1572872 | tf_op jit(solution)/shard_map/ppermute | solution.py:16
  66.3 50.6 %collective-permute-start.1 = (bf16[2,1024,4,32]{1,0,3,2:T(2,128)(2,1)S(1)}, bf16[2,1024,4,32]{1,0,3,2:T(2,128)(2,1)S(1)}, u32[]{:S(2)}, u32[]{:S(2)}) collective-permute-start(bf16[2,1024,4,32]{1,0,3,2:T(2,128)(2,1)S(1)} %slice.29), channel_id=1, source_target_pairs={{0,24},{8,32},{16,40},{24,48},{32,56},{40,64},{48,72},{56,80},{64,... | collective-permute-start | bytes 1572872 | tf_op jit(solution)/shard_map/ppermute | solution.py:16
  68.2 56.0 %collective-permute-start.2 = (bf16[2,1024,4,32]{1,0,3,2:T(2,128)(2,1)S(1)}, bf16[2,1024,4,32]{1,0,3,2:T(2,128)(2,1)S(1)}, u32[]{:S(2)}, u32[]{:S(2)}) collective-permute-start(bf16[2,1024,4,32]{1,0,3,2:T(2,128)(2,1)S(1)} %slice.29), channel_id=1, source_target_pairs={{0,16},{8,24},{16,32},{24,40},{32,48},{40,56},{48,64},{56,72},{64,... | collective-permute-start | bytes 1572872 | tf_op jit(solution)/shard_map/ppermute | solution.py:16
  68.4 77.5 %collective-permute-start.3 = (bf16[2,1024,4,32]{1,0,3,2:T(2,128)(2,1)S(1)}, bf16[2,1024,4,32]{1,0,3,2:T(2,128)(2,1)S(1)}, u32[]{:S(2)}, u32[]{:S(2)}) collective-permute-start(bf16[2,1024,4,32]{1,0,3,2:T(2,128)(2,1)S(1)} %slice.29), channel_id=1, source_target_pairs={{0,8},{8,16},{16,24},{24,32},{32,40},{40,48},{48,56},{56,64},{64,7... | collective-permute-start | bytes 1572872 | tf_op jit(solution)/shard_map/ppermute | solution.py:16
  69.4 76.9 %collective-permute-start.4 = (bf16[2,1024,4,32]{1,0,3,2:T(2,128)(2,1)S(1)}, bf16[2,1024,4,32]{1,0,3,2:T(2,128)(2,1)S(1)}, u32[]{:S(2)}, u32[]{:S(2)}) collective-permute-start(bf16[2,1024,4,32]{1,0,3,2:T(2,128)(2,1)S(1)} %slice.29), channel_id=1, source_target_pairs={{0,248},{8,0},{16,8},{24,16},{32,24},{40,32},{48,40},{56,48},{64,5... | collective-permute-start | bytes 1572872 | tf_op jit(solution)/shard_map/ppermute | solution.py:16
  73.4 73.2 %collective-permute-start.5 = (bf16[2,1024,4,32]{1,0,3,2:T(2,128)(2,1)S(1)}, bf16[2,1024,4,32]{1,0,3,2:T(2,128)(2,1)S(1)}, u32[]{:S(2)}, u32[]{:S(2)}) collective-permute-start(bf16[2,1024,4,32]{1,0,3,2:T(2,128)(2,1)S(1)} %slice.29), channel_id=1, source_target_pairs={{0,240},{8,248},{16,0},{24,8},{32,16},{40,24},{48,32},{56,40},{64,... | collective-permute-start | bytes 1572872 | tf_op jit(solution)/shard_map/ppermute | solution.py:16
  117.0 32.1 %collective-permute-start.6 = (bf16[2,1024,4,32]{1,0,3,2:T(2,128)(2,1)S(1)}, bf16[2,1024,4,32]{1,0,3,2:T(2,128)(2,1)S(1)}, u32[]{:S(2)}, u32[]{:S(2)}) collective-permute-start(bf16[2,1024,4,32]{1,0,3,2:T(2,128)(2,1)S(1)} %slice.29), channel_id=1, source_target_pairs={{0,232},{8,240},{16,248},{24,0},{32,8},{40,16},{48,24},{56,32},{64... | collective-permute-start | bytes 1572872 | tf_op jit(solution)/shard_map/ppermute | solution.py:16
  124.1 44.1 %collective-permute-start.7 = (bf16[2,1024,4,32]{1,0,3,2:T(2,128)(2,1)S(1)}, bf16[2,1024,4,32]{1,0,3,2:T(2,128)(2,1)S(1)}, u32[]{:S(2)}, u32[]{:S(2)}) collective-permute-start(bf16[2,1024,4,32]{1,0,3,2:T(2,128)(2,1)S(1)} %slice.29), channel_id=1, source_target_pairs={{0,224},{8,232},{16,240},{24,248},{32,0},{40,8},{48,16},{56,24},{6... | collective-permute-start | bytes 1572872 | tf_op jit(solution)/shard_map/ppermute | solution.py:16
  174.8 1.0 copy-start.7
  175.7 1.0 copy-start.3
  219.1 18.1 %copy-start.4 = (bf16[2,2,1024,4,32]{2,4,3,1,0:T(8,128)(2,1)S(1)}, bf16[2,2,1024,4,32]{2,4,3,1,0:T(8,128)(2,1)}, u32[]{:S(2)}) copy-start(bf16[2,2,1024,4,32]{2,4,3,1,0:T(8,128)(2,1)} %copy-done.3) | copy-start | bytes 3145732 | tf_op jit(solution)/shard_map/while
  237.2 1.0 copy-start.3
  280.6 18.1 %copy-start.4 = (bf16[2,2,1024,4,32]{2,4,3,1,0:T(8,128)(2,1)S(1)}, bf16[2,2,1024,4,32]{2,4,3,1,0:T(8,128)(2,1)}, u32[]{:S(2)}) copy-start(bf16[2,2,1024,4,32]{2,4,3,1,0:T(8,128)(2,1)} %copy-done.3) | copy-start | bytes 3145732 | tf_op jit(solution)/shard_map/while
  301.2 13.3 %copy-start.5 = (bf16[256,512]{1,0:T(8,128)(2,1)S(1)}, bf16[256,512]{1,0:T(8,128)(2,1)}, u32[]{:S(2)}) copy-start(bf16[256,512]{1,0:T(8,128)(2,1)} %param.14) | copy-start | bytes 786436
  301.2 13.3 %copy-start.6 = (bf16[512,512]{1,0:T(8,128)(2,1)S(1)}, bf16[512,512]{1,0:T(8,128)(2,1)}, u32[]{:S(2)}) copy-start(bf16[512,512]{1,0:T(8,128)(2,1)} %param.17) | copy-start | bytes 1572868
  313.7 1.4 copy-start.8
  314.3 29.1 %copy-start.9 = (bf16[256,512]{1,0:T(8,128)(2,1)S(1)}, bf16[256,512]{1,0:T(8,128)(2,1)}, u32[]{:S(2)}) copy-start(bf16[256,512]{1,0:T(8,128)(2,1)} %param.20) | copy-start | bytes 786436
  314.3 29.1 %copy-start.10 = (bf16[512,256]{1,0:T(8,128)(2,1)S(1)}, bf16[512,256]{1,0:T(8,128)(2,1)}, u32[]{:S(2)}) copy-start(bf16[512,256]{1,0:T(8,128)(2,1)} %param.19) | copy-start | bytes 786436
  316.0 72.1 %reduce-scatter.2.cloned.1.call-start = ((), (), s32[]{:S(2)}) async-start(), calls=%async_computation.4 | async-start | bytes 2359296 | tf_op jit(solution)/shard_map/reduce_scatter | solution.py:107
  343.5 46.4 %copy-start.1 = (bf16[512,1536]{1,0:T(8,128)(2,1)S(1)}, bf16[512,1536]{1,0:T(8,128)(2,1)}, u32[]{:S(2)}) copy-start(bf16[512,1536]{1,0:T(8,128)(2,1)} %param.16) | copy-start | bytes 4718596
Sparse Core Ops, SparseCore 0:
  316.1 27.2 all-gather.1
  352.6 35.5 reduce-scatter.1
where the time goes:
time: 399 us; the launch traced here: 397 us
  waiting for transfers between devices  138 us (35%)
  matrix products  83.9 us (21%)
  local copies, waits for them, and re-layouts  60.4 us (15%)
  other arithmetic  52.7 us (13%)
  starting transfers between devices  35.6 us (9%)
  between operations  13.8 us (3%)
  blocking collectives  11.9 us (3%)
    ppermute x8, waiting for transfers between devices, passed_along(): return lax.ppermute(value, axis, pairs)  75.2 us
    reduce_sum x2, other arithmetic, attend_patch(): denominator = jnp.sum(weights, axis=-1)  42.6 us
    gather x4, local copies, waits for them, and re-layouts, point_valid(): return positions % tok_rows < jnp.take(counts, positions // tok_rows)  38.9 us
    dot_general x2, matrix products, attend_patch(): jnp.einsum('qhd,khd->hqk', queries, keys_all[..., :HEAD_DIM], preferred_e...  36.7 us
    dot_general x2, matrix products, attend_patch(): jnp.einsum('hqk,khd->qhd', rounded, keys_all[..., HEAD_DIM:], preferred_e...  36.2 us
    reduce_scatter x1, waiting for transfers between devices, per_device(): lax.psum_scatter(jnp.dot(hidden, w_fc2, preferred_element_type=jnp.float3...  35.7 us
    ppermute x8, starting transfers between devices, passed_along(): return lax.ppermute(value, axis, pairs)  29.8 us
    all_gather x1, waiting for transfers between devices, per_device(): gathered = lax.all_gather(normed_mlp, 'head', axis=0, tiled=True)  27.4 us
  transfers between devices with their start and end apart: 11, of which 7 were waited for; matrix products, arithmetic and copies ran while one was open for 11% of the time, Pallas kernels for 0%

commit v1 on v0

v1 whole, which is shorter than its diff:
```python
import functools
import math

import jax
import jax.numpy as jnp
import numpy as np
from jax import lax
from jax.experimental import pallas as pl
from jax.experimental.pallas import tpu as pltpu
from jax.sharding import PartitionSpec as P

D = 512
HEADS = 32
HEAD_DIM = 16
PATCH = 1024
CB = 2
NPL = 2
REACH = 4
TOK = 256
GROUPS = 8
LANES = 128
CHUNK = 256
F32 = jnp.float32
BF16 = jnp.bfloat16
MASKED = -3.3e38
ROWS = 8 * LANES


def placing():
    kv = np.zeros((384, 256), np.float32)
    low = np.zeros((384, 256), np.float32)
    high = np.zeros((384, 256), np.float32)
    for group in range(2):
        for head in range(4):
            for dim in range(HEAD_DIM):
                source = group * 192 + head * 48 + dim
                lane = group * 128 + head * 16 + dim
                low[source, lane] = 1
                high[source, lane + 64] = 1
                kv[source + 16, lane] = 1
                kv[source + 32, lane + 64] = 1
    return np.concatenate([kv, low, high], axis=1)


def lane_of(shape):
    return lax.broadcasted_iota(jnp.int32, shape, len(shape) - 1)


def normalise(values, gain):
    centred = values - jnp.mean(values, axis=-1, keepdims=True)
    spread = jnp.mean(centred * centred, axis=-1, keepdims=True)
    return centred * lax.rsqrt(spread + 1e-05) * gain


def project_kernel(points_ref, gain_ref, w_ref, scale_ref, place_ref, kv_ref, q_ref):
    normed = normalise(points_ref[...].astype(F32), gain_ref[...]).astype(BF16)
    for pair in range(GROUPS // 2):
        columns = slice(384 * pair, 384 * pair + 384)
        projected = jnp.dot(normed, w_ref[:, columns], preferred_element_type=F32)
        projected = (projected * scale_ref[:, columns]).astype(BF16)
        kv = jnp.dot(projected, place_ref[:, :256], preferred_element_type=F32).astype(BF16)
        q = jnp.dot(projected[:128], place_ref[:, 256:512], preferred_element_type=F32)
        q = q + jnp.dot(projected[128:], place_ref[:, 512:], preferred_element_type=F32)
        q = q.astype(BF16)
        for side in range(2):
            kv_ref[2 * pair + side] = kv[:, 128 * side:128 * side + 128]
            q_ref[2 * pair + side] = q[:, 128 * side:128 * side + 128]


def project(points, gain, w_qkv):
    scale = np.ones((1, 1536), np.float32)
    scale[0, np.arange(1536) % 48 < 16] = HEAD_DIM ** -0.5 * math.log2(math.e)
    return pl.pallas_call(
        project_kernel,
        out_shape=(
            jax.ShapeDtypeStruct((GROUPS, TOK, LANES), BF16),
            jax.ShapeDtypeStruct((GROUPS, LANES, LANES), BF16),
        ),
        name="project",
    )(points, gain.reshape(1, D), w_qkv, jnp.asarray(scale), jnp.asarray(placing(), BF16))


def attend_kernel(
    slot_of, sides, routes_ref, local_ref, counts_ref, place_ref, q_ref, kv_ref, out_ref,
    raw, keys, vals, lhs, acc, top, sems,
):
    seq = place_ref[0]
    core = place_ref[1]
    own_slot = slot_of(0, core) * NPL

    def source(patch, which):
        if which == 0:
            return own_slot + patch, seq * GROUPS + patch * 4
        row = seq * NPL * CB + patch * CB + which - 1
        route = routes_ref[row]
        offset = jnp.where(route < REACH, route - REACH, route - REACH + 1)
        local = local_ref[row]
        owner = lax.rem(seq + offset + 32, 32)
        return slot_of(offset, core) * NPL + local, owner * GROUPS + local * 4

    for patch in range(NPL):
        for which in range(CB + 1):
            slot, _ = source(patch, which)
            pltpu.make_async_copy(kv_ref.at[slot], raw.at[patch * 3 + which], sems.at[patch * 3 + which]).start()

    lane_kv = lane_of((TOK, LANES))
    row_kv = lax.broadcasted_iota(jnp.int32, (TOK, LANES), 0)
    lane_q = lane_of((LANES, LANES))
    one = jnp.ones((TOK, LANES), BF16)
    zero = jnp.zeros((TOK, LANES), BF16)
    low_lane = lane_kv < 64
    sum_of = ((lane_of((LANES, LANES)) == (lax.broadcasted_iota(jnp.int32, (LANES, LANES), 0) // 16))).astype(BF16)
    sum_of = jnp.where(lane_q < 4, sum_of, jnp.zeros_like(sum_of))

    def patch_body(patch, _):
        for which in range(CB + 1):
            pltpu.make_async_copy(kv_ref.at[0], raw.at[patch * 3 + which], sems.at[patch * 3 + which]).wait()

        first = jnp.int32(0)
        key_top = jnp.zeros((1, LANES), F32)
        val_top = jnp.zeros((1, LANES), F32)
        for which in range(CB + 1):
            row = seq * NPL * CB + patch * CB + max(which - 1, 0)
            if which == 0:
                shard = seq * GROUPS + patch * 4
            else:
                route = routes_ref[row]
                offset = jnp.where(route < REACH, route - REACH, route - REACH + 1)
                shard = lax.rem(seq + offset + 32, 32) * GROUPS + local_ref[row] * 4
            for part in range(4):
                count = counts_ref[shard + part]
                block = raw[patch * 3 + which, TOK * part:TOK * part + TOK, :]
                valid = row_kv < count
                flag = jnp.where(valid, zero, jnp.where(lane_kv < 66, jnp.full_like(zero, MASKED), zero))
                keyed = jnp.where(low_lane & valid, block, zero)
                at = pl.ds(pl.multiple_of(first, 16), TOK)
                keys[at, :] = jnp.where(low_lane, keyed, flag)
                vals[at, :] = jnp.where(low_lane, one, block)
                squares = jnp.dot(keyed * keyed, sum_of, preferred_element_type=F32)
                key_top = jnp.maximum(key_top, jnp.max(squares, axis=0, keepdims=True))
                size = jnp.max(jnp.where(low_lane, zero, jnp.abs(block)).astype(F32), axis=0, keepdims=True)
                val_top = jnp.maximum(val_top, size)
                first = first + (count + 15) // 16 * 16
        tail = pl.ds(pl.multiple_of(first, 16), TOK)
        keys[tail, :] = jnp.where(low_lane | (lane_kv >= 66), zero, jnp.full_like(zero, MASKED))
        vals[tail, :] = jnp.where(low_lane, one, zero)
        chunks = (first + CHUNK - 1) // CHUNK

        query_top = jnp.zeros((1, LANES), F32)
        for part in range(4):
            packed = q_ref[patch * 4 + part]
            for half in range(2):
                q = packed if half == 0 else pltpu.roll(packed.astype(F32), 64, 1).astype(BF16)
                q = jnp.where(lane_q < 64, q, jnp.zeros_like(q))
                squares = jnp.dot(q * q, sum_of, preferred_element_type=F32)
                query_top = jnp.maximum(query_top, jnp.max(squares, axis=0, keepdims=True))
        bound = jnp.max(query_top * key_top)
        small = (bound < 3000.0) & (jnp.max(val_top) < 1e9)

        def shard_body(part, _):
            packed = q_ref[patch * 4 + part]
            for half in range(2):
                q = packed if half == 0 else pltpu.roll(packed.astype(F32), 64, 1).astype(BF16)
                for head in range(4):
                    mine = (lane_q >= 16 * head) & (lane_q < 16 * head + 16)
                    flags = jnp.where((lane_q >= 64) & (lane_q < 66), jnp.ones_like(q), jnp.zeros_like(q))
                    lhs[pl.ds((half * 4 + head) * LANES, LANES), :] = jnp.where(mine, q, flags)
            acc[...] = jnp.zeros_like(acc)

            def scores_of(chunk):
                at = pl.ds(pl.multiple_of(chunk * CHUNK, CHUNK), CHUNK)
                return at, lax.dot_general(
                    lhs[...], keys[at, :], (((1,), (1,)), ((), ())), preferred_element_type=F32
                )

            @pl.when(small)
            def _():
                def chunk_body(chunk, _):
                    at, scores = scores_of(chunk)
                    weights = jnp.exp2(scores).astype(BF16)
                    acc[...] += jnp.dot(weights, vals[at, :], preferred_element_type=F32)
                    return 0

                lax.fori_loop(0, chunks, chunk_body, 0)

            @pl.when(jnp.logical_not(small))
            def _():
                top[...] = jnp.full_like(top, -jnp.inf)

                def top_body(chunk, _):
                    _, scores = scores_of(chunk)
                    top[...] = jnp.maximum(top[...], jnp.max(scores, axis=1, keepdims=True))
                    return 0

                lax.fori_loop(0, chunks, top_body, 0)

                def chunk_body(chunk, _):
                    at, scores = scores_of(chunk)
                    weights = jnp.exp2(scores - top[:, :1]).astype(BF16)
                    acc[...] += jnp.dot(weights, vals[at, :], preferred_element_type=F32)
                    return 0

                lax.fori_loop(0, chunks, chunk_body, 0)

            halves = []
            for half in range(2):
                joined = jnp.zeros((LANES, LANES), F32)
                for head in range(4):
                    part_acc = acc[pl.ds((half * 4 + head) * LANES, LANES), :]
                    mine = (lane_q >= 64 + 16 * head) & (lane_q < 80 + 16 * head)
                    joined = jnp.where(mine, part_acc / pltpu.roll(part_acc, 64, 1), joined)
                halves.append(joined)
            out_ref[patch * 4 + part] = (pltpu.roll(halves[0], 64, 1) + halves[1]).astype(BF16)
            return 0

        lax.fori_loop(0, 4, shard_body, 0)
        return 0

    lax.fori_loop(0, NPL, patch_body, 0)


def attend(slot_of, place, routes, local, counts, q, kv):
    smem = pl.BlockSpec(memory_space=pltpu.SMEM)
    vmem = pl.BlockSpec(memory_space=pltpu.VMEM)
    return pl.pallas_call(
        functools.partial(attend_kernel, slot_of, 0),
        out_shape=jax.ShapeDtypeStruct((GROUPS, LANES, LANES), BF16),
        in_specs=[smem, smem, smem, smem, vmem, pl.BlockSpec(memory_space=pl.ANY)],
        out_specs=vmem,
        scratch_shapes=[
            pltpu.VMEM((6, PATCH, LANES), BF16),
            pltpu.VMEM((3 * PATCH + TOK, LANES), BF16),
            pltpu.VMEM((3 * PATCH + TOK, LANES), BF16),
            pltpu.VMEM((ROWS, LANES), BF16),
            pltpu.VMEM((ROWS, LANES), F32),
            pltpu.VMEM((ROWS, LANES), F32),
            pltpu.SemaphoreType.DMA((6,)),
        ],
        compiler_params=pltpu.CompilerParams(vmem_limit_bytes=40 << 20),
        name="attend",
    )(routes, local, counts, place, q, kv)


def finish_kernel(points_ref, packed_ref, w_out_ref, gain_ref, w1_ref, w2_ref, out_ref):
    lane = lane_of((LANES, LANES))
    low, high = [], []
    for pair in range(GROUPS // 2):
        first, second = packed_ref[2 * pair].astype(F32), packed_ref[2 * pair + 1].astype(F32)
        low.append(jnp.where(lane < 64, first, pltpu.roll(second, 64, 1)))
        high.append(jnp.where(lane < 64, pltpu.roll(first, 64, 1), second))
    attended = jnp.concatenate([jnp.concatenate(low, axis=1), jnp.concatenate(high, axis=1)], axis=0)
    updated = points_ref[...].astype(F32) + jnp.dot(
        attended.astype(BF16), w_out_ref[...], preferred_element_type=F32
    )
    updated = updated.astype(BF16).astype(F32)
    normed = normalise(updated, gain_ref[...]).astype(BF16)
    total = updated
    for part in range(GROUPS):
        hidden = jnp.dot(normed, w1_ref[part], preferred_element_type=F32)
        hidden = hidden * (0.5 * (1.0 + lax.erf(hidden * (2.0 ** -0.5))))
        total = total + jnp.dot(hidden.astype(BF16), w2_ref[part], preferred_element_type=F32)
    out_ref[...] = total.astype(BF16)


def finish(points, packed, w_out, gain, w1, w2):
    return pl.pallas_call(
        finish_kernel,
        out_shape=jax.ShapeDtypeStruct((TOK, D), BF16),
        compiler_params=pltpu.CompilerParams(vmem_limit_bytes=40 << 20),
        name="finish",
    )(points, packed, w_out, gain.reshape(1, D), w1, w2)


def passed_along(value, axis, steps):
    count = lax.axis_size(axis)
    return lax.ppermute(value, axis, [(source, (source + steps) % count) for source in range(count)])


def per_device(
    points, gain_attn, w_qkv, w_out, gain_mlp, w_fc1, w_fc2, contact_route, contact_patch, counts
):
    w1 = lax.all_gather(w_fc1, "head", axis=0)
    w2 = lax.all_gather(w_fc2, "head", axis=0)
    kv, q = project(points, gain_attn, w_qkv)
    kv = lax.all_to_all(kv, "head", split_axis=0, concat_axis=0, tiled=True)
    q = lax.all_to_all(q, "head", split_axis=0, concat_axis=0, tiled=True)
    own = kv.reshape(NPL, PATCH, LANES)
    slots = [own if offset == 0 else passed_along(own, "seq", -offset) for offset in range(-REACH, REACH + 1)]
    slots = jnp.concatenate(slots, axis=0)
    place = jnp.stack([lax.axis_index("seq"), jnp.int32(0)])
    packed = attend(
        lambda offset, core: offset + REACH, place, contact_route.reshape(-1), contact_patch.reshape(-1), counts, q, slots
    )
    packed = lax.all_to_all(packed, "head", split_axis=0, concat_axis=0, tiled=True)
    return finish(points, packed, w_out, gain_mlp, w1, w2)


def solution(mesh):
    return jax.shard_map(
        per_device,
        mesh=mesh,
        in_specs=(
            P(("seq", "head"), None), P(), P(), P(), P(), P(None, "head"), P("head", None),
            P("head", None, None), P("head", None), P(),
        ),
        out_specs=P(("seq", "head"), None),
        check_vma=False,
    )
```

time: 399 us -> 254 us (0.64)
  the two profiles are of different devices: /device:TPU:25 before, /device:TPU:228 now
where the time goes in v1:
time: 254 us
  waiting for transfers between devices  95.8 us (38%)
  Pallas kernels  79.9 us (31%)
  blocking collectives  29.6 us (12%)
  starting transfers between devices  26.4 us (10%)
  between operations  13.6 us (5%)
  local copies, waits for them, and re-layouts  8.26 us (3%)
    ppermute x8, waiting for transfers between devices, passed_along(): lax.ppermute(value, axis, [(source, (source + steps) % count) for source...  94.3 us
    pallas_call x1, Pallas kernels, attend(): pl.pallas_call(functools.partial(attend_kernel, slot_of, 0), out_shape=ja...  73.1 us
    ppermute x8, starting transfers between devices, passed_along(): lax.ppermute(value, axis, [(source, (source + steps) % count) for source...  23 us
    all_to_all x1, blocking collectives, per_device(): kv = lax.all_to_all(kv, 'head', split_axis=0, concat_axis=0, tiled=True)  16.4 us
    all_to_all x1, blocking collectives, per_device(): lax.all_to_all(packed, 'head', split_axis=0, concat_axis=0, tiled=True)  13.2 us
    unnamed x28, local copies, waits for them, and re-layouts  8.19 us
  transfers between devices with their start and end apart: 11, of which 6 were waited for; matrix products, arithmetic and copies ran while one was open for 0% of the time, Pallas kernels for 30%

profile of v1, /device:TPU:228, one launch (start us, length us, event | category | flops | bytes accessed | tf_op | source)
XLA Modules:
  0.0 253.6 jit_solution(902470954474824272)
XLA Ops:
  6.5 0.0 all-gather.5.cloned.1.call-start
  6.5 0.7 all-gather.5.cloned.1.call-update
  7.3 0.0 all-gather.7.cloned.1.call-start
  7.3 0.7 all-gather.7.cloned.1.call-update
  8.0 4.2 %project.1 = (bf16[8,256,128]{2,1,0:T(8,128)(2,1)}, bf16[8,128,128]{2,1,0:T(8,128)(2,1)}) custom-call(bf16[256,512]{1,0:T(8,128)(2,1)} %points_ref.3, f32[1,512]{1,0:T(1,128)} %bitcast.24, bf16[512,1536]{1,0:T(8,128)(2,1)} %w_ref.1, f32[1,1536]{1,0:T(1,128)} %constant.12.clone.scale_ref, bf16[384,768]{1,0:T(8,128)(2,1)} %constant.13.clone.place_ref), custom_call_target="tpu_custom_call" | custom-call | tf_op jit(solution)/shard_map/project/pallas_call | solution.py:73
  12.2 16.4 %all_to_all.15 = bf16[8,256,128]{2,1,0:T(8,128)(2,1)S(1)} all-to-all(bf16[8,256,128]{2,1,0:T(8,128)(2,1)} %get-tuple-element.8), channel_id=1, replica_groups=mesh['seq'=32,'head'=8] {'head'}, dimensions={0} | all-to-all | bytes 1048576 | tf_op jit(solution)/shard_map/all_to_all | solution.py:285
  28.6 0.5 collective-permute-start
  29.1 5.2 %collective-permute-start.1 = (bf16[2,1024,128]{2,1,0:T(8,128)(2,1)S(1)}, bf16[2,1024,128]{2,1,0:T(8,128)(2,1)S(1)}, u32[]{:S(2)}, u32[]{:S(2)}) collective-permute-start(bf16[2,1024,128]{2,1,0:T(8,128)(2,1)S(1)} %bitcast.16), channel_id=1, source_target_pairs={{0,24},{8,32},{16,40},{24,48},{32,56},{40,64},{48,72},{56,80},{64,... | collective-permute-start | bytes 1572872 | tf_op jit(solution)/shard_map/ppermute | solution.py:276
  34.4 0.0 collective-permute-start.2
  34.4 1.4 collective-permute-start.3
  35.8 3.4 %all-to-all-start = ((bf16[8,128,128]{2,1,0:T(8,128)(2,1)}), bf16[8,128,128]{2,1,0:T(8,128)(2,1)S(1)}, u32[]{:S(2)}, u32[]{:S(2)}) async-start(bf16[8,128,128]{2,1,0:T(8,128)(2,1)} %get-tuple-element.7), calls=%async_computation | async-start | bytes 524288 | tf_op jit(solution)/shard_map/all_to_all | solution.py:286
  39.2 0.1 pad_add_fusion.place_ref
  39.3 1.5 collective-permute-start.4
  40.8 15.2 %collective-permute-done = bf16[2,1024,128]{2,1,0:T(8,128)(2,1)S(1)} collective-permute-done((bf16[2,1024,128]{2,1,0:T(8,128)(2,1)S(1)}, bf16[2,1024,128]{2,1,0:T(8,128)(2,1)S(1)}, u32[]{:S(2)}, u32[]{:S(2)}) %collective-permute-start) | collective-permute-done | bytes 524320 | tf_op jit(solution)/shard_map/ppermute | solution.py:276
  56.0 3.4 %collective-permute-start.5 = (bf16[2,1024,128]{2,1,0:T(8,128)(2,1)S(1)}, bf16[2,1024,128]{2,1,0:T(8,128)(2,1)S(1)}, u32[]{:S(2)}, u32[]{:S(2)}) collective-permute-start(bf16[2,1024,128]{2,1,0:T(8,128)(2,1)S(1)} %bitcast.20), channel_id=1, source_target_pairs={{0,240},{8,248},{16,0},{24,8},{32,16},{40,24},{48,32},{56,40},{64,... | collective-permute-start | bytes 1572872 | tf_op jit(solution)/shard_map/ppermute | solution.py:276
  59.4 24.2 %collective-permute-done.1 = bf16[2,1024,128]{2,1,0:T(8,128)(2,1)S(1)} collective-permute-done((bf16[2,1024,128]{2,1,0:T(8,128)(2,1)S(1)}, bf16[2,1024,128]{2,1,0:T(8,128)(2,1)S(1)}, u32[]{:S(2)}, u32[]{:S(2)}) %collective-permute-start.1) | collective-permute-done | bytes 524320 | tf_op jit(solution)/shard_map/ppermute | solution.py:276
  83.6 6.5 %collective-permute-start.6 = (bf16[2,1024,128]{2,1,0:T(8,128)(2,1)S(1)}, bf16[2,1024,128]{2,1,0:T(8,128)(2,1)S(1)}, u32[]{:S(2)}, u32[]{:S(2)}) collective-permute-start(bf16[2,1024,128]{2,1,0:T(8,128)(2,1)S(1)} %bitcast.21), channel_id=1, source_target_pairs={{0,232},{8,240},{16,248},{24,0},{32,8},{40,16},{48,24},{56,32},{64... | collective-permute-start | bytes 1572872 | tf_op jit(solution)/shard_map/ppermute | solution.py:276
  90.1 0.1 constant_dynamic-update-slice_fusion.7
  90.2 18.0 %collective-permute-done.2 = bf16[2,1024,128]{2,1,0:T(8,128)(2,1)S(1)} collective-permute-done((bf16[2,1024,128]{2,1,0:T(8,128)(2,1)S(1)}, bf16[2,1024,128]{2,1,0:T(8,128)(2,1)S(1)}, u32[]{:S(2)}, u32[]{:S(2)}) %collective-permute-start.2) | collective-permute-done | bytes 524320 | tf_op jit(solution)/shard_map/ppermute | solution.py:276
  108.1 4.5 %collective-permute-start.7 = (bf16[2,1024,128]{2,1,0:T(8,128)(2,1)S(1)}, bf16[2,1024,128]{2,1,0:T(8,128)(2,1)S(1)}, u32[]{:S(2)}, u32[]{:S(2)}) collective-permute-start(bf16[2,1024,128]{2,1,0:T(8,128)(2,1)S(1)} %bitcast.22), channel_id=1, source_target_pairs={{0,224},{8,232},{16,240},{24,248},{32,0},{40,8},{48,16},{56,24},{6... | collective-permute-start | bytes 1572872 | tf_op jit(solution)/shard_map/ppermute | solution.py:276
  112.6 0.1 constant_dynamic-update-slice_fusion.6
  112.7 8.0 %collective-permute-done.3 = bf16[2,1024,128]{2,1,0:T(8,128)(2,1)S(1)} collective-permute-done((bf16[2,1024,128]{2,1,0:T(8,128)(2,1)S(1)}, bf16[2,1024,128]{2,1,0:T(8,128)(2,1)S(1)}, u32[]{:S(2)}, u32[]{:S(2)}) %collective-permute-start.3) | collective-permute-done | bytes 524320 | tf_op jit(solution)/shard_map/ppermute | solution.py:276
  120.6 0.1 constant_dynamic-update-slice_fusion.5
  120.7 0.1 constant_dynamic-update-slice_fusion.4
  120.8 0.0 collective-permute-done.4
  120.8 0.1 constant_dynamic-update-slice_fusion.3
  120.9 0.0 copy-start.4
  120.9 0.0 copy-start.5
  120.9 0.0 copy-start.6
  120.9 0.0 collective-permute-done.5
  120.9 0.1 constant_dynamic-update-slice_fusion.2
  121.0 15.2 %collective-permute-done.6 = bf16[2,1024,128]{2,1,0:T(8,128)(2,1)S(1)} collective-permute-done((bf16[2,1024,128]{2,1,0:T(8,128)(2,1)S(1)}, bf16[2,1024,128]{2,1,0:T(8,128)(2,1)S(1)}, u32[]{:S(2)}, u32[]{:S(2)}) %collective-permute-start.6) | collective-permute-done | bytes 524320 | tf_op jit(solution)/shard_map/ppermute | solution.py:276
  136.2 0.1 constant_dynamic-update-slice_fusion.1
  136.3 13.8 %collective-permute-done.7 = bf16[2,1024,128]{2,1,0:T(8,128)(2,1)S(1)} collective-permute-done((bf16[2,1024,128]{2,1,0:T(8,128)(2,1)S(1)}, bf16[2,1024,128]{2,1,0:T(8,128)(2,1)S(1)}, u32[]{:S(2)}, u32[]{:S(2)}) %collective-permute-start.7) | collective-permute-done | bytes 524320 | tf_op jit(solution)/shard_map/ppermute | solution.py:276
  150.1 0.1 constant_dynamic-update-slice_fusion.kv_ref
  150.1 0.0 copy-start
  150.2 2.1 copy-done
  152.3 0.0 all-to-all-done.q_ref
  152.3 0.0 copy-done.7
  152.3 0.0 copy-done.8
  152.3 2.3 copy-done.1
  154.6 73.1 %attend.1 = bf16[8,128,128]{2,1,0:T(8,128)(2,1)S(1)} custom-call(s32[128]{0:T(128)S(1)} %bitcast.13, s32[128]{0:T(128)S(1)} %bitcast.14, s32[256]{0:T(256)S(1)} %copy-done.7, s32[2]{0:T(128)S(1)} %pad_add_fusion.place_ref, bf16[8,128,128]{2,1,0:T(8,128)(2,1)S(1)} %all-to-all-done.q_ref, bf16[18,1024,128]{2,1,0:T(8,128)(2,1)S(1)} %copy-done.1), custom_call_target="tpu_custom_call" | custom-call | tf_op jit(solution)/shard_map/attend/pallas_call | solution.py:225
  227.7 13.2 %all_to_all.16.packed_ref = bf16[8,128,128]{2,1,0:T(8,128)(2,1)S(1)} all-to-all(bf16[8,128,128]{2,1,0:T(8,128)(2,1)S(1)} %attend.1), channel_id=1, replica_groups=mesh['seq'=32,'head'=8] {'head'}, dimensions={0} | all-to-all | bytes 524288 | tf_op jit(solution)/shard_map/all_to_all | solution.py:294
  241.0 0.0 copy-done.6
  241.0 0.0 copy-start.2
  241.0 1.6 copy-done.2
  242.6 1.6 copy-done.3
  244.2 2.6 %finish.1 = bf16[256,512]{1,0:T(8,128)(2,1)} custom-call(bf16[256,512]{1,0:T(8,128)(2,1)S(1)} %copy-done.4, bf16[8,128,128]{2,1,0:T(8,128)(2,1)S(1)} %all_to_all.16.packed_ref, bf16[512,512]{1,0:T(8,128)(2,1)S(1)} %copy-done.5, f32[1,512]{1,0:T(1,128)S(1)} %bitcast.12, bf16[8,512,256]{2,1,0:T(8,128)(2,1)S(1)} %bitcast.10, bf16[8,256,512]{2,1,0:T(8,128)(2,1)S(1)} %bitcast.11), custom_call_target="tpu_custom_call" | custom-call | tf_op jit(solution)/shard_map/finish/pallas_call | solution.py:266
  (11 shorter events, 0.1 us)
Async XLA Ops:
  6.5 234.4 %all-gather.5.cloned.1.call-start = ((), (), s32[]{:S(2)}) async-start(), calls=%async_computation.3 | async-start | bytes 2359296 | tf_op jit(solution)/shard_map/all_gather | solution.py:282
  7.3 233.7 %all-gather.7.cloned.1.call-start = ((), (), s32[]{:S(2)}) async-start(), calls=%async_computation.4 | async-start | bytes 2359296 | tf_op jit(solution)/shard_map/all_gather | solution.py:283
  28.6 27.4 %collective-permute-start = (bf16[2,1024,128]{2,1,0:T(8,128)(2,1)S(1)}, bf16[2,1024,128]{2,1,0:T(8,128)(2,1)S(1)}, u32[]{:S(2)}, u32[]{:S(2)}) collective-permute-start(bf16[2,1024,128]{2,1,0:T(8,128)(2,1)S(1)} %bitcast.15), channel_id=1, source_target_pairs={{0,32},{8,40},{16,48},{24,56},{32,64},{40,72},{48,80},{56,88},{64,... | collective-permute-start | bytes 1572872 | tf_op jit(solution)/shard_map/ppermute | solution.py:276
  29.1 54.5 %collective-permute-start.1 = (bf16[2,1024,128]{2,1,0:T(8,128)(2,1)S(1)}, bf16[2,1024,128]{2,1,0:T(8,128)(2,1)S(1)}, u32[]{:S(2)}, u32[]{:S(2)}) collective-permute-start(bf16[2,1024,128]{2,1,0:T(8,128)(2,1)S(1)} %bitcast.16), channel_id=1, source_target_pairs={{0,24},{8,32},{16,40},{24,48},{32,56},{40,64},{48,72},{56,80},{64,... | collective-permute-start | bytes 1572872 | tf_op jit(solution)/shard_map/ppermute | solution.py:276
  34.4 73.8 %collective-permute-start.2 = (bf16[2,1024,128]{2,1,0:T(8,128)(2,1)S(1)}, bf16[2,1024,128]{2,1,0:T(8,128)(2,1)S(1)}, u32[]{:S(2)}, u32[]{:S(2)}) collective-permute-start(bf16[2,1024,128]{2,1,0:T(8,128)(2,1)S(1)} %bitcast.17), channel_id=1, source_target_pairs={{0,16},{8,24},{16,32},{24,40},{32,48},{40,56},{48,64},{56,72},{64,... | collective-permute-start | bytes 1572872 | tf_op jit(solution)/shard_map/ppermute | solution.py:276
  34.4 86.2 %collective-permute-start.3 = (bf16[2,1024,128]{2,1,0:T(8,128)(2,1)S(1)}, bf16[2,1024,128]{2,1,0:T(8,128)(2,1)S(1)}, u32[]{:S(2)}, u32[]{:S(2)}) collective-permute-start(bf16[2,1024,128]{2,1,0:T(8,128)(2,1)S(1)} %bitcast.18), channel_id=1, source_target_pairs={{0,8},{8,16},{16,24},{24,32},{32,40},{40,48},{48,56},{56,64},{64,7... | collective-permute-start | bytes 1572872 | tf_op jit(solution)/shard_map/ppermute | solution.py:276
  35.8 116.5 %all-to-all-start = ((bf16[8,128,128]{2,1,0:T(8,128)(2,1)}), bf16[8,128,128]{2,1,0:T(8,128)(2,1)S(1)}, u32[]{:S(2)}, u32[]{:S(2)}) async-start(bf16[8,128,128]{2,1,0:T(8,128)(2,1)} %get-tuple-element.7), calls=%async_computation | async-start | bytes 524288 | tf_op jit(solution)/shard_map/all_to_all | solution.py:286
  39.3 113.0 %copy-start.7 = (s32[256]{0:T(256)S(1)}, s32[256]{0:T(256)}, u32[]{:S(2)}) copy-start(s32[256]{0:T(256)} %counts_ref.1) | copy-start | bytes 3076
  39.3 113.0 %copy-start.8 = (s32[1,128,1]{1,2,0:T(1,128)S(1)}, s32[1,128,1]{1,2,0:T(1,128)}, u32[]{:S(2)}) copy-start(s32[1,128,1]{1,2,0:T(1,128)} %param.19) | copy-start | bytes 1540
  39.3 113.0 %copy-start.9 = (s32[1,128]{1,0:T(1,128)S(1)}, s32[1,128]{1,0:T(1,128)}, u32[]{:S(2)}) copy-start(s32[1,128]{1,0:T(1,128)} %param.20) | copy-start | bytes 1540
  39.3 81.5 %collective-permute-start.4 = (bf16[2,1024,128]{2,1,0:T(8,128)(2,1)S(1)}, bf16[2,1024,128]{2,1,0:T(8,128)(2,1)S(1)}, u32[]{:S(2)}, u32[]{:S(2)}) collective-permute-start(bf16[2,1024,128]{2,1,0:T(8,128)(2,1)S(1)} %bitcast.19), channel_id=1, source_target_pairs={{0,248},{8,0},{16,8},{24,16},{32,24},{40,32},{48,40},{56,48},{64,5... | collective-permute-start | bytes 1572872 | tf_op jit(solution)/shard_map/ppermute | solution.py:276
  56.0 64.9 %collective-permute-start.5 = (bf16[2,1024,128]{2,1,0:T(8,128)(2,1)S(1)}, bf16[2,1024,128]{2,1,0:T(8,128)(2,1)S(1)}, u32[]{:S(2)}, u32[]{:S(2)}) collective-permute-start(bf16[2,1024,128]{2,1,0:T(8,128)(2,1)S(1)} %bitcast.20), channel_id=1, source_target_pairs={{0,240},{8,248},{16,0},{24,8},{32,16},{40,24},{48,32},{56,40},{64,... | collective-permute-start | bytes 1572872 | tf_op jit(solution)/shard_map/ppermute | solution.py:276
  83.6 52.6 %collective-permute-start.6 = (bf16[2,1024,128]{2,1,0:T(8,128)(2,1)S(1)}, bf16[2,1024,128]{2,1,0:T(8,128)(2,1)S(1)}, u32[]{:S(2)}, u32[]{:S(2)}) collective-permute-start(bf16[2,1024,128]{2,1,0:T(8,128)(2,1)S(1)} %bitcast.21), channel_id=1, source_target_pairs={{0,232},{8,240},{16,248},{24,0},{32,8},{40,16},{48,24},{56,32},{64... | collective-permute-start | bytes 1572872 | tf_op jit(solution)/shard_map/ppermute | solution.py:276
  108.1 41.9 %collective-permute-start.7 = (bf16[2,1024,128]{2,1,0:T(8,128)(2,1)S(1)}, bf16[2,1024,128]{2,1,0:T(8,128)(2,1)S(1)}, u32[]{:S(2)}, u32[]{:S(2)}) collective-permute-start(bf16[2,1024,128]{2,1,0:T(8,128)(2,1)S(1)} %bitcast.22), channel_id=1, source_target_pairs={{0,224},{8,232},{16,240},{24,248},{32,0},{40,8},{48,16},{56,24},{6... | collective-permute-start | bytes 1572872 | tf_op jit(solution)/shard_map/ppermute | solution.py:276
  120.9 120.1 %copy-start.4 = (bf16[256,512]{1,0:T(8,128)(2,1)S(1)}, bf16[256,512]{1,0:T(8,128)(2,1)}, u32[]{:S(2)}) copy-start(bf16[256,512]{1,0:T(8,128)(2,1)} %points_ref.3) | copy-start | bytes 786436
  120.9 120.1 %copy-start.5 = (bf16[512,512]{1,0:T(8,128)(2,1)S(1)}, bf16[512,512]{1,0:T(8,128)(2,1)}, u32[]{:S(2)}) copy-start(bf16[512,512]{1,0:T(8,128)(2,1)} %w_out_ref.1) | copy-start | bytes 1572868
  120.9 120.1 %copy-start.6 = (f32[512]{0:T(512)S(1)}, f32[512]{0:T(512)}, u32[]{:S(2)}) copy-start(f32[512]{0:T(512)} %param.16) | copy-start | bytes 6148
  150.1 2.1 copy-start
  152.3 2.3 copy-start.1
  241.0 1.6 copy-start.2
  242.6 1.6 copy-start.3
Sparse Core Ops, SparseCore 0:
  9.2 29.2 all-gather.4
  40.4 27.1 all-gather.6

commit v2 on v1

--- a/solution.py
+++ b/solution.py
@@ -24,6 +24,7 @@
 BF16 = jnp.bfloat16
 MASKED = -3.3e38
 ROWS = 8 * LANES
+MESH = pl.DeviceIdType.MESH
 
 
 def placing():
@@ -81,20 +82,21 @@
 
 
 def attend_kernel(
-    slot_of, sides, routes_ref, local_ref, counts_ref, place_ref, q_ref, kv_ref, out_ref,
+    slot_of, routes_ref, counts_ref, q_ref, kv_ref, out_ref,
     raw, keys, vals, lhs, acc, top, sems,
 ):
-    seq = place_ref[0]
-    core = place_ref[1]
+    column, _, head_index = swap_ids()
+    seq = column * 8 + head_index
+    core = lax.rem(head_index, 2)
     own_slot = slot_of(0, core) * NPL
 
     def source(patch, which):
         if which == 0:
             return own_slot + patch, seq * GROUPS + patch * 4
         row = seq * NPL * CB + patch * CB + which - 1
-        route = routes_ref[row]
+        route = routes_ref[0, row]
         offset = jnp.where(route < REACH, route - REACH, route - REACH + 1)
-        local = local_ref[row]
+        local = routes_ref[1, row]
         owner = lax.rem(seq + offset + 32, 32)
         return slot_of(offset, core) * NPL + local, owner * GROUPS + local * 4
 
@@ -124,9 +126,9 @@
             if which == 0:
                 shard = seq * GROUPS + patch * 4
             else:
-                route = routes_ref[row]
+                route = routes_ref[0, row]
                 offset = jnp.where(route < REACH, route - REACH, route - REACH + 1)
-                shard = lax.rem(seq + offset + 32, 32) * GROUPS + local_ref[row] * 4
+                shard = lax.rem(seq + offset + 32, 32) * GROUPS + routes_ref[1, row] * 4
             for part in range(4):
                 count = counts_ref[shard + part]
                 block = raw[patch * 3 + which, TOK * part:TOK * part + TOK, :]
@@ -219,13 +221,13 @@
     lax.fori_loop(0, NPL, patch_body, 0)
 
 
-def attend(slot_of, place, routes, local, counts, q, kv):
+def attend(slot_of, routes, counts, q, kv):
     smem = pl.BlockSpec(memory_space=pltpu.SMEM)
     vmem = pl.BlockSpec(memory_space=pltpu.VMEM)
     return pl.pallas_call(
-        functools.partial(attend_kernel, slot_of, 0),
+        functools.partial(attend_kernel, slot_of),
         out_shape=jax.ShapeDtypeStruct((GROUPS, LANES, LANES), BF16),
-        in_specs=[smem, smem, smem, smem, vmem, pl.BlockSpec(memory_space=pl.ANY)],
+        in_specs=[smem, smem, vmem, pl.BlockSpec(memory_space=pl.ANY)],
         out_specs=vmem,
         scratch_shapes=[
             pltpu.VMEM((6, PATCH, LANES), BF16),
@@ -238,7 +240,7 @@
         ],
         compiler_params=pltpu.CompilerParams(vmem_limit_bytes=40 << 20),
         name="attend",
-    )(routes, local, counts, place, q, kv)
+    )(routes, counts, q, kv)
 
 
 def finish_kernel(points_ref, packed_ref, w_out_ref, gain_ref, w1_ref, w2_ref, out_ref):
@@ -271,9 +273,308 @@
     )(points, packed, w_out, gain.reshape(1, D), w1, w2)
 
 
-def passed_along(value, axis, steps):
-    count = lax.axis_size(axis)
-    return lax.ppermute(value, axis, [(source, (source + steps) % count) for source in range(count)])
+def swap_ids():
+    seq, head = lax.axis_index("seq"), lax.axis_index("head")
+    column = seq // 8
+    return column, seq - column * 8, head
+
+
+def exchange_kernel(
+    kv_ref, q_ref, route_ref, kv_out, q_out, route_out,
+    all_send, all_recv, ring_send, ring_recv, pair_send, pair_recv, route_sem, local_sem,
+):
+    column, plane, head = swap_ids()
+    core = lax.rem(head, 2)
+    spot = column * 4 + head // 2
+    after, before = lax.rem(spot + 1, 16), lax.rem(spot + 15, 16)
+    right = ((after // 4) * 8 + plane, lax.rem(after, 4) * 2 + core)
+    left = ((before // 4) * 8 + plane, lax.rem(before, 4) * 2 + core)
+    pair = (column * 8 + plane, head + 1 - 2 * core)
+    partner = (column * 8 + head, plane)
+    diagonal = plane == head
+    across = jnp.logical_not(diagonal)
+
+    barrier = pltpu.get_barrier_semaphore()
+
+    def greet(index, _):
+        @pl.when(across | (index != head))
+        def _():
+            pl.semaphore_signal(barrier, inc=1, device_id=(column * 8 + head, index), device_id_type=MESH)
+        return 0
+
+    lax.fori_loop(0, 8, greet, 0)
+    for other in (right, left, pair):
+        pl.semaphore_signal(barrier, inc=1, device_id=other, device_id_type=MESH)
+
+    @pl.when(diagonal)
+    def _():
+        pl.semaphore_wait(barrier, 10)
+
+    @pl.when(across)
+    def _():
+        pl.semaphore_wait(barrier, 11)
+
+    def rows(half):
+        return pl.ds(half * LANES, LANES)
+
+    def spread(group, half, shard):
+        return pltpu.make_async_remote_copy(
+            src_ref=kv_ref.at[group, rows(half)],
+            dst_ref=kv_out.at[4 + lax.rem(plane, 2), shard, rows(half)],
+            send_sem=all_send.at[half, group],
+            recv_sem=all_recv.at[half, shard],
+            device_id=(column * 8 + group, plane),
+            device_id_type=MESH,
+        )
+
+    def landed(half, shard):
+        return pltpu.make_async_remote_copy(
+            src_ref=kv_ref.at[0, rows(half)],
+            dst_ref=kv_out.at[4 + core, shard, rows(half)],
+            send_sem=all_send.at[half, 0],
+            recv_sem=all_recv.at[half, shard],
+            device_id=pair,
+            device_id_type=MESH,
+        )
+
+    def spread_q(group, shard):
+        return pltpu.make_async_remote_copy(
+            src_ref=q_ref.at[group],
+            dst_ref=q_out.at[shard],
+            send_sem=all_send.at[2, group],
+            recv_sem=all_recv.at[2, shard],
+            device_id=(column * 8 + group, plane),
+            device_id_type=MESH,
+        )
+
+    def at_home(half):
+        return pltpu.make_async_copy(
+            kv_ref.at[plane, rows(half)], kv_out.at[4 + core, head, rows(half)], local_sem.at[half]
+        )
+
+    q_at_home = pltpu.make_async_copy(q_ref.at[plane], q_out.at[head], local_sem.at[2])
+    route_at_home = pltpu.make_async_copy(route_ref, route_out, local_sem.at[3])
+    route_sent = pltpu.make_async_remote_copy(
+        src_ref=route_ref, dst_ref=route_out, send_sem=route_sem.at[0], recv_sem=route_sem.at[1],
+        device_id=partner, device_id_type=MESH,
+    )
+
+    def each(body):
+        def step(index, _):
+            body(index)
+            return 0
+
+        lax.fori_loop(0, 8, step, 0)
+
+    for half in range(2):
+        def start(group):
+            @pl.when(across | (group != plane))
+            def _():
+                spread(group, half, head).start()
+
+        each(start)
+
+    def start_q(group):
+        @pl.when(across | (group != plane))
+        def _():
+            spread_q(group, head).start()
+
+    each(start_q)
+
+    @pl.when(diagonal)
+    def _():
+        at_home(0).start()
+        at_home(1).start()
+        q_at_home.start()
+        route_at_home.start()
+
+    @pl.when(across)
+    def _():
+        route_sent.start()
+
+    def moved(source, target, half, send, recv, to):
+        return pltpu.make_async_remote_copy(
+            src_ref=kv_out.at[source, :, rows(half)], dst_ref=kv_out.at[target, :, rows(half)],
+            send_sem=send, recv_sem=recv, device_id=to, device_id_type=MESH,
+        )
+
+    def hop(way, step, half):
+        if way == 0:
+            source, to = 4 - 2 * step + core, right
+            target = 2 - 2 * step + core
+        else:
+            source, to = 4 + 2 * step + core, left
+            target = 6 + 2 * step + core
+        return moved(source, target, half, ring_send.at[way, step, half], ring_recv.at[way, step, half], to)
+
+    def shared(place, half):
+        return moved(2 * place + core, 2 * place + core, half, pair_send.at[place, half], pair_recv.at[place, half], pair)
+
+    def taken(place, half):
+        return moved(2 * place + 1 - core, 2 * place + 1 - core, half, pair_send.at[place, half], pair_recv.at[place, half], pair)
+
+    for half in range(2):
+        def wait(shard):
+            @pl.when(across | (shard != head))
+            def _():
+                landed(half, shard).wait_recv()
+
+        each(wait)
+
+        @pl.when(diagonal)
+        def _():
+            at_home(half).wait()
+
+        hop(0, 0, half).start()
+        hop(1, 0, half).start()
+        shared(2, half).start()
+    for half in range(2):
+        hop(0, 0, half).wait_recv()
+        hop(0, 1, half).start()
+        hop(1, 0, half).wait_recv()
+        hop(1, 1, half).start()
+        shared(1, half).start()
+        shared(3, half).start()
+    for half in range(2):
+        hop(0, 1, half).wait_recv()
+        shared(0, half).start()
+        hop(1, 1, half).wait_recv()
+        shared(4, half).start()
+
+    def wait_q(shard):
+        @pl.when(across | (shard != head))
+        def _():
+            spread_q(0, shard).wait_recv()
+
+    each(wait_q)
+
+    def sent(group):
+        @pl.when(across | (group != plane))
+        def _():
+            spread(group, 0, head).wait_send()
+            spread(group, 1, head).wait_send()
+            spread_q(group, head).wait_send()
+
+    each(sent)
+
+    @pl.when(diagonal)
+    def _():
+        q_at_home.wait()
+        route_at_home.wait()
+
+    @pl.when(across)
+    def _():
+        route_sent.wait()
+
+    for half in range(2):
+        for way in range(2):
+            for step in range(2):
+                hop(way, step, half).wait_send()
+        for place in range(5):
+            shared(place, half).wait_send()
+            taken(place, half).wait_recv()
+
+
+def exchange(kv, q, routes):
+    anywhere = pl.BlockSpec(memory_space=pl.ANY)
+    return pl.pallas_call(
+        exchange_kernel,
+        out_shape=(
+            jax.ShapeDtypeStruct((10, GROUPS, TOK, LANES), BF16),
+            jax.ShapeDtypeStruct((GROUPS, LANES, LANES), BF16),
+            jax.ShapeDtypeStruct((8, LANES), jnp.int32),
+        ),
+        in_specs=[anywhere] * 3,
+        out_specs=(anywhere,) * 3,
+        scratch_shapes=[
+            pltpu.SemaphoreType.DMA((3, 8)),
+            pltpu.SemaphoreType.DMA((3, 8)),
+            pltpu.SemaphoreType.DMA((2, 2, 2)),
+            pltpu.SemaphoreType.DMA((2, 2, 2)),
+            pltpu.SemaphoreType.DMA((5, 2)),
+            pltpu.SemaphoreType.DMA((5, 2)),
+            pltpu.SemaphoreType.DMA((2,)),
+            pltpu.SemaphoreType.DMA((4,)),
+        ],
+        compiler_params=pltpu.CompilerParams(collective_id=0, has_side_effects=True),
+        name="exchange",
+    )(kv, q, routes)
+
+
+def give_back_kernel(packed_ref, out_ref, send, recv, local_sem):
+    column, plane, head = swap_ids()
+    diagonal = plane == head
+    across = jnp.logical_not(diagonal)
+    barrier = pltpu.get_barrier_semaphore()
+
+    def each(body):
+        def step(index, _):
+            body(index)
+            return 0
+
+        lax.fori_loop(0, 8, step, 0)
+
+    def greet(group):
+        @pl.when(across | (group != plane))
+        def _():
+            pl.semaphore_signal(barrier, inc=1, device_id=(column * 8 + group, plane), device_id_type=MESH)
+
+    each(greet)
+
+    @pl.when(diagonal)
+    def _():
+        pl.semaphore_wait(barrier, 7)
+
+    @pl.when(across)
+    def _():
+        pl.semaphore_wait(barrier, 8)
+
+    def copy(shard, group):
+        return pltpu.make_async_remote_copy(
+            src_ref=packed_ref.at[shard], dst_ref=out_ref.at[group],
+            send_sem=send.at[shard], recv_sem=recv.at[group],
+            device_id=(column * 8 + head, shard), device_id_type=MESH,
+        )
+
+    at_home = pltpu.make_async_copy(packed_ref.at[head], out_ref.at[plane], local_sem.at[0])
+
+    def start(shard):
+        @pl.when(across | (shard != head))
+        def _():
+            copy(shard, plane).start()
+
+    each(start)
+
+    @pl.when(diagonal)
+    def _():
+        at_home.start()
+        at_home.wait()
+
+    def wait(index):
+        @pl.when(across | (index != plane))
+        def _():
+            copy(0, index).wait_recv()
+
+        @pl.when(across | (index != head))
+        def _():
+            copy(index, plane).wait_send()
+
+    each(wait)
+
+
+def give_back(packed):
+    vmem = pl.BlockSpec(memory_space=pltpu.VMEM)
+    return pl.pallas_call(
+        give_back_kernel,
+        out_shape=jax.ShapeDtypeStruct((GROUPS, LANES, LANES), BF16),
+        in_specs=[vmem],
+        out_specs=vmem,
+        scratch_shapes=[
+            pltpu.SemaphoreType.DMA((8,)), pltpu.SemaphoreType.DMA((8,)), pltpu.SemaphoreType.DMA((1,)),
+        ],
+        compiler_params=pltpu.CompilerParams(collective_id=1, has_side_effects=True),
+        name="give_back",
+    )(packed)
 
 
 def per_device(
@@ -281,17 +582,13 @@
 ):
     w1 = lax.all_gather(w_fc1, "head", axis=0)
     w2 = lax.all_gather(w_fc2, "head", axis=0)
+    routes = jnp.concatenate([contact_route.reshape(1, -1), contact_patch, jnp.zeros((6, LANES), jnp.int32)])
     kv, q = project(points, gain_attn, w_qkv)
-    kv = lax.all_to_all(kv, "head", split_axis=0, concat_axis=0, tiled=True)
-    q = lax.all_to_all(q, "head", split_axis=0, concat_axis=0, tiled=True)
-    own = kv.reshape(NPL, PATCH, LANES)
-    slots = [own if offset == 0 else passed_along(own, "seq", -offset) for offset in range(-REACH, REACH + 1)]
-    slots = jnp.concatenate(slots, axis=0)
-    place = jnp.stack([lax.axis_index("seq"), jnp.int32(0)])
+    slots, q, routes = exchange(kv, q, routes)
     packed = attend(
-        lambda offset, core: offset + REACH, place, contact_route.reshape(-1), contact_patch.reshape(-1), counts, q, slots
+        lambda offset, core: offset + REACH + core, routes, counts, q, slots.reshape(20, PATCH, LANES)
     )
-    packed = lax.all_to_all(packed, "head", split_axis=0, concat_axis=0, tiled=True)
+    packed = give_back(packed)
     return finish(points, packed, w_out, gain_mlp, w1, w2)
 
 

time: 254 us -> 187 us (0.74)
  the two profiles are of different devices: /device:TPU:228 before, /device:TPU:95 now
where the time goes in v2:
time: 187 us; the launch traced here: 186 us
  Pallas kernels  162 us (87%)
  between operations  13.5 us (7%)
  local copies, waits for them, and re-layouts  9.02 us (5%)
    pallas_call x1, Pallas kernels, attend(): pl.pallas_call(functools.partial(attend_kernel, slot_of), out_shape=jax.S...  76.8 us
    pallas_call x1, Pallas kernels, exchange(): pl.pallas_call(exchange_kernel, out_shape=(jax.ShapeDtypeStruct((10, GROU...  52.8 us
    pallas_call x1, Pallas kernels, give_back(): pl.pallas_call(give_back_kernel, out_shape=jax.ShapeDtypeStruct((GROUPS,...  25.1 us
    unnamed x26, local copies, waits for them, and re-layouts  8.95 us
    pallas_call x1, Pallas kernels, project(): pl.pallas_call(project_kernel, out_shape=(jax.ShapeDtypeStruct((GROUPS, T...  4.21 us
  transfers between devices with their start and end apart: 2, of which 0 were waited for; matrix products, arithmetic and copies ran while one was open for 0% of the time, Pallas kernels for 85%

profile of v2, /device:TPU:95, one launch (start us, length us, event | category | flops | bytes accessed | tf_op | source)
XLA Modules:
  0.0 186.2 jit_solution(5513881166433162772)
XLA Ops:
  6.5 0.0 copy-start.12
  6.5 0.0 copy-start.11
  6.5 0.0 copy-start.10
  6.5 0.0 all-gather.5.cloned.1.call-start
  6.5 0.7 all-gather.5.cloned.1.call-update
  7.3 0.0 all-gather.7.cloned.1.call-start
  7.3 0.7 all-gather.7.cloned.1.call-update
  8.0 0.1 pad.2.clone
  8.1 4.2 %project.1 = (bf16[8,256,128]{2,1,0:T(8,128)(2,1)}, bf16[8,128,128]{2,1,0:T(8,128)(2,1)}) custom-call(bf16[256,512]{1,0:T(8,128)(2,1)} %points_ref.3, f32[1,512]{1,0:T(1,128)} %bitcast.10, bf16[512,1536]{1,0:T(8,128)(2,1)} %w_ref.1, f32[1,1536]{1,0:T(1,128)} %constant.6.clone.scale_ref, bf16[384,768]{1,0:T(8,128)(2,1)} %constant.7.clone.place_ref), custom_call_target="tpu_custom_call" | custom-call | tf_op jit(solution)/shard_map/project/pallas_call | solution.py:74
  12.3 0.0 copy-done.12
  12.3 0.0 copy-done.11
  12.3 0.7 add_add_fusion.route_ref
  13.0 52.8 %exchange.1 = (bf16[10,8,256,128]{3,2,1,0:T(8,128)(2,1)}, bf16[8,128,128]{2,1,0:T(8,128)(2,1)}, s32[8,128]{1,0:T(8,128)}) custom-call(bf16[8,256,128]{2,1,0:T(8,128)(2,1)} %get-tuple-element.10.kv_ref, bf16[8,128,128]{2,1,0:T(8,128)(2,1)} %get-tuple-element.11.q_ref, s32[8,128]{1,0:T(8,128)} %add_add_fusion.route_ref), custom_call_target="tpu_custom_call" | custom-call | tf_op jit(solution)/shard_map/exchange/pallas_call | solution.py:480
  65.8 0.0 copy-done.10
  65.8 0.0 copy-start
  65.8 2.5 %copy-done = bf16[10,8,256,128]{3,2,1,0:T(8,128)(2,1)S(1)} copy-done((bf16[10,8,256,128]{3,2,1,0:T(8,128)(2,1)S(1)}, bf16[10,8,256,128]{3,2,1,0:T(8,128)(2,1)}, u32[]{:S(2)}) %copy-start) | copy-done | bytes 5242904
  68.3 0.0 copy-start.7
  68.3 0.9 copy-done.7
  69.2 0.0 copy-start.8
  69.2 0.7 copy-done.8
  69.9 0.0 copy-start.3
  69.9 0.0 copy-start.6
  69.9 0.0 copy-start.9
  69.9 76.8 %attend.1.packed_ref = bf16[8,128,128]{2,1,0:T(8,128)(2,1)S(1)} custom-call(s32[8,128]{1,0:T(8,128)S(1)} %copy-done.8, s32[256]{0:T(256)S(1)} %copy-done.10, bf16[8,128,128]{2,1,0:T(8,128)(2,1)S(1)} %copy-done.7, bf16[20,1024,128]{2,1,0:T(8,128)(2,1)S(1)} %bitcast.6), custom_call_target="tpu_custom_call" | custom-call | tf_op jit(solution)/shard_map/attend/pallas_call | solution.py:227
  146.7 0.0 copy-start.5
  146.7 0.7 copy-done.5
  147.4 25.1 %give_back.1.packed_ref = bf16[8,128,128]{2,1,0:T(8,128)(2,1)} custom-call(bf16[8,128,128]{2,1,0:T(8,128)(2,1)} %copy-done.5), custom_call_target="tpu_custom_call" | custom-call | tf_op jit(solution)/shard_map/give_back/pallas_call | solution.py:567
  172.5 0.0 all-gather.5.cloned.1.call-done
  172.6 0.0 all-gather.7.cloned.1.call-done
  172.6 0.0 copy-done.3
  172.6 0.0 copy-done.6
  172.6 0.0 copy-done.9
  172.6 0.0 copy-start.1
  172.6 1.6 copy-done.1
  174.2 0.0 copy-start.2
  174.2 1.6 copy-done.2
  175.8 0.0 copy-start.4
  175.8 0.9 copy-done.4
  176.8 2.6 %finish.1 = bf16[256,512]{1,0:T(8,128)(2,1)} custom-call(bf16[256,512]{1,0:T(8,128)(2,1)S(1)} %copy-done.3, bf16[8,128,128]{2,1,0:T(8,128)(2,1)S(1)} %copy-done.4, bf16[512,512]{1,0:T(8,128)(2,1)S(1)} %copy-done.6, f32[1,512]{1,0:T(1,128)S(1)} %bitcast.9, bf16[8,512,256]{2,1,0:T(8,128)(2,1)S(1)} %bitcast.7, bf16[8,256,512]{2,1,0:T(8,128)(2,1)S(1)} %bitcast.8), custom_call_target="tpu_custom_call" | custom-call | tf_op jit(solution)/shard_map/finish/pallas_call | solution.py:268
  (1 shorter events, 0.0 us)
Async XLA Ops:
  6.5 5.8 %copy-start.12 = (s32[1,128,1]{1,2,0:T(1,128)S(1)}, s32[1,128,1]{1,2,0:T(1,128)}, u32[]{:S(2)}) copy-start(s32[1,128,1]{1,2,0:T(1,128)} %param.19) | copy-start | bytes 1540
  6.5 5.8 %copy-start.11 = (s32[1,128]{1,0:T(1,128)S(1)}, s32[1,128]{1,0:T(1,128)}, u32[]{:S(2)}) copy-start(s32[1,128]{1,0:T(1,128)} %param.20) | copy-start | bytes 1540
  6.5 59.3 %copy-start.10 = (s32[256]{0:T(256)S(1)}, s32[256]{0:T(256)}, u32[]{:S(2)}) copy-start(s32[256]{0:T(256)} %counts_ref.1) | copy-start | bytes 3076
  6.5 166.0 %all-gather.5.cloned.1.call-start = ((), (), s32[]{:S(2)}) async-start(), calls=%async_computation | async-start | bytes 2359296 | tf_op jit(solution)/shard_map/all_gather | solution.py:583
  7.3 165.3 %all-gather.7.cloned.1.call-start = ((), (), s32[]{:S(2)}) async-start(), calls=%async_computation.1 | async-start | bytes 2359296 | tf_op jit(solution)/shard_map/all_gather | solution.py:584
  65.8 2.5 %copy-start = (bf16[10,8,256,128]{3,2,1,0:T(8,128)(2,1)S(1)}, bf16[10,8,256,128]{3,2,1,0:T(8,128)(2,1)}, u32[]{:S(2)}) copy-start(bf16[10,8,256,128]{3,2,1,0:T(8,128)(2,1)} %get-tuple-element.14) | copy-start | bytes 15728644
  68.3 0.9 copy-start.7
  69.2 0.7 copy-start.8
  69.9 102.7 %copy-start.3 = (bf16[256,512]{1,0:T(8,128)(2,1)S(1)}, bf16[256,512]{1,0:T(8,128)(2,1)}, u32[]{:S(2)}) copy-start(bf16[256,512]{1,0:T(8,128)(2,1)} %points_ref.3) | copy-start | bytes 786436
  69.9 102.7 %copy-start.6 = (bf16[512,512]{1,0:T(8,128)(2,1)S(1)}, bf16[512,512]{1,0:T(8,128)(2,1)}, u32[]{:S(2)}) copy-start(bf16[512,512]{1,0:T(8,128)(2,1)} %w_out_ref.1) | copy-start | bytes 1572868
  69.9 102.7 %copy-start.9 = (f32[512]{0:T(512)S(1)}, f32[512]{0:T(512)}, u32[]{:S(2)}) copy-start(f32[512]{0:T(512)} %param.16) | copy-start | bytes 6148
  146.7 0.7 copy-start.5
  172.6 1.6 copy-start.1
  174.2 1.6 copy-start.2
  175.8 0.9 copy-start.4
Sparse Core Ops, SparseCore 0:
  9.2 56.8 all-gather.4
  68.0 27.2 all-gather.6

commit v3 on v2

v3 whole, which is shorter than its diff:
```python
import functools
import math

import jax
import jax.numpy as jnp
import numpy as np
from jax import lax
from jax.experimental import pallas as pl
from jax.experimental.pallas import tpu as pltpu
from jax.sharding import PartitionSpec as P

D = 512
HEADS = 32
HEAD_DIM = 16
PATCH = 1024
CB = 2
NPL = 2
REACH = 4
TOK = 256
GROUPS = 8
LANES = 128
CHUNK = 512
F32 = jnp.float32
BF16 = jnp.bfloat16
MASKED = -3.3e38
ROWS = 8 * LANES
MESH = pl.DeviceIdType.MESH


def placing():
    kv = np.zeros((384, 256), np.float32)
    low = np.zeros((384, 256), np.float32)
    high = np.zeros((384, 256), np.float32)
    for group in range(2):
        for head in range(4):
            for dim in range(HEAD_DIM):
                source = group * 192 + head * 48 + dim
                lane = group * 128 + head * 16 + dim
                low[source, lane] = 1
                high[source, lane + 64] = 1
                kv[source + 16, lane] = 1
                kv[source + 32, lane + 64] = 1
    return np.concatenate([kv, low, high], axis=1)


def lane_of(shape):
    return lax.broadcasted_iota(jnp.int32, shape, len(shape) - 1)


def normalise(values, gain):
    centred = values - jnp.mean(values, axis=-1, keepdims=True)
    spread = jnp.mean(centred * centred, axis=-1, keepdims=True)
    return centred * lax.rsqrt(spread + 1e-05) * gain


def project_kernel(points_ref, gain_ref, w_ref, scale_ref, place_ref, kv_ref, q_ref):
    normed = normalise(points_ref[...].astype(F32), gain_ref[...]).astype(BF16)
    for pair in range(GROUPS // 2):
        columns = slice(384 * pair, 384 * pair + 384)
        projected = jnp.dot(normed, w_ref[:, columns], preferred_element_type=F32)
        projected = (projected * scale_ref[:, columns]).astype(BF16)
        kv = jnp.dot(projected, place_ref[:, :256], preferred_element_type=F32).astype(BF16)
        q = jnp.dot(projected[:128], place_ref[:, 256:512], preferred_element_type=F32)
        q = q + jnp.dot(projected[128:], place_ref[:, 512:], preferred_element_type=F32)
        q = q.astype(BF16)
        for side in range(2):
            kv_ref[2 * pair + side] = kv[:, 128 * side:128 * side + 128]
            q_ref[2 * pair + side] = q[:, 128 * side:128 * side + 128]


def project(points, gain, w_qkv):
    scale = np.ones((1, 1536), np.float32)
    scale[0, np.arange(1536) % 48 < 16] = HEAD_DIM ** -0.5 * math.log2(math.e)
    return pl.pallas_call(
        project_kernel,
        out_shape=(
            jax.ShapeDtypeStruct((GROUPS, TOK, LANES), BF16),
            jax.ShapeDtypeStruct((GROUPS, LANES, LANES), BF16),
        ),
        name="project",
    )(points, gain.reshape(1, D), w_qkv, jnp.asarray(scale), jnp.asarray(placing(), BF16))


def swap_ids():
    seq, head = lax.axis_index("seq"), lax.axis_index("head")
    column = seq // 8
    return column, seq - column * 8, head


def attend_kernel(
    routes_hbm, local_hbm, counts_hbm, q_hbm, kv_ref, out_ref,
    routes_ref, local_ref, counts_ref, q_ref, raw, keys, vals, turned, lhs, acc, top, done, sems, small_sems, out_sems,
):
    column, _, head_index = swap_ids()
    seq = column * 8 + head_index
    core = lax.rem(head_index, 2)
    loads = [
        pltpu.make_async_copy(routes_hbm, routes_ref, small_sems.at[0]),
        pltpu.make_async_copy(local_hbm, local_ref, small_sems.at[1]),
        pltpu.make_async_copy(counts_hbm, counts_ref, small_sems.at[2]),
        pltpu.make_async_copy(q_hbm, q_ref, small_sems.at[3]),
    ]
    for load in loads:
        load.start()
    for load in loads[:3]:
        load.wait()

    def source(patch, which):
        if which == 0:
            return (REACH + core) * NPL + patch, seq * GROUPS + patch * 4
        row = seq * NPL * CB + patch * CB + which - 1
        route = routes_ref[0, row]
        offset = jnp.where(route < REACH, route - REACH, route - REACH + 1)
        local = local_ref[0, row]
        owner = lax.rem(seq + offset + 32, 32)
        return (offset + REACH + core) * NPL + local, owner * GROUPS + local * 4

    for patch in range(NPL):
        for which in range(CB + 1):
            slot, _ = source(patch, which)
            pltpu.make_async_copy(kv_ref.at[slot], raw.at[patch * 3 + which], sems.at[patch * 3 + which]).start()
    loads[3].wait()

    lane_kv = lane_of((TOK, LANES))
    row_kv = lax.broadcasted_iota(jnp.int32, (TOK, LANES), 0)
    lane_q = lane_of((LANES, LANES))
    row_q = lax.broadcasted_iota(jnp.int32, (LANES, LANES), 0)
    zero = jnp.zeros((TOK, LANES), BF16)
    low_lane = lane_kv < 64
    sum_of = ((lane_q == row_q // 16) & (lane_q < 4)).astype(F32).astype(BF16)
    value_of = ((row_q % 32 < 16) & (lane_q == 64 + row_q // 32 * 16 + row_q % 32)).astype(F32).astype(BF16)
    ones_row = lax.broadcasted_iota(jnp.int32, (LANES, CHUNK), 0) % 32 >= 16

    def patch_body(patch, _):
        for which in range(CB + 1):
            pltpu.make_async_copy(kv_ref.at[0], raw.at[patch * 3 + which], sems.at[patch * 3 + which]).wait()

        first = jnp.int32(0)
        key_top = jnp.zeros((1, LANES), F32)
        val_top = jnp.zeros((1, LANES), F32)
        for which in range(CB + 1):
            _, shard = source(patch, which)
            for part in range(4):
                count = counts_ref[shard + part]
                block = raw[patch * 3 + which, TOK * part:TOK * part + TOK, :]
                valid = row_kv < count
                flag = jnp.where(valid, zero, jnp.where(lane_kv < 66, jnp.full_like(zero, MASKED), zero))
                keyed = jnp.where(low_lane & valid, block, zero)
                at = pl.ds(pl.multiple_of(first, 16), TOK)
                keys[at, :] = jnp.where(low_lane, keyed, flag)
                vals[at, :] = block
                squares = jnp.dot(keyed * keyed, sum_of, preferred_element_type=F32)
                key_top = jnp.maximum(key_top, jnp.max(squares, axis=0, keepdims=True))
                size = jnp.max(jnp.where(low_lane, zero, jnp.abs(block)).astype(F32), axis=0, keepdims=True)
                val_top = jnp.maximum(val_top, size)
                first = first + (count + 15) // 16 * 16
        for more in range(CHUNK // TOK):
            tail = pl.ds(pl.multiple_of(first + more * TOK, 16), TOK)
            keys[tail, :] = jnp.where(low_lane | (lane_kv >= 66), zero, jnp.full_like(zero, MASKED))
            vals[tail, :] = zero
        chunks = (first + CHUNK - 1) // CHUNK

        def turn(chunk, _):
            at = pl.ds(pl.multiple_of(chunk * CHUNK, CHUNK), CHUNK)
            picked = lax.dot_general(value_of, vals[at, :], (((1,), (1,)), ((), ())), preferred_element_type=F32)
            turned[:, at] = jnp.where(ones_row, 1.0, picked).astype(BF16)
            return 0

        lax.fori_loop(0, chunks, turn, 0)

        query_top = jnp.zeros((1, LANES), F32)
        for part in range(4):
            packed = q_ref[patch * 4 + part]
            for half in range(2):
                q = packed if half == 0 else pltpu.roll(packed.astype(F32), 64, 1).astype(BF16)
                q = jnp.where(lane_q < 64, q, jnp.zeros_like(q))
                squares = jnp.dot(q * q, sum_of, preferred_element_type=F32)
                query_top = jnp.maximum(query_top, jnp.max(squares, axis=0, keepdims=True))
        bound = jnp.max(query_top * key_top)
        small = (bound < 3000.0) & (jnp.max(val_top) < 1e9)

        def shard_body(part, _):
            packed = q_ref[patch * 4 + part]
            flags = jnp.where((lane_q >= 64) & (lane_q < 66), jnp.ones_like(packed), jnp.zeros_like(packed))
            for half in range(2):
                q = packed if half == 0 else pltpu.roll(packed.astype(F32), 64, 1).astype(BF16)
                for head in range(4):
                    mine = (lane_q >= 16 * head) & (lane_q < 16 * head + 16)
                    lhs[pl.ds((head * 2 + half) * LANES, LANES), :] = jnp.where(mine, q, flags)
            acc[...] = jnp.zeros_like(acc)

            def scores_of(chunk):
                at = pl.ds(pl.multiple_of(chunk * CHUNK, CHUNK), CHUNK)
                return at, lax.dot_general(
                    keys[at, :], lhs[...], (((1,), (1,)), ((), ())), preferred_element_type=F32
                )

            def gather(at, weights):
                for head in range(4):
                    rows = slice(32 * head, 32 * head + 32)
                    acc[rows] += jnp.dot(
                        turned[rows, at], weights[:, TOK * head:TOK * head + TOK], preferred_element_type=F32
                    )

            @pl.when(small)
            def _():
                def chunk_body(chunk, _):
                    at, scores = scores_of(chunk)
                    gather(at, jnp.exp2(scores).astype(BF16))
                    return 0

                lax.fori_loop(0, chunks, chunk_body, 0)

            @pl.when(jnp.logical_not(small))
            def _():
                top[...] = jnp.full_like(top, -jnp.inf)

                def top_body(chunk, _):
                    _, scores = scores_of(chunk)
                    top[...] = jnp.maximum(top[...], jnp.max(scores, axis=0, keepdims=True))
                    return 0

                lax.fori_loop(0, chunks, top_body, 0)

                def chunk_body(chunk, _):
                    at, scores = scores_of(chunk)
                    gather(at, jnp.exp2(scores - top[...]).astype(BF16))
                    return 0

                lax.fori_loop(0, chunks, chunk_body, 0)

            joined = [acc[32 * head:32 * head + 16] / acc[32 * head + 16:32 * head + 32] for head in range(4)]
            done[patch * 4 + part] = jnp.concatenate(joined, axis=0).astype(BF16)
            pltpu.make_async_copy(
                done.at[patch * 4 + part], out_ref.at[patch * 4 + part], out_sems.at[patch * 4 + part]
            ).start()
            return 0

        lax.fori_loop(0, 4, shard_body, 0)
        return 0

    lax.fori_loop(0, NPL, patch_body, 0)
    for shard in range(GROUPS):
        pltpu.make_async_copy(done.at[shard], out_ref.at[shard], out_sems.at[shard]).wait()


def attend(routes, local, counts, q, kv):
    hbm = pl.BlockSpec(memory_space=pltpu.HBM)
    return pl.pallas_call(
        attend_kernel,
        out_shape=jax.ShapeDtypeStruct((GROUPS, 64, TOK), BF16),
        in_specs=[hbm] * 5,
        out_specs=hbm,
        scratch_shapes=[
            pltpu.SMEM((1, LANES), jnp.int32),
            pltpu.SMEM((1, LANES), jnp.int32),
            pltpu.SMEM((256,), jnp.int32),
            pltpu.VMEM((GROUPS, LANES, LANES), BF16),
            pltpu.VMEM((6, PATCH, LANES), BF16),
            pltpu.VMEM((3 * PATCH + CHUNK, LANES), BF16),
            pltpu.VMEM((3 * PATCH + CHUNK, LANES), BF16),
            pltpu.VMEM((LANES, 3 * PATCH + CHUNK), BF16),
            pltpu.VMEM((ROWS, LANES), BF16),
            pltpu.VMEM((LANES, TOK), F32),
            pltpu.VMEM((1, ROWS), F32),
            pltpu.VMEM((GROUPS, 64, TOK), BF16),
            pltpu.SemaphoreType.DMA((6,)),
            pltpu.SemaphoreType.DMA((4,)),
            pltpu.SemaphoreType.DMA((8,)),
        ],
        compiler_params=pltpu.CompilerParams(vmem_limit_bytes=40 << 20),
        name="attend",
    )(routes, local, counts, q, kv)


def each(body):
    def step(index, _):
        body(index)
        return 0

    lax.fori_loop(0, 8, step, 0)


def finish_kernel(
    points_ref, packed_ref, w_out_ref, gain_ref, w1_ref, w2_ref, out_ref,
    points, w_out, gain, w1, w2, back, send, recv, local_sem, load_sem, weight_sem,
):
    column, plane, head = swap_ids()
    diagonal = plane == head
    across = jnp.logical_not(diagonal)
    barrier = pltpu.get_barrier_semaphore()

    def greet(group):
        @pl.when(across | (group != plane))
        def _():
            pl.semaphore_signal(barrier, inc=1, device_id=(column * 8 + group, plane), device_id_type=MESH)

    each(greet)
    loads = [
        pltpu.make_async_copy(points_ref, points, load_sem.at[0]),
        pltpu.make_async_copy(w_out_ref, w_out, load_sem.at[1]),
        pltpu.make_async_copy(gain_ref, gain, load_sem.at[2]),
    ]
    for load in loads:
        load.start()

    def weights(part):
        return (
            pltpu.make_async_copy(w1_ref.at[part], w1.at[part], weight_sem.at[0, part]),
            pltpu.make_async_copy(w2_ref.at[part], w2.at[part], weight_sem.at[1, part]),
        )

    for part in range(GROUPS):
        for copy in weights(part):
            copy.start()

    @pl.when(diagonal)
    def _():
        pl.semaphore_wait(barrier, 7)

    @pl.when(across)
    def _():
        pl.semaphore_wait(barrier, 8)

    def copy(shard, group):
        return pltpu.make_async_remote_copy(
            src_ref=packed_ref.at[shard], dst_ref=back.at[group],
            send_sem=send.at[shard], recv_sem=recv.at[group],
            device_id=(column * 8 + head, shard), device_id_type=MESH,
        )

    at_home = pltpu.make_async_copy(packed_ref.at[head], back.at[plane], local_sem.at[0])

    def start(shard):
        @pl.when(across | (shard != head))
        def _():
            copy(shard, plane).start()

    each(start)

    @pl.when(diagonal)
    def _():
        at_home.start()
        at_home.wait()

    for load in loads:
        load.wait()

    def wait(index):
        @pl.when(across | (index != plane))
        def _():
            copy(0, index).wait_recv()

    each(wait)

    attended = back[...].reshape(D, TOK)
    updated = points[...].astype(F32) + lax.dot_general(
        attended, w_out[...], (((0,), (0,)), ((), ())), preferred_element_type=F32
    )
    updated = updated.astype(BF16).astype(F32)
    normed = normalise(updated, gain[...]).astype(BF16)
    total = updated
    for part in range(GROUPS):
        for load in weights(part):
            load.wait()
        hidden = jnp.dot(normed, w1[part], preferred_element_type=F32)
        hidden = hidden * (0.5 * (1.0 + lax.erf(hidden * (2.0 ** -0.5))))
        total = total + jnp.dot(hidden.astype(BF16), w2[part], preferred_element_type=F32)
    out_ref[...] = total.astype(BF16)

    def sent(index):
        @pl.when(across | (index != head))
        def _():
            copy(index, plane).wait_send()

    each(sent)


def finish(points, packed, w_out, gain, w1, w2):
    hbm = pl.BlockSpec(memory_space=pltpu.HBM)
    return pl.pallas_call(
        finish_kernel,
        out_shape=jax.ShapeDtypeStruct((TOK, D), BF16),
        in_specs=[hbm] * 6,
        out_specs=pl.BlockSpec(memory_space=pltpu.VMEM),
        scratch_shapes=[
            pltpu.VMEM((TOK, D), BF16),
            pltpu.VMEM((D, D), BF16),
            pltpu.VMEM((1, D), F32),
            pltpu.VMEM((GROUPS, D, 256), BF16),
            pltpu.VMEM((GROUPS, 256, D), BF16),
            pltpu.VMEM((GROUPS, 64, TOK), BF16),
            pltpu.SemaphoreType.DMA((8,)),
            pltpu.SemaphoreType.DMA((8,)),
            pltpu.SemaphoreType.DMA((1,)),
            pltpu.SemaphoreType.DMA((3,)),
            pltpu.SemaphoreType.DMA((2, 8)),
        ],
        compiler_params=pltpu.CompilerParams(
            collective_id=1, has_side_effects=True, vmem_limit_bytes=40 << 20
        ),
        name="finish",
    )(points, packed, w_out, gain.reshape(1, D), w1, w2)


def exchange_kernel(
    kv_ref, q_ref, route_ref, local_ref, w1_ref, w2_ref, kv_out, q_out, route_out, local_out, w1_out, w2_out,
    all_send, all_recv, ring_send, ring_recv, pair_send, pair_recv, route_sem, local_sem,
    down_send, down_recv, over_send, over_recv, share_send, share_recv,
):
    column, plane, head = swap_ids()
    core = lax.rem(head, 2)
    spot = column * 4 + head // 2
    after, before = lax.rem(spot + 1, 16), lax.rem(spot + 15, 16)
    right = ((after // 4) * 8 + plane, lax.rem(after, 4) * 2 + core)
    left = ((before // 4) * 8 + plane, lax.rem(before, 4) * 2 + core)
    pair = (column * 8 + plane, head + 1 - 2 * core)
    partner = (column * 8 + head, plane)
    diagonal = plane == head
    across = jnp.logical_not(diagonal)

    barrier = pltpu.get_barrier_semaphore()

    def greet(index, _):
        @pl.when(across | (index != head))
        def _():
            pl.semaphore_signal(barrier, inc=1, device_id=(column * 8 + head, index), device_id_type=MESH)
        return 0

    lax.fori_loop(0, 8, greet, 0)
    level = head // 2
    downs = [(column * 8 + plane, lax.rem(level + step, 4) * 2 + core) for step in range(1, 4)]
    overs = [(lax.rem(column + step, 4) * 8 + plane, head) for step in range(1, 4)]
    for other in (right, left, pair, *downs, *overs):
        pl.semaphore_signal(barrier, inc=1, device_id=other, device_id_type=MESH)

    @pl.when(diagonal)
    def _():
        pl.semaphore_wait(barrier, 16)

    @pl.when(across)
    def _():
        pl.semaphore_wait(barrier, 17)

    def rows(half):
        return pl.ds(half * LANES, LANES)

    def spread(group, half, shard):
        return pltpu.make_async_remote_copy(
            src_ref=kv_ref.at[group, rows(half)],
            dst_ref=kv_out.at[4 + lax.rem(plane, 2), shard, rows(half)],
            send_sem=all_send.at[half, group],
            recv_sem=all_recv.at[half, shard],
            device_id=(column * 8 + group, plane),
            device_id_type=MESH,
        )

    def landed(half, shard):
        return pltpu.make_async_remote_copy(
            src_ref=kv_ref.at[0, rows(half)],
            dst_ref=kv_out.at[4 + core, shard, rows(half)],
            send_sem=all_send.at[half, 0],
            recv_sem=all_recv.at[half, shard],
            device_id=pair,
            device_id_type=MESH,
        )

    def spread_q(group, shard):
        return pltpu.make_async_remote_copy(
            src_ref=q_ref.at[group],
            dst_ref=q_out.at[shard],
            send_sem=all_send.at[2, group],
            recv_sem=all_recv.at[2, shard],
            device_id=(column * 8 + group, plane),
            device_id_type=MESH,
        )

    def at_home(half):
        return pltpu.make_async_copy(
            kv_ref.at[plane, rows(half)], kv_out.at[4 + core, head, rows(half)], local_sem.at[half]
        )

    q_at_home = pltpu.make_async_copy(q_ref.at[plane], q_out.at[head], local_sem.at[2])
    routes_at_home = [
        pltpu.make_async_copy(route_ref, route_out, local_sem.at[3]),
        pltpu.make_async_copy(local_ref, local_out, local_sem.at[4]),
    ]
    routes_sent = [
        pltpu.make_async_remote_copy(
            src_ref=source, dst_ref=target, send_sem=route_sem.at[0, index], recv_sem=route_sem.at[1, index],
            device_id=partner, device_id_type=MESH,
        )
        for index, (source, target) in enumerate(((route_ref, route_out), (local_ref, local_out)))
    ]

    slabs = (
        (w1_ref, w1_out, pl.ds(column * LANES, LANES)),
        (w2_ref, w2_out, pl.ds(column * 64, 64)),
    )
    weights_at_home = [
        pltpu.make_async_copy(source, target.at[core, level], local_sem.at[5 + index])
        for index, (source, target, _) in enumerate(slabs)
    ]

    def down(index, step):
        source, target, quarter = slabs[index]
        return pltpu.make_async_remote_copy(
            src_ref=source.at[quarter], dst_ref=target.at[core, level, quarter],
            send_sem=down_send.at[index, step - 1], recv_sem=down_recv.at[index, step - 1],
            device_id=downs[step - 1], device_id_type=MESH,
        )

    def over(index, rise, step):
        _, target, quarter = slabs[index]
        spot_of = target.at[core, lax.rem(level + 4 - rise, 4), quarter]
        return pltpu.make_async_remote_copy(
            src_ref=spot_of, dst_ref=spot_of,
            send_sem=over_send.at[index, rise - 1, step - 1], recv_sem=over_recv.at[index, rise - 1, step - 1],
            device_id=overs[step - 1], device_id_type=MESH,
        )

    def share(index):
        _, target, _ = slabs[index]
        return pltpu.make_async_remote_copy(
            src_ref=target.at[core], dst_ref=target.at[core],
            send_sem=share_send.at[index], recv_sem=share_recv.at[index], device_id=pair, device_id_type=MESH,
        )

    for index in range(2):
        weights_at_home[index].start()
        for step in range(1, 4):
            down(index, step).start()

    for half in range(2):
        def start(group):
            @pl.when(across | (group != plane))
            def _():
                spread(group, half, head).start()

        each(start)

    def start_q(group):
        @pl.when(across | (group != plane))
        def _():
            spread_q(group, head).start()

    each(start_q)

    @pl.when(diagonal)
    def _():
        at_home(0).start()
        at_home(1).start()
        q_at_home.start()
        for copy in routes_at_home:
            copy.start()

    @pl.when(across)
    def _():
        for copy in routes_sent:
            copy.start()

    for rise in range(1, 4):
        for index in range(2):
            down(index, rise).wait_recv()
            for step in range(1, 4):
                over(index, rise, step).start()

    def moved(source, target, half, send, recv, to):
        return pltpu.make_async_remote_copy(
            src_ref=kv_out.at[source, :, rows(half)], dst_ref=kv_out.at[target, :, rows(half)],
            send_sem=send, recv_sem=recv, device_id=to, device_id_type=MESH,
        )

    def hop(way, step, half):
        if way == 0:
            source, to = 4 - 2 * step + core, right
            target = 2 - 2 * step + core
        else:
            source, to = 4 + 2 * step + core, left
            target = 6 + 2 * step + core
        return moved(source, target, half, ring_send.at[way, step, half], ring_recv.at[way, step, half], to)

    def shared(place, half):
        return moved(2 * place + core, 2 * place + core, half, pair_send.at[place, half], pair_recv.at[place, half], pair)

    def taken(place, half):
        return moved(2 * place + 1 - core, 2 * place + 1 - core, half, pair_send.at[place, half], pair_recv.at[place, half], pair)

    for half in range(2):
        def wait(shard):
            @pl.when(across | (shard != head))
            def _():
                landed(half, shard).wait_recv()

        each(wait)

        @pl.when(diagonal)
        def _():
            at_home(half).wait()

        hop(0, 0, half).start()
        hop(1, 0, half).start()
        shared(2, half).start()
    for half in range(2):
        hop(0, 0, half).wait_recv()
        hop(0, 1, half).start()
        hop(1, 0, half).wait_recv()
        hop(1, 1, half).start()
        shared(1, half).start()
        shared(3, half).start()
    for half in range(2):
        hop(0, 1, half).wait_recv()
        shared(0, half).start()
        hop(1, 1, half).wait_recv()
        shared(4, half).start()

    def wait_q(shard):
        @pl.when(across | (shard != head))
        def _():
            spread_q(0, shard).wait_recv()

    each(wait_q)

    def sent(group):
        @pl.when(across | (group != plane))
        def _():
            spread(group, 0, head).wait_send()
            spread(group, 1, head).wait_send()
            spread_q(group, head).wait_send()

    each(sent)

    @pl.when(diagonal)
    def _():
        q_at_home.wait()
        for copy in routes_at_home:
            copy.wait()

    @pl.when(across)
    def _():
        for copy in routes_sent:
            copy.wait()

    for index in range(2):
        weights_at_home[index].wait()
        for rise in range(1, 4):
            for step in range(1, 4):
                over(index, rise, step).wait_recv()
        share(index).start()

    for half in range(2):
        for way in range(2):
            for step in range(2):
                hop(way, step, half).wait_send()
        for place in range(5):
            shared(place, half).wait_send()
            taken(place, half).wait_recv()
    for index in range(2):
        for rise in range(1, 4):
            down(index, rise).wait_send()
            for step in range(1, 4):
                over(index, rise, step).wait_send()
        share(index).wait()


def exchange(kv, q, routes, local, w1, w2):
    anywhere = pl.BlockSpec(memory_space=pltpu.HBM)
    return pl.pallas_call(
        exchange_kernel,
        out_shape=(
            jax.ShapeDtypeStruct((10, GROUPS, TOK, LANES), BF16),
            jax.ShapeDtypeStruct((GROUPS, LANES, LANES), BF16),
            jax.ShapeDtypeStruct((1, LANES), jnp.int32),
            jax.ShapeDtypeStruct((1, LANES), jnp.int32),
            jax.ShapeDtypeStruct((2, 4, D, 256), BF16),
            jax.ShapeDtypeStruct((2, 4, 256, D), BF16),
        ),
        in_specs=[anywhere] * 6,
        out_specs=(anywhere,) * 6,
        scratch_shapes=[
            pltpu.SemaphoreType.DMA((3, 8)),
            pltpu.SemaphoreType.DMA((3, 8)),
            pltpu.SemaphoreType.DMA((2, 2, 2)),
            pltpu.SemaphoreType.DMA((2, 2, 2)),
            pltpu.SemaphoreType.DMA((5, 2)),
            pltpu.SemaphoreType.DMA((5, 2)),
            pltpu.SemaphoreType.DMA((2, 2)),
            pltpu.SemaphoreType.DMA((7,)),
            pltpu.SemaphoreType.DMA((2, 3)),
            pltpu.SemaphoreType.DMA((2, 3)),
            pltpu.SemaphoreType.DMA((2, 3, 3)),
            pltpu.SemaphoreType.DMA((2, 3, 3)),
            pltpu.SemaphoreType.DMA((2,)),
            pltpu.SemaphoreType.DMA((2,)),
        ],
        compiler_params=pltpu.CompilerParams(collective_id=0, has_side_effects=True),
        name="exchange",
    )(kv, q, routes, local, w1, w2)


def per_device(
    points, gain_attn, w_qkv, w_out, gain_mlp, w_fc1, w_fc2, contact_route, contact_patch, counts
):
    kv, q = project(points, gain_attn, w_qkv)
    slots, q, routes, local, w1, w2 = exchange(kv, q, contact_route.reshape(1, -1), contact_patch, w_fc1, w_fc2)
    packed = attend(routes, local, counts, q, slots.reshape(20, PATCH, LANES))
    w1 = w1.reshape(GROUPS, D, 256)
    return finish(points, packed, w_out, gain_mlp, w1, w2.reshape(GROUPS, 256, D))


def solution(mesh):
    return jax.shard_map(
        per_device,
        mesh=mesh,
        in_specs=(
            P(("seq", "head"), None), P(), P(), P(), P(), P(None, "head"), P("head", None),
            P("head", None, None), P("head", None), P(),
        ),
        out_specs=P(("seq", "head"), None),
        check_vma=False,
    )
```

time: 187 us -> 145 us (0.78)
  the two profiles are of different devices: /device:TPU:95 before, /device:TPU:127 now
where the time goes in v3:
time: 145 us
  Pallas kernels  140 us (97%)
  local copies, waits for them, and re-layouts  5.36 us (4%)
    pallas_call x1, Pallas kernels, exchange(): pl.pallas_call(exchange_kernel, out_shape=(jax.ShapeDtypeStruct((10, GROU...  65.2 us
    pallas_call x1, Pallas kernels, attend(): pl.pallas_call(attend_kernel, out_shape=jax.ShapeDtypeStruct((GROUPS, 64,...  44.4 us
    pallas_call x1, Pallas kernels, finish(): pl.pallas_call(finish_kernel, out_shape=jax.ShapeDtypeStruct((TOK, D), BF...  25.8 us
    unnamed x21, local copies, waits for them, and re-layouts  5.36 us
    pallas_call x1, Pallas kernels, project(): pl.pallas_call(project_kernel, out_shape=(jax.ShapeDtypeStruct((GROUPS, T...  4.21 us

profile of v3, /device:TPU:127, one launch (start us, length us, event | category | flops | bytes accessed | tf_op | source)
XLA Modules:
  0.0 145.1 jit_solution(5090504557022191097)
XLA Ops:
  0.0 0.0 copy-start.7
  0.0 4.2 %project.1 = (bf16[8,256,128]{2,1,0:T(8,128)(2,1)}, bf16[8,128,128]{2,1,0:T(8,128)(2,1)}) custom-call(bf16[256,512]{1,0:T(8,128)(2,1)} %points_ref.3, f32[1,512]{1,0:T(1,128)} %bitcast.10, bf16[512,1536]{1,0:T(8,128)(2,1)} %w_ref.1, f32[1,1536]{1,0:T(1,128)} %constant.4.clone.scale_ref, bf16[384,768]{1,0:T(8,128)(2,1)} %constant.5.clone.place_ref), custom_call_target="tpu_custom_call" | custom-call | tf_op jit(solution)/shard_map/project/pallas_call | solution.py:74
  4.2 65.2 %exchange.1 = (bf16[10,8,256,128]{3,2,1,0:T(8,128)(2,1)}, bf16[8,128,128]{2,1,0:T(8,128)(2,1)}, s32[1,128]{1,0:T(1,128)}, s32[1,128]{1,0:T(1,128)}, bf16[2,4,512...) custom-call(bf16[8,256,128]{2,1,0:T(8,128)(2,1)} %get-tuple-element.13.kv_ref, ...), custom_call_target="tpu_custom_call" | custom-call | tf_op jit(solution)/shard_map/exchange/pallas_call | solution.py:668
  69.4 0.0 copy-done.7
  69.4 0.0 copy-start
  69.4 2.5 %copy-done = bf16[10,8,256,128]{3,2,1,0:T(8,128)(2,1)S(1)} copy-done((bf16[10,8,256,128]{3,2,1,0:T(8,128)(2,1)S(1)}, bf16[10,8,256,128]{3,2,1,0:T(8,128)(2,1)}, u32[]{:S(2)}) %copy-start) | copy-done | bytes 5242904
  71.9 0.0 copy-start.5
  71.9 0.9 copy-done.5
  72.9 0.0 copy-start.8
  72.9 0.6 copy-done.8
  73.5 0.0 copy-start.9
  73.5 0.6 copy-done.9
  74.1 0.0 copy-start.1
  74.1 0.0 copy-start.2
  74.1 0.0 copy-start.3
  74.1 0.0 copy-start.4
  74.1 0.0 copy-start.6
  74.1 44.4 %attend.1.packed_ref = bf16[8,64,256]{2,1,0:T(8,128)(2,1)S(1)} custom-call(s32[1,128]{1,0:T(1,128)S(1)} %copy-done.8, s32[1,128]{1,0:T(1,128)S(1)} %copy-done.9, s32[256]{0:T(256)S(1)} %copy-done.7, bf16[8,128,128]{2,1,0:T(8,128)(2,1)S(1)} %copy-done.5, bf16[20,1024,128]{2,1,0:T(8,128)(2,1)S(1)} %bitcast.6), custom_call_target="tpu_custom_call" | custom-call | tf_op jit(solution)/shard_map/attend/pallas_call | solution.py:249
  118.5 0.0 copy-done.1
  118.5 0.0 copy-done.2
  118.5 0.0 copy-done.3
  118.5 0.0 copy-done.4
  118.5 0.0 copy-done.6
  118.5 25.8 %finish.1 = bf16[256,512]{1,0:T(8,128)(2,1)S(1)} custom-call(bf16[256,512]{1,0:T(8,128)(2,1)S(1)} %copy-done.3, bf16[8,64,256]{2,1,0:T(8,128)(2,1)S(1)} %attend.1.packed_ref, bf16[512,512]{1,0:T(8,128)(2,1)S(1)} %copy-done.4, f32[1,512]{1,0:T(1,128)S(1)} %bitcast.9, bf16[8,512,256]{2,1,0:T(8,128)(2,1)S(1)} %bitcast.7, bf16[8,256,512]{2,1,0:T(8,128)(2,1)S(1)} %bitcast.8), custom_call_target="tpu_custom_call" | custom-call | tf_op jit(solution)/shard_map/finish/pallas_call | solution.py:381
  144.4 0.7 copy.14
Async XLA Ops:
  0.0 69.4 %copy-start.7 = (s32[256]{0:T(256)S(1)}, s32[256]{0:T(256)}, u32[]{:S(2)}) copy-start(s32[256]{0:T(256)} %counts_hbm.1) | copy-start | bytes 3076
  69.4 2.5 %copy-start = (bf16[10,8,256,128]{3,2,1,0:T(8,128)(2,1)S(1)}, bf16[10,8,256,128]{3,2,1,0:T(8,128)(2,1)}, u32[]{:S(2)}) copy-start(bf16[10,8,256,128]{3,2,1,0:T(8,128)(2,1)} %get-tuple-element.18) | copy-start | bytes 15728644
  71.9 0.9 copy-start.5
  72.9 0.6 copy-start.8
  73.5 0.6 copy-start.9
  74.1 44.4 %copy-start.1 = (bf16[2,4,512,256]{3,2,1,0:T(8,128)(2,1)S(1)}, bf16[2,4,512,256]{3,2,1,0:T(8,128)(2,1)}, u32[]{:S(2)}) copy-start(bf16[2,4,512,256]{3,2,1,0:T(8,128)(2,1)} %get-tuple-element.19) | copy-start | bytes 6291460
  74.1 44.4 %copy-start.2 = (bf16[2,4,256,512]{3,2,1,0:T(8,128)(2,1)S(1)}, bf16[2,4,256,512]{3,2,1,0:T(8,128)(2,1)}, u32[]{:S(2)}) copy-start(bf16[2,4,256,512]{3,2,1,0:T(8,128)(2,1)} %get-tuple-element.20) | copy-start | bytes 6291460
  74.1 44.5 %copy-start.3 = (bf16[256,512]{1,0:T(8,128)(2,1)S(1)}, bf16[256,512]{1,0:T(8,128)(2,1)}, u32[]{:S(2)}) copy-start(bf16[256,512]{1,0:T(8,128)(2,1)} %points_ref.3) | copy-start | bytes 786436
  74.1 44.5 %copy-start.4 = (bf16[512,512]{1,0:T(8,128)(2,1)S(1)}, bf16[512,512]{1,0:T(8,128)(2,1)}, u32[]{:S(2)}) copy-start(bf16[512,512]{1,0:T(8,128)(2,1)} %w_out_ref.1) | copy-start | bytes 1572868
  74.1 44.5 %copy-start.6 = (f32[512]{0:T(512)S(1)}, f32[512]{0:T(512)}, u32[]{:S(2)}) copy-start(f32[512]{0:T(512)} %param.16) | copy-start | bytes 6148

commit v4 on v3

--- a/solution.py
+++ b/solution.py
@@ -51,34 +51,6 @@
     centred = values - jnp.mean(values, axis=-1, keepdims=True)
     spread = jnp.mean(centred * centred, axis=-1, keepdims=True)
     return centred * lax.rsqrt(spread + 1e-05) * gain
-
-
-def project_kernel(points_ref, gain_ref, w_ref, scale_ref, place_ref, kv_ref, q_ref):
-    normed = normalise(points_ref[...].astype(F32), gain_ref[...]).astype(BF16)
-    for pair in range(GROUPS // 2):
-        columns = slice(384 * pair, 384 * pair + 384)
-        projected = jnp.dot(normed, w_ref[:, columns], preferred_element_type=F32)
-        projected = (projected * scale_ref[:, columns]).astype(BF16)
-        kv = jnp.dot(projected, place_ref[:, :256], preferred_element_type=F32).astype(BF16)
-        q = jnp.dot(projected[:128], place_ref[:, 256:512], preferred_element_type=F32)
-        q = q + jnp.dot(projected[128:], place_ref[:, 512:], preferred_element_type=F32)
-        q = q.astype(BF16)
-        for side in range(2):
-            kv_ref[2 * pair + side] = kv[:, 128 * side:128 * side + 128]
-            q_ref[2 * pair + side] = q[:, 128 * side:128 * side + 128]
-
-
-def project(points, gain, w_qkv):
-    scale = np.ones((1, 1536), np.float32)
-    scale[0, np.arange(1536) % 48 < 16] = HEAD_DIM ** -0.5 * math.log2(math.e)
-    return pl.pallas_call(
-        project_kernel,
-        out_shape=(
-            jax.ShapeDtypeStruct((GROUPS, TOK, LANES), BF16),
-            jax.ShapeDtypeStruct((GROUPS, LANES, LANES), BF16),
-        ),
-        name="project",
-    )(points, gain.reshape(1, D), w_qkv, jnp.asarray(scale), jnp.asarray(placing(), BF16))
 
 
 def swap_ids():
@@ -268,7 +240,8 @@
             pltpu.SemaphoreType.DMA((4,)),
             pltpu.SemaphoreType.DMA((8,)),
         ],
-        compiler_params=pltpu.CompilerParams(vmem_limit_bytes=40 << 20),
+        compiler_params=pltpu.CompilerParams(vmem_limit_bytes=60 << 20),
+        cost_estimate=pl.CostEstimate(flops=30_000_000_000, bytes_accessed=8_000_000, transcendentals=25_000_000),
         name="attend",
     )(routes, local, counts, q, kv)
 
@@ -282,8 +255,8 @@
 
 
 def finish_kernel(
-    points_ref, packed_ref, w_out_ref, gain_ref, w1_ref, w2_ref, out_ref,
-    points, w_out, gain, w1, w2, back, send, recv, local_sem, load_sem, weight_sem,
+    points_ref, packed_ref, w_out_ref, gain_ref, w0_ref, w1_ref, w2_ref, w3_ref, out_ref,
+    points, w_out, gain, slabs, back, send, recv, local_sem, load_sem, weight_sem, pair_send, pair_recv,
 ):
     column, plane, head = swap_ids()
     diagonal = plane == head
@@ -296,6 +269,8 @@
             pl.semaphore_signal(barrier, inc=1, device_id=(column * 8 + group, plane), device_id_type=MESH)
 
     each(greet)
+    pair = (column * 8 + plane, head + 1 - 2 * lax.rem(head, 2))
+    pl.semaphore_signal(barrier, inc=1, device_id=pair, device_id_type=MESH)
     loads = [
         pltpu.make_async_copy(points_ref, points, load_sem.at[0]),
         pltpu.make_async_copy(w_out_ref, w_out, load_sem.at[1]),
@@ -304,23 +279,25 @@
     for load in loads:
         load.start()
 
-    def weights(part):
-        return (
-            pltpu.make_async_copy(w1_ref.at[part], w1.at[part], weight_sem.at[0, part]),
-            pltpu.make_async_copy(w2_ref.at[part], w2.at[part], weight_sem.at[1, part]),
-        )
-
-    for part in range(GROUPS):
-        for copy in weights(part):
-            copy.start()
+    shards = (w0_ref, w1_ref, w2_ref, w3_ref)
+    own = [pltpu.make_async_copy(shard, slabs.at[part], weight_sem.at[part]) for part, shard in enumerate(shards)]
+    lent = [
+        pltpu.make_async_remote_copy(
+            src_ref=shard, dst_ref=slabs.at[4 + part], send_sem=pair_send.at[part], recv_sem=pair_recv.at[part],
+            device_id=pair, device_id_type=MESH,
+        )
+        for part, shard in enumerate(shards)
+    ]
+    for load in own:
+        load.start()
 
     @pl.when(diagonal)
     def _():
-        pl.semaphore_wait(barrier, 7)
+        pl.semaphore_wait(barrier, 8)
 
     @pl.when(across)
     def _():
-        pl.semaphore_wait(barrier, 8)
+        pl.semaphore_wait(barrier, 9)
 
     def copy(shard, group):
         return pltpu.make_async_remote_copy(
@@ -337,6 +314,8 @@
             copy(shard, plane).start()
 
     each(start)
+    for load in lent:
+        load.start()
 
     @pl.when(diagonal)
     def _():
@@ -359,14 +338,18 @@
     )
     updated = updated.astype(BF16).astype(F32)
     normed = normalise(updated, gain[...]).astype(BF16)
-    total = updated
+    low, high = updated[:, :256], updated[:, 256:]
     for part in range(GROUPS):
-        for load in weights(part):
-            load.wait()
-        hidden = jnp.dot(normed, w1[part], preferred_element_type=F32)
-        hidden = hidden * (0.5 * (1.0 + lax.erf(hidden * (2.0 ** -0.5))))
-        total = total + jnp.dot(hidden.astype(BF16), w2[part], preferred_element_type=F32)
-    out_ref[...] = total.astype(BF16)
+        if part < 4:
+            own[part].wait()
+        else:
+            lent[part - 4].wait_recv()
+        hidden = jnp.dot(normed, slabs[part, :D], preferred_element_type=F32)
+        hidden = (hidden * (0.5 * (1.0 + lax.erf(hidden * (2.0 ** -0.5))))).astype(BF16)
+        low = low + jnp.dot(hidden, slabs[part, D:D + 256], preferred_element_type=F32)
+        high = high + jnp.dot(hidden, slabs[part, D + 256:], preferred_element_type=F32)
+    out_ref[:, :256] = low.astype(BF16)
+    out_ref[:, 256:] = high.astype(BF16)
 
     def sent(index):
         @pl.when(across | (index != head))
@@ -374,39 +357,42 @@
             copy(index, plane).wait_send()
 
     each(sent)
-
-
-def finish(points, packed, w_out, gain, w1, w2):
+    for load in lent:
+        load.wait_send()
+
+
+def finish(points, packed, w_out, gain, weights):
     hbm = pl.BlockSpec(memory_space=pltpu.HBM)
     return pl.pallas_call(
         finish_kernel,
         out_shape=jax.ShapeDtypeStruct((TOK, D), BF16),
-        in_specs=[hbm] * 6,
+        in_specs=[hbm] * 8,
         out_specs=pl.BlockSpec(memory_space=pltpu.VMEM),
         scratch_shapes=[
             pltpu.VMEM((TOK, D), BF16),
             pltpu.VMEM((D, D), BF16),
             pltpu.VMEM((1, D), F32),
-            pltpu.VMEM((GROUPS, D, 256), BF16),
-            pltpu.VMEM((GROUPS, 256, D), BF16),
+            pltpu.VMEM((GROUPS, 2 * D, 256), BF16),
             pltpu.VMEM((GROUPS, 64, TOK), BF16),
             pltpu.SemaphoreType.DMA((8,)),
             pltpu.SemaphoreType.DMA((8,)),
             pltpu.SemaphoreType.DMA((1,)),
             pltpu.SemaphoreType.DMA((3,)),
-            pltpu.SemaphoreType.DMA((2, 8)),
+            pltpu.SemaphoreType.DMA((4,)),
+            pltpu.SemaphoreType.DMA((4,)),
+            pltpu.SemaphoreType.DMA((4,)),
         ],
         compiler_params=pltpu.CompilerParams(
             collective_id=1, has_side_effects=True, vmem_limit_bytes=40 << 20
         ),
         name="finish",
-    )(points, packed, w_out, gain.reshape(1, D), w1, w2)
+    )(points, packed, w_out, gain.reshape(1, D), *weights)
 
 
 def exchange_kernel(
-    kv_ref, q_ref, route_ref, local_ref, w1_ref, w2_ref, kv_out, q_out, route_out, local_out, w1_out, w2_out,
+    points_ref, gain_ref, w_ref, scale_ref, place_ref, route_ref, local_ref, kv_out, q_out, route_out, local_out,
+    kv_ref, q_ref,
     all_send, all_recv, ring_send, ring_recv, pair_send, pair_recv, route_sem, local_sem,
-    down_send, down_recv, over_send, over_recv, share_send, share_recv,
 ):
     column, plane, head = swap_ids()
     core = lax.rem(head, 2)
@@ -428,19 +414,17 @@
         return 0
 
     lax.fori_loop(0, 8, greet, 0)
-    level = head // 2
-    downs = [(column * 8 + plane, lax.rem(level + step, 4) * 2 + core) for step in range(1, 4)]
-    overs = [(lax.rem(column + step, 4) * 8 + plane, head) for step in range(1, 4)]
-    for other in (right, left, pair, *downs, *overs):
+    for other in (right, left, pair):
         pl.semaphore_signal(barrier, inc=1, device_id=other, device_id_type=MESH)
 
-    @pl.when(diagonal)
-    def _():
-        pl.semaphore_wait(barrier, 16)
-
-    @pl.when(across)
-    def _():
-        pl.semaphore_wait(barrier, 17)
+    def enter():
+        @pl.when(diagonal)
+        def _():
+            pl.semaphore_wait(barrier, 10)
+
+        @pl.when(across)
+        def _():
+            pl.semaphore_wait(barrier, 11)
 
     def rows(half):
         return pl.ds(half * LANES, LANES)
@@ -493,57 +477,32 @@
         for index, (source, target) in enumerate(((route_ref, route_out), (local_ref, local_out)))
     ]
 
-    slabs = (
-        (w1_ref, w1_out, pl.ds(column * LANES, LANES)),
-        (w2_ref, w2_out, pl.ds(column * 64, 64)),
-    )
-    weights_at_home = [
-        pltpu.make_async_copy(source, target.at[core, level], local_sem.at[5 + index])
-        for index, (source, target, _) in enumerate(slabs)
-    ]
-
-    def down(index, step):
-        source, target, quarter = slabs[index]
-        return pltpu.make_async_remote_copy(
-            src_ref=source.at[quarter], dst_ref=target.at[core, level, quarter],
-            send_sem=down_send.at[index, step - 1], recv_sem=down_recv.at[index, step - 1],
-            device_id=downs[step - 1], device_id_type=MESH,
-        )
-
-    def over(index, rise, step):
-        _, target, quarter = slabs[index]
-        spot_of = target.at[core, lax.rem(level + 4 - rise, 4), quarter]
-        return pltpu.make_async_remote_copy(
-            src_ref=spot_of, dst_ref=spot_of,
-            send_sem=over_send.at[index, rise - 1, step - 1], recv_sem=over_recv.at[index, rise - 1, step - 1],
-            device_id=overs[step - 1], device_id_type=MESH,
-        )
-
-    def share(index):
-        _, target, _ = slabs[index]
-        return pltpu.make_async_remote_copy(
-            src_ref=target.at[core], dst_ref=target.at[core],
-            send_sem=share_send.at[index], recv_sem=share_recv.at[index], device_id=pair, device_id_type=MESH,
-        )
-
-    for index in range(2):
-        weights_at_home[index].start()
-        for step in range(1, 4):
-            down(index, step).start()
-
-    for half in range(2):
-        def start(group):
-            @pl.when(across | (group != plane))
-            def _():
-                spread(group, half, head).start()
-
-        each(start)
+    def start(group):
+        @pl.when(across | (group != plane))
+        def _():
+            spread(group, 0, head).start()
+            spread(group, 1, head).start()
 
     def start_q(group):
         @pl.when(across | (group != plane))
         def _():
             spread_q(group, head).start()
 
+    normed = normalise(points_ref[...].astype(F32), gain_ref[...]).astype(BF16)
+    for couple in range(GROUPS // 2):
+        columns = slice(384 * couple, 384 * couple + 384)
+        projected = jnp.dot(normed, w_ref[:, columns], preferred_element_type=F32)
+        projected = (projected * scale_ref[:, columns]).astype(BF16)
+        kv = jnp.dot(projected, place_ref[:, :256], preferred_element_type=F32).astype(BF16)
+        q = jnp.dot(projected[:128], place_ref[:, 256:512], preferred_element_type=F32)
+        q = (q + jnp.dot(projected[128:], place_ref[:, 512:], preferred_element_type=F32)).astype(BF16)
+        for side in range(2):
+            kv_ref[2 * couple + side] = kv[:, 128 * side:128 * side + 128]
+            q_ref[2 * couple + side] = q[:, 128 * side:128 * side + 128]
+        if couple == 0:
+            enter()
+        start(2 * couple)
+        start(2 * couple + 1)
     each(start_q)
 
     @pl.when(diagonal)
@@ -559,11 +518,6 @@
         for copy in routes_sent:
             copy.start()
 
-    for rise in range(1, 4):
-        for index in range(2):
-            down(index, rise).wait_recv()
-            for step in range(1, 4):
-                over(index, rise, step).start()
 
     def moved(source, target, half, send, recv, to):
         return pltpu.make_async_remote_copy(
@@ -641,12 +595,6 @@
         for copy in routes_sent:
             copy.wait()
 
-    for index in range(2):
-        weights_at_home[index].wait()
-        for rise in range(1, 4):
-            for step in range(1, 4):
-                over(index, rise, step).wait_recv()
-        share(index).start()
 
     for half in range(2):
         for way in range(2):
@@ -655,15 +603,12 @@
         for place in range(5):
             shared(place, half).wait_send()
             taken(place, half).wait_recv()
-    for index in range(2):
-        for rise in range(1, 4):
-            down(index, rise).wait_send()
-            for step in range(1, 4):
-                over(index, rise, step).wait_send()
-        share(index).wait()
-
-
-def exchange(kv, q, routes, local, w1, w2):
+
+
+def exchange(points, gain, w_qkv, routes, local):
+    scale = np.ones((1, 1536), np.float32)
+    scale[0, np.arange(1536) % 48 < 16] = HEAD_DIM ** -0.5 * math.log2(math.e)
+    vmem = pl.BlockSpec(memory_space=pltpu.VMEM)
     anywhere = pl.BlockSpec(memory_space=pltpu.HBM)
     return pl.pallas_call(
         exchange_kernel,
@@ -672,12 +617,12 @@
             jax.ShapeDtypeStruct((GROUPS, LANES, LANES), BF16),
             jax.ShapeDtypeStruct((1, LANES), jnp.int32),
             jax.ShapeDtypeStruct((1, LANES), jnp.int32),
-            jax.ShapeDtypeStruct((2, 4, D, 256), BF16),
-            jax.ShapeDtypeStruct((2, 4, 256, D), BF16),
         ),
-        in_specs=[anywhere] * 6,
-        out_specs=(anywhere,) * 6,
+        in_specs=[vmem] * 5 + [anywhere] * 2,
+        out_specs=(anywhere,) * 4,
         scratch_shapes=[
+            pltpu.VMEM((GROUPS, TOK, LANES), BF16),
+            pltpu.VMEM((GROUPS, LANES, LANES), BF16),
             pltpu.SemaphoreType.DMA((3, 8)),
             pltpu.SemaphoreType.DMA((3, 8)),
             pltpu.SemaphoreType.DMA((2, 2, 2)),
@@ -686,26 +631,26 @@
             pltpu.SemaphoreType.DMA((5, 2)),
             pltpu.SemaphoreType.DMA((2, 2)),
             pltpu.SemaphoreType.DMA((7,)),
-            pltpu.SemaphoreType.DMA((2, 3)),
-            pltpu.SemaphoreType.DMA((2, 3)),
-            pltpu.SemaphoreType.DMA((2, 3, 3)),
-            pltpu.SemaphoreType.DMA((2, 3, 3)),
-            pltpu.SemaphoreType.DMA((2,)),
-            pltpu.SemaphoreType.DMA((2,)),
         ],
-        compiler_params=pltpu.CompilerParams(collective_id=0, has_side_effects=True),
+        compiler_params=pltpu.CompilerParams(collective_id=0, has_side_effects=True, vmem_limit_bytes=60 << 20),
         name="exchange",
-    )(kv, q, routes, local, w1, w2)
+    )(
+        points, gain.reshape(1, D), w_qkv, jnp.asarray(scale), jnp.asarray(placing(), BF16), routes, local,
+    )
 
 
 def per_device(
     points, gain_attn, w_qkv, w_out, gain_mlp, w_fc1, w_fc2, contact_route, contact_patch, counts
 ):
-    kv, q = project(points, gain_attn, w_qkv)
-    slots, q, routes, local, w1, w2 = exchange(kv, q, contact_route.reshape(1, -1), contact_patch, w_fc1, w_fc2)
+    slots, q, routes, local = exchange(points, gain_attn, w_qkv, contact_route.reshape(1, -1), contact_patch)
+    own = jnp.concatenate([w_fc1, w_fc2[:, :256], w_fc2[:, 256:]], axis=0)
+    own, routes = lax.optimization_barrier((own, routes))
+    weights = [own]
+    for step in range(1, 4):
+        pairs = [(head, (head + 2 * step) % GROUPS) for head in range(GROUPS)]
+        weights.append(lax.ppermute(own, "head", pairs))
     packed = attend(routes, local, counts, q, slots.reshape(20, PATCH, LANES))
-    w1 = w1.reshape(GROUPS, D, 256)
-    return finish(points, packed, w_out, gain_mlp, w1, w2.reshape(GROUPS, 256, D))
+    return finish(points, packed, w_out, gain_mlp, weights)
 
 
 def solution(mesh):

time: 145 us -> 132 us (0.910)
  the two profiles are of different devices: /device:TPU:127 before, /device:TPU:25 now
where the time goes in v4:
time: 132 us
  Pallas kernels  125 us (95%)
  starting transfers between devices  3.67 us (3%)
  local copies, waits for them, and re-layouts  2.65 us (2%)
    pallas_call x1, Pallas kernels, exchange(): pl.pallas_call(exchange_kernel, out_shape=(jax.ShapeDtypeStruct((10, GROU...  47.8 us
    pallas_call x1, Pallas kernels, attend(): pl.pallas_call(attend_kernel, out_shape=jax.ShapeDtypeStruct((GROUPS, 64,...  45.9 us
    pallas_call x1, Pallas kernels, finish(): pl.pallas_call(finish_kernel, out_shape=jax.ShapeDtypeStruct((TOK, D), BF...  31 us
    ppermute x3, starting transfers between devices, per_device(): weights.append(lax.ppermute(own, 'head', pairs))  3.67 us
  transfers between devices with their start and end apart: 3, of which 0 were waited for; matrix products, arithmetic and copies ran while one was open for 0% of the time, Pallas kernels for 35%

profile of v4, /device:TPU:25, one launch (start us, length us, event | category | flops | bytes accessed | tf_op | source)
XLA Modules:
  0.0 132.0 jit_solution(11527044587797411062)
XLA Ops:
  0.0 1.0 fusion
  1.0 1.0 pad_maximum_fusion.w0_ref
  2.0 47.8 %exchange.1 = (bf16[10,8,256,128]{3,2,1,0:T(8,128)(2,1)}, bf16[8,128,128]{2,1,0:T(8,128)(2,1)}, s32[1,128]{1,0:T(1,128)}, s32[1,128]{1,0:T(1,128)}) custom-call(bf16[256,512]{1,0:T(8,128)(2,1)} %points_ref.3, f32[1,512]{1,0:T(1,128)} %bitcast.5, bf16[512,1536]{1,0:T(8,128)(2,1)} %w_ref.1, f32[1,1536]{1,0:T(1,128)} %constant.4.clone.scale_ref, ...), custom_call_target="tpu_custom_call" | custom-call | tf_op jit(solution)/shard_map/exchange/pallas_call | solution.py:613
  49.8 1.2 collective-permute-start.2
  50.9 2.3 %collective-permute-start.1 = (bf16[1024,256]{1,0:T(8,128)(2,1)S(1)}, bf16[1024,256]{1,0:T(8,128)(2,1)S(1)}, u32[]{:S(2)}, u32[]{:S(2)}) collective-permute-start(bf16[1024,256]{1,0:T(8,128)(2,1)S(1)} %pad_maximum_fusion.w0_ref), channel_id=1, source_target_pairs={{0,4},{1,5},{2,6},{3,7},{4,0},{5,1},{6,2},{7,3},{8,12},{9,13},{10,... | collective-permute-start | bytes 1572872 | tf_op jit(solution)/shard_map/ppermute | solution.py:651
  53.3 0.2 collective-permute-start
  53.4 0.0 copy-start
  53.4 0.0 copy-start.1
  53.4 0.0 copy-start.3
  53.4 45.9 %attend.1.packed_ref = bf16[8,64,256]{2,1,0:T(8,128)(2,1)} custom-call(s32[1,128]{1,0:T(1,128)} %get-tuple-element.12.routes_hbm, s32[1,128]{1,0:T(1,128)} %get-tuple-element.13.local_hbm, s32[256]{0:T(256)} %counts_hbm.1, bf16[8,128,128]{2,1,0:T(8,128)(2,1)} %get-tuple-element.14.q_hbm, bf16[20,1024,128]{2,1,0:T(8,128)(2,1)} %bitcast.7), custom_call_target="tpu_custom_call" | custom-call | flops 30000001024 | bytes 8000000 | tf_op jit(solution)/shard_map/attend/pallas_call | solution.py:221
  99.3 0.0 collective-permute-done.2.w3_ref
  99.3 0.0 collective-permute-done.1.w2_ref
  99.4 0.0 collective-permute-done.w1_ref
  99.4 0.0 copy-done
  99.4 0.0 copy-done.1
  99.4 0.0 copy-done.3
  99.4 0.0 copy-start.2
  99.4 0.9 copy-done.2
  100.4 31.0 %finish.1 = bf16[256,512]{1,0:T(8,128)(2,1)S(1)} custom-call(bf16[256,512]{1,0:T(8,128)(2,1)S(1)} %copy-done, bf16[8,64,256]{2,1,0:T(8,128)(2,1)S(1)} %copy-done.2, bf16[512,512]{1,0:T(8,128)(2,1)S(1)} %copy-done.1, f32[1,512]{1,0:T(1,128)S(1)} %bitcast.4, bf16[1024,256]{1,0:T(8,128)(2,1)S(1)} %pad_maximum_fusion.w0_ref, ...), custom_call_target="tpu_custom_call" | custom-call | tf_op jit(solution)/shard_map/finish/pallas_call | solution.py:366
  131.3 0.7 copy.14
Async XLA Ops:
  49.8 49.6 %collective-permute-start.2 = (bf16[1024,256]{1,0:T(8,128)(2,1)S(1)}, bf16[1024,256]{1,0:T(8,128)(2,1)S(1)}, u32[]{:S(2)}, u32[]{:S(2)}) collective-permute-start(bf16[1024,256]{1,0:T(8,128)(2,1)S(1)} %pad_maximum_fusion.w0_ref), channel_id=1, source_target_pairs={{0,6},{1,7},{2,0},{3,1},{4,2},{5,3},{6,4},{7,5},{8,14},{9,15},{10,... | collective-permute-start | bytes 1572872 | tf_op jit(solution)/shard_map/ppermute | solution.py:651
  50.9 48.4 %collective-permute-start.1 = (bf16[1024,256]{1,0:T(8,128)(2,1)S(1)}, bf16[1024,256]{1,0:T(8,128)(2,1)S(1)}, u32[]{:S(2)}, u32[]{:S(2)}) collective-permute-start(bf16[1024,256]{1,0:T(8,128)(2,1)S(1)} %pad_maximum_fusion.w0_ref), channel_id=1, source_target_pairs={{0,4},{1,5},{2,6},{3,7},{4,0},{5,1},{6,2},{7,3},{8,12},{9,13},{10,... | collective-permute-start | bytes 1572872 | tf_op jit(solution)/shard_map/ppermute | solution.py:651
  53.3 46.1 %collective-permute-start = (bf16[1024,256]{1,0:T(8,128)(2,1)S(1)}, bf16[1024,256]{1,0:T(8,128)(2,1)S(1)}, u32[]{:S(2)}, u32[]{:S(2)}) collective-permute-start(bf16[1024,256]{1,0:T(8,128)(2,1)S(1)} %pad_maximum_fusion.w0_ref), channel_id=1, source_target_pairs={{0,2},{1,3},{2,4},{3,5},{4,6},{5,7},{6,0},{7,1},{8,10},{9,11},{10,... | collective-permute-start | bytes 1572872 | tf_op jit(solution)/shard_map/ppermute | solution.py:651
  53.4 45.9 %copy-start = (bf16[256,512]{1,0:T(8,128)(2,1)S(1)}, bf16[256,512]{1,0:T(8,128)(2,1)}, u32[]{:S(2)}) copy-start(bf16[256,512]{1,0:T(8,128)(2,1)} %points_ref.3) | copy-start | bytes 786436
  53.4 46.0 %copy-start.1 = (bf16[512,512]{1,0:T(8,128)(2,1)S(1)}, bf16[512,512]{1,0:T(8,128)(2,1)}, u32[]{:S(2)}) copy-start(bf16[512,512]{1,0:T(8,128)(2,1)} %w_out_ref.1) | copy-start | bytes 1572868
  53.4 46.0 %copy-start.3 = (f32[512]{0:T(512)S(1)}, f32[512]{0:T(512)}, u32[]{:S(2)}) copy-start(f32[512]{0:T(512)} %param.16) | copy-start | bytes 6148
  99.4 1.0 copy-start.2

commit v5 on v4

--- a/solution.py
+++ b/solution.py
@@ -59,18 +59,67 @@
     return column, seq - column * 8, head
 
 
+def iotas(rows):
+    shape = (rows, LANES)
+    return lax.broadcasted_iota(jnp.int32, shape, 0), lax.broadcasted_iota(jnp.int32, shape, 1)
+
+
+def value_picker():
+    row, lane = iotas(LANES)
+    return ((row % 32 < 16) & (lane == 64 + row // 32 * 16 + row % 32)).astype(F32).astype(BF16)
+
+
+def keyed_rows(block, count):
+    row, lane = iotas(TOK)
+    zero = jnp.zeros((TOK, LANES), BF16)
+    valid = row < count
+    flag = jnp.where(valid, zero, jnp.where(lane < 66, jnp.full_like(zero, MASKED), zero))
+    keyed = jnp.where((lane < 64) & valid, block, zero)
+    return keyed, jnp.where(lane < 64, keyed, flag)
+
+
+def turn_values(vals, turned, at, size):
+    ones_row = lax.broadcasted_iota(jnp.int32, (LANES, size), 0) % 32 >= 16
+    picked = lax.dot_general(value_picker(), vals, (((1,), (1,)), ((), ())), preferred_element_type=F32)
+    turned[:, at] = jnp.where(ones_row, 1.0, picked).astype(BF16)
+
+
+def half_of(packed, half):
+    return packed if half == 0 else pltpu.roll(packed.astype(F32), 64, 1).astype(BF16)
+
+
+def spread_heads(packed, lhs):
+    _, lane = iotas(LANES)
+    flags = jnp.where((lane >= 64) & (lane < 66), jnp.ones_like(packed), jnp.zeros_like(packed))
+    for half in range(2):
+        q = half_of(packed, half)
+        for head in range(4):
+            mine = (lane >= 16 * head) & (lane < 16 * head + 16)
+            lhs[pl.ds((head * 2 + half) * LANES, LANES), :] = jnp.where(mine, q, flags)
+
+
+def scores_of(keys, lhs):
+    return lax.dot_general(keys, lhs[...], (((1,), (1,)), ((), ())), preferred_element_type=F32)
+
+
+def head_columns(values, head):
+    return values[:, TOK * head:TOK * head + TOK]
+
+
 def attend_kernel(
-    routes_hbm, local_hbm, counts_hbm, q_hbm, kv_ref, out_ref,
-    routes_ref, local_ref, counts_ref, q_ref, raw, keys, vals, turned, lhs, acc, top, done, sems, small_sems, out_sems,
+    routes_hbm, local_hbm, counts_hbm, q_hbm, kv_ref, own_hbm, own_top_hbm, out_ref,
+    routes_ref, local_ref, counts_ref, q_ref, own_ref, own_top_ref,
+    raw, keys, vals, turned, lhs, acc, top, done, sems, small_sems, out_sems,
 ):
     column, _, head_index = swap_ids()
     seq = column * 8 + head_index
     core = lax.rem(head_index, 2)
     loads = [
-        pltpu.make_async_copy(routes_hbm, routes_ref, small_sems.at[0]),
-        pltpu.make_async_copy(local_hbm, local_ref, small_sems.at[1]),
-        pltpu.make_async_copy(counts_hbm, counts_ref, small_sems.at[2]),
-        pltpu.make_async_copy(q_hbm, q_ref, small_sems.at[3]),
+        pltpu.make_async_copy(source, target, small_sems.at[index])
+        for index, (source, target) in enumerate((
+            (routes_hbm, routes_ref), (local_hbm, local_ref), (counts_hbm, counts_ref),
+            (q_hbm, q_ref), (own_hbm, own_ref), (own_top_hbm, own_top_ref),
+        ))
     ]
     for load in loads:
         load.start()
@@ -78,9 +127,7 @@
         load.wait()
 
     def source(patch, which):
-        if which == 0:
-            return (REACH + core) * NPL + patch, seq * GROUPS + patch * 4
-        row = seq * NPL * CB + patch * CB + which - 1
+        row = seq * NPL * CB + patch * CB + which
         route = routes_ref[0, row]
         offset = jnp.where(route < REACH, route - REACH, route - REACH + 1)
         local = local_ref[0, row]
@@ -88,124 +135,109 @@
         return (offset + REACH + core) * NPL + local, owner * GROUPS + local * 4
 
     for patch in range(NPL):
-        for which in range(CB + 1):
+        for which in range(CB):
             slot, _ = source(patch, which)
-            pltpu.make_async_copy(kv_ref.at[slot], raw.at[patch * 3 + which], sems.at[patch * 3 + which]).start()
-    loads[3].wait()
-
-    lane_kv = lane_of((TOK, LANES))
-    row_kv = lax.broadcasted_iota(jnp.int32, (TOK, LANES), 0)
-    lane_q = lane_of((LANES, LANES))
-    row_q = lax.broadcasted_iota(jnp.int32, (LANES, LANES), 0)
+            pltpu.make_async_copy(kv_ref.at[slot], raw.at[patch * CB + which], sems.at[patch * CB + which]).start()
+    for load in loads[3:]:
+        load.wait()
+
+    row_q, lane_q = iotas(LANES)
+    _, lane_kv = iotas(TOK)
     zero = jnp.zeros((TOK, LANES), BF16)
-    low_lane = lane_kv < 64
     sum_of = ((lane_q == row_q // 16) & (lane_q < 4)).astype(F32).astype(BF16)
-    value_of = ((row_q % 32 < 16) & (lane_q == 64 + row_q // 32 * 16 + row_q % 32)).astype(F32).astype(BF16)
-    ones_row = lax.broadcasted_iota(jnp.int32, (LANES, CHUNK), 0) % 32 >= 16
 
     def patch_body(patch, _):
-        for which in range(CB + 1):
-            pltpu.make_async_copy(kv_ref.at[0], raw.at[patch * 3 + which], sems.at[patch * 3 + which]).wait()
+        for which in range(CB):
+            pltpu.make_async_copy(kv_ref.at[0], raw.at[patch * CB + which], sems.at[patch * CB + which]).wait()
 
         first = jnp.int32(0)
         key_top = jnp.zeros((1, LANES), F32)
         val_top = jnp.zeros((1, LANES), F32)
-        for which in range(CB + 1):
+        for which in range(CB):
             _, shard = source(patch, which)
             for part in range(4):
                 count = counts_ref[shard + part]
-                block = raw[patch * 3 + which, TOK * part:TOK * part + TOK, :]
-                valid = row_kv < count
-                flag = jnp.where(valid, zero, jnp.where(lane_kv < 66, jnp.full_like(zero, MASKED), zero))
-                keyed = jnp.where(low_lane & valid, block, zero)
+                block = raw[patch * CB + which, TOK * part:TOK * part + TOK, :]
+                keyed, marked = keyed_rows(block, count)
                 at = pl.ds(pl.multiple_of(first, 16), TOK)
-                keys[at, :] = jnp.where(low_lane, keyed, flag)
+                keys[at, :] = marked
                 vals[at, :] = block
                 squares = jnp.dot(keyed * keyed, sum_of, preferred_element_type=F32)
                 key_top = jnp.maximum(key_top, jnp.max(squares, axis=0, keepdims=True))
-                size = jnp.max(jnp.where(low_lane, zero, jnp.abs(block)).astype(F32), axis=0, keepdims=True)
+                size = jnp.max(jnp.where(lane_kv < 64, zero, jnp.abs(block)).astype(F32), axis=0, keepdims=True)
                 val_top = jnp.maximum(val_top, size)
                 first = first + (count + 15) // 16 * 16
-        for more in range(CHUNK // TOK):
-            tail = pl.ds(pl.multiple_of(first + more * TOK, 16), TOK)
-            keys[tail, :] = jnp.where(low_lane | (lane_kv >= 66), zero, jnp.full_like(zero, MASKED))
-            vals[tail, :] = zero
-        chunks = (first + CHUNK - 1) // CHUNK
-
-        def turn(chunk, _):
-            at = pl.ds(pl.multiple_of(chunk * CHUNK, CHUNK), CHUNK)
-            picked = lax.dot_general(value_of, vals[at, :], (((1,), (1,)), ((), ())), preferred_element_type=F32)
-            turned[:, at] = jnp.where(ones_row, 1.0, picked).astype(BF16)
+        tail = pl.ds(pl.multiple_of(first, 16), TOK)
+        keys[tail, :] = keyed_rows(zero, 0)[1]
+        vals[tail, :] = zero
+        pieces = (first + TOK - 1) // TOK
+        chunks = pieces // 2
+        odd = pieces % 2 == 1
+
+        def turn(piece, _):
+            at = pl.ds(pl.multiple_of(piece * TOK, TOK), TOK)
+            turn_values(vals[at, :], turned, at, TOK)
             return 0
 
-        lax.fori_loop(0, chunks, turn, 0)
+        lax.fori_loop(0, pieces, turn, 0)
 
         query_top = jnp.zeros((1, LANES), F32)
         for part in range(4):
             packed = q_ref[patch * 4 + part]
             for half in range(2):
-                q = packed if half == 0 else pltpu.roll(packed.astype(F32), 64, 1).astype(BF16)
+                q = half_of(packed, half)
                 q = jnp.where(lane_q < 64, q, jnp.zeros_like(q))
                 squares = jnp.dot(q * q, sum_of, preferred_element_type=F32)
                 query_top = jnp.maximum(query_top, jnp.max(squares, axis=0, keepdims=True))
-        bound = jnp.max(query_top * key_top)
-        small = (bound < 3000.0) & (jnp.max(val_top) < 1e9)
+        small = (jnp.max(query_top * key_top) < 3000.0) & (jnp.max(val_top) < 1e9)
 
         def shard_body(part, _):
-            packed = q_ref[patch * 4 + part]
-            flags = jnp.where((lane_q >= 64) & (lane_q < 66), jnp.ones_like(packed), jnp.zeros_like(packed))
-            for half in range(2):
-                q = packed if half == 0 else pltpu.roll(packed.astype(F32), 64, 1).astype(BF16)
+            shard = patch * 4 + part
+            spread_heads(q_ref[shard], lhs)
+            own_top = own_top_ref[shard]
+
+            def over_chunks(body):
+                def chunk_body(chunk, _):
+                    body(pl.ds(pl.multiple_of(chunk * CHUNK, CHUNK), CHUNK))
+                    return 0
+
+                lax.fori_loop(0, chunks, chunk_body, 0)
+
+                @pl.when(odd)
+                def _():
+                    body(pl.ds(pl.multiple_of(chunks * CHUNK, CHUNK), TOK))
+
+            def begin(scale):
                 for head in range(4):
-                    mine = (lane_q >= 16 * head) & (lane_q < 16 * head + 16)
-                    lhs[pl.ds((head * 2 + half) * LANES, LANES), :] = jnp.where(mine, q, flags)
-            acc[...] = jnp.zeros_like(acc)
-
-            def scores_of(chunk):
-                at = pl.ds(pl.multiple_of(chunk * CHUNK, CHUNK), CHUNK)
-                return at, lax.dot_general(
-                    keys[at, :], lhs[...], (((1,), (1,)), ((), ())), preferred_element_type=F32
-                )
+                    rows = slice(32 * head, 32 * head + 32)
+                    acc[rows] = own_ref[shard, rows] * head_columns(scale, head)
 
             def gather(at, weights):
                 for head in range(4):
                     rows = slice(32 * head, 32 * head + 32)
-                    acc[rows] += jnp.dot(
-                        turned[rows, at], weights[:, TOK * head:TOK * head + TOK], preferred_element_type=F32
-                    )
-
-            @pl.when(small)
+                    acc[rows] += jnp.dot(turned[rows, at], head_columns(weights, head), preferred_element_type=F32)
+
+            fits = small & (jnp.max(jnp.abs(own_top)) < 55.0) & (jnp.max(jnp.abs(own_ref[shard])) < 1e12)
+
+            @pl.when(fits)
             def _():
-                def chunk_body(chunk, _):
-                    at, scores = scores_of(chunk)
-                    gather(at, jnp.exp2(scores).astype(BF16))
-                    return 0
-
-                lax.fori_loop(0, chunks, chunk_body, 0)
-
-            @pl.when(jnp.logical_not(small))
+                begin(jnp.exp2(own_top))
+                over_chunks(lambda at: gather(at, jnp.exp2(scores_of(keys[at, :], lhs)).astype(BF16)))
+
+            @pl.when(jnp.logical_not(fits))
             def _():
-                top[...] = jnp.full_like(top, -jnp.inf)
-
-                def top_body(chunk, _):
-                    _, scores = scores_of(chunk)
-                    top[...] = jnp.maximum(top[...], jnp.max(scores, axis=0, keepdims=True))
-                    return 0
-
-                lax.fori_loop(0, chunks, top_body, 0)
-
-                def chunk_body(chunk, _):
-                    at, scores = scores_of(chunk)
-                    gather(at, jnp.exp2(scores - top[...]).astype(BF16))
-                    return 0
-
-                lax.fori_loop(0, chunks, chunk_body, 0)
+                top[...] = own_top
+
+                def raise_top(at):
+                    top[...] = jnp.maximum(top[...], jnp.max(scores_of(keys[at, :], lhs), axis=0, keepdims=True))
+
+                over_chunks(raise_top)
+                begin(jnp.exp2(own_top - top[...]))
+                over_chunks(lambda at: gather(at, jnp.exp2(scores_of(keys[at, :], lhs) - top[...]).astype(BF16)))
 
             joined = [acc[32 * head:32 * head + 16] / acc[32 * head + 16:32 * head + 32] for head in range(4)]
-            done[patch * 4 + part] = jnp.concatenate(joined, axis=0).astype(BF16)
-            pltpu.make_async_copy(
-                done.at[patch * 4 + part], out_ref.at[patch * 4 + part], out_sems.at[patch * 4 + part]
-            ).start()
+            done[shard] = jnp.concatenate(joined, axis=0).astype(BF16)
+            pltpu.make_async_copy(done.at[shard], out_ref.at[shard], out_sems.at[shard]).start()
             return 0
 
         lax.fori_loop(0, 4, shard_body, 0)
@@ -216,34 +248,37 @@
         pltpu.make_async_copy(done.at[shard], out_ref.at[shard], out_sems.at[shard]).wait()
 
 
-def attend(routes, local, counts, q, kv):
+def attend(routes, local, counts, q, kv, own, own_top):
     hbm = pl.BlockSpec(memory_space=pltpu.HBM)
+    most = CB * PATCH + TOK
     return pl.pallas_call(
         attend_kernel,
         out_shape=jax.ShapeDtypeStruct((GROUPS, 64, TOK), BF16),
-        in_specs=[hbm] * 5,
+        in_specs=[hbm] * 7,
         out_specs=hbm,
         scratch_shapes=[
             pltpu.SMEM((1, LANES), jnp.int32),
             pltpu.SMEM((1, LANES), jnp.int32),
             pltpu.SMEM((256,), jnp.int32),
             pltpu.VMEM((GROUPS, LANES, LANES), BF16),
-            pltpu.VMEM((6, PATCH, LANES), BF16),
-            pltpu.VMEM((3 * PATCH + CHUNK, LANES), BF16),
-            pltpu.VMEM((3 * PATCH + CHUNK, LANES), BF16),
-            pltpu.VMEM((LANES, 3 * PATCH + CHUNK), BF16),
+            pltpu.VMEM((GROUPS, LANES, TOK), F32),
+            pltpu.VMEM((GROUPS, 1, ROWS), F32),
+            pltpu.VMEM((NPL * CB, PATCH, LANES), BF16),
+            pltpu.VMEM((most, LANES), BF16),
+            pltpu.VMEM((most, LANES), BF16),
+            pltpu.VMEM((LANES, most), BF16),
             pltpu.VMEM((ROWS, LANES), BF16),
             pltpu.VMEM((LANES, TOK), F32),
             pltpu.VMEM((1, ROWS), F32),
             pltpu.VMEM((GROUPS, 64, TOK), BF16),
+            pltpu.SemaphoreType.DMA((NPL * CB,)),
             pltpu.SemaphoreType.DMA((6,)),
-            pltpu.SemaphoreType.DMA((4,)),
             pltpu.SemaphoreType.DMA((8,)),
         ],
         compiler_params=pltpu.CompilerParams(vmem_limit_bytes=60 << 20),
-        cost_estimate=pl.CostEstimate(flops=30_000_000_000, bytes_accessed=8_000_000, transcendentals=25_000_000),
+        cost_estimate=pl.CostEstimate(flops=20_000_000_000, bytes_accessed=6_000_000, transcendentals=17_000_000),
         name="attend",
-    )(routes, local, counts, q, kv)
+    )(routes, local, counts, q, kv, own, own_top)
 
 
 def each(body):
@@ -390,9 +425,10 @@
 
 
 def exchange_kernel(
-    points_ref, gain_ref, w_ref, scale_ref, place_ref, route_ref, local_ref, kv_out, q_out, route_out, local_out,
-    kv_ref, q_ref,
-    all_send, all_recv, ring_send, ring_recv, pair_send, pair_recv, route_sem, local_sem,
+    points_ref, gain_ref, w_ref, scale_ref, place_ref, counts_ref, route_ref, local_ref, w1_ref, w2_ref,
+    kv_out, q_out, route_out, local_out, own_out, own_top_out, weights_out,
+    kv_ref, q_ref, raw, queries, keys, turned, lhs, scores, own, own_top,
+    all_send, all_recv, ring_send, ring_recv, pair_send, pair_recv, route_sem, local_sem, load_sem, own_sem,
 ):
     column, plane, head = swap_ids()
     core = lax.rem(head, 2)
@@ -487,6 +523,15 @@
         @pl.when(across | (group != plane))
         def _():
             spread_q(group, head).start()
+
+    joins = [
+        pltpu.make_async_copy(source, weights_out.at[rows_at], load_sem.at[2 + index])
+        for index, (source, rows_at) in enumerate((
+            (w1_ref, pl.ds(0, D)), (w2_ref.at[:, pl.ds(0, 256)], pl.ds(D, 256)), (w2_ref.at[:, pl.ds(256, 256)], pl.ds(D + 256, 256)),
+        ))
+    ]
+    for join in joins:
+        join.start()
 
     normed = normalise(points_ref[...].astype(F32), gain_ref[...]).astype(BF16)
     for couple in range(GROUPS // 2):
@@ -555,7 +600,69 @@
         hop(0, 0, half).start()
         hop(1, 0, half).start()
         shared(2, half).start()
+    def wait_q(shard):
+        @pl.when(across | (shard != head))
+        def _():
+            spread_q(0, shard).wait_recv()
+
+    each(wait_q)
+
+    @pl.when(diagonal)
+    def _():
+        q_at_home.wait()
+
+    loads = [
+        pltpu.make_async_copy(kv_out.at[4 + core], raw, load_sem.at[0]),
+        pltpu.make_async_copy(q_out, queries, load_sem.at[1]),
+    ]
+    for load in loads:
+        load.start()
+    for load in loads:
+        load.wait()
+
+    def own_keys(shard):
+        at = pl.ds(pl.multiple_of(shard * TOK, TOK), TOK)
+        keys[at, :] = keyed_rows(raw[shard], counts_ref[(column * 8 + head) * GROUPS + shard])[1]
+        turn_values(raw[shard], turned, at, TOK)
+
+    each(own_keys)
+
+    def own_saved(shard):
+        return (
+            pltpu.make_async_copy(own.at[shard], own_out.at[shard], own_sem.at[0, shard]),
+            pltpu.make_async_copy(own_top.at[shard], own_top_out.at[shard], own_sem.at[1, shard]),
+        )
+
+    def own_patch(patch):
+        def own_shard(part, _):
+            shard = patch * 4 + part
+            spread_heads(queries[shard], lhs)
+            most = None
+            for piece in range(2):
+                at = slice(patch * PATCH + piece * CHUNK, patch * PATCH + piece * CHUNK + CHUNK)
+                found = scores_of(keys[at, :], lhs)
+                scores[piece] = found
+                found = jnp.max(found, axis=0, keepdims=True)
+                most = found if piece == 0 else jnp.maximum(most, found)
+            own_top[shard] = most
+            total = [None] * 4
+            for piece in range(2):
+                at = slice(patch * PATCH + piece * CHUNK, patch * PATCH + piece * CHUNK + CHUNK)
+                weights = jnp.exp2(scores[piece] - most).astype(BF16)
+                for index in range(4):
+                    rows_of = slice(32 * index, 32 * index + 32)
+                    term = jnp.dot(turned[rows_of, at], head_columns(weights, index), preferred_element_type=F32)
+                    total[index] = term if piece == 0 else total[index] + term
+            for index in range(4):
+                own[shard, 32 * index:32 * index + 32] = total[index]
+            for save in own_saved(shard):
+                save.start()
+            return 0
+
+        lax.fori_loop(0, 4, own_shard, 0)
+
     for half in range(2):
+        own_patch(half)
         hop(0, 0, half).wait_recv()
         hop(0, 1, half).start()
         hop(1, 0, half).wait_recv()
@@ -568,13 +675,6 @@
         hop(1, 1, half).wait_recv()
         shared(4, half).start()
 
-    def wait_q(shard):
-        @pl.when(across | (shard != head))
-        def _():
-            spread_q(0, shard).wait_recv()
-
-    each(wait_q)
-
     def sent(group):
         @pl.when(across | (group != plane))
         def _():
@@ -586,7 +686,6 @@
 
     @pl.when(diagonal)
     def _():
-        q_at_home.wait()
         for copy in routes_at_home:
             copy.wait()
 
@@ -603,9 +702,17 @@
         for place in range(5):
             shared(place, half).wait_send()
             taken(place, half).wait_recv()
-
-
-def exchange(points, gain, w_qkv, routes, local):
+    for join in joins:
+        join.wait()
+
+    def saved(shard):
+        for save in own_saved(shard):
+            save.wait()
+
+    each(saved)
+
+
+def exchange(points, gain, w_qkv, counts, routes, local, w1, w2):
     scale = np.ones((1, 1536), np.float32)
     scale[0, np.arange(1536) % 48 < 16] = HEAD_DIM ** -0.5 * math.log2(math.e)
     vmem = pl.BlockSpec(memory_space=pltpu.VMEM)
@@ -617,12 +724,23 @@
             jax.ShapeDtypeStruct((GROUPS, LANES, LANES), BF16),
             jax.ShapeDtypeStruct((1, LANES), jnp.int32),
             jax.ShapeDtypeStruct((1, LANES), jnp.int32),
+            jax.ShapeDtypeStruct((GROUPS, LANES, TOK), F32),
+            jax.ShapeDtypeStruct((GROUPS, 1, ROWS), F32),
+            jax.ShapeDtypeStruct((2 * D, 256), BF16),
         ),
-        in_specs=[vmem] * 5 + [anywhere] * 2,
-        out_specs=(anywhere,) * 4,
+        in_specs=[vmem] * 5 + [pl.BlockSpec(memory_space=pltpu.SMEM)] + [anywhere] * 4,
+        out_specs=(anywhere,) * 7,
         scratch_shapes=[
             pltpu.VMEM((GROUPS, TOK, LANES), BF16),
             pltpu.VMEM((GROUPS, LANES, LANES), BF16),
+            pltpu.VMEM((GROUPS, TOK, LANES), BF16),
+            pltpu.VMEM((GROUPS, LANES, LANES), BF16),
+            pltpu.VMEM((NPL * PATCH, LANES), BF16),
+            pltpu.VMEM((LANES, NPL * PATCH), BF16),
+            pltpu.VMEM((ROWS, LANES), BF16),
+            pltpu.VMEM((2, CHUNK, ROWS), F32),
+            pltpu.VMEM((GROUPS, LANES, TOK), F32),
+            pltpu.VMEM((GROUPS, 1, ROWS), F32),
             pltpu.SemaphoreType.DMA((3, 8)),
             pltpu.SemaphoreType.DMA((3, 8)),
             pltpu.SemaphoreType.DMA((2, 2, 2)),
@@ -630,26 +748,29 @@
             pltpu.SemaphoreType.DMA((5, 2)),
             pltpu.SemaphoreType.DMA((5, 2)),
             pltpu.SemaphoreType.DMA((2, 2)),
-            pltpu.SemaphoreType.DMA((7,)),
+            pltpu.SemaphoreType.DMA((5,)),
+            pltpu.SemaphoreType.DMA((5,)),
+            pltpu.SemaphoreType.DMA((2, 8)),
         ],
         compiler_params=pltpu.CompilerParams(collective_id=0, has_side_effects=True, vmem_limit_bytes=60 << 20),
         name="exchange",
     )(
-        points, gain.reshape(1, D), w_qkv, jnp.asarray(scale), jnp.asarray(placing(), BF16), routes, local,
+        points, gain.reshape(1, D), w_qkv, jnp.asarray(scale), jnp.asarray(placing(), BF16),
+        counts, routes, local, w1, w2,
     )
 
 
 def per_device(
     points, gain_attn, w_qkv, w_out, gain_mlp, w_fc1, w_fc2, contact_route, contact_patch, counts
 ):
-    slots, q, routes, local = exchange(points, gain_attn, w_qkv, contact_route.reshape(1, -1), contact_patch)
-    own = jnp.concatenate([w_fc1, w_fc2[:, :256], w_fc2[:, 256:]], axis=0)
-    own, routes = lax.optimization_barrier((own, routes))
-    weights = [own]
+    slots, q, routes, local, sums, tops, joined = exchange(
+        points, gain_attn, w_qkv, counts, contact_route.reshape(1, -1), contact_patch, w_fc1, w_fc2
+    )
+    weights = [joined]
     for step in range(1, 4):
         pairs = [(head, (head + 2 * step) % GROUPS) for head in range(GROUPS)]
-        weights.append(lax.ppermute(own, "head", pairs))
-    packed = attend(routes, local, counts, q, slots.reshape(20, PATCH, LANES))
+        weights.append(lax.ppermute(joined, "head", pairs))
+    packed = attend(routes, local, counts, q, slots.reshape(20, PATCH, LANES), sums, tops)
     return finish(points, packed, w_out, gain_mlp, weights)
 
 

time: 132 us -> 126 us (0.955)
  Pallas kernels: 125 us -> 116 us
  starting transfers between devices: 3.67 us -> 8.13 us
    pallas_call x1, Pallas kernels: 45.9 us -> 32.3 us  [attend(): pl.pallas_call(attend_kernel, out_shape=jax.ShapeDtypeStruct((GROUPS, 64,...]
    ppermute x3, starting transfers between devices: 3.67 us -> 8.13 us  [per_device(): weights.append(lax.ppermute(joined, 'head', pairs))]
    pallas_call x1, Pallas kernels: 47.8 us -> 51.8 us  [exchange(): pl.pallas_call(exchange_kernel, out_shape=(jax.ShapeDtypeStruct((10, GROU...]
  transfers between devices with their start and end apart: 3 -> 3, of which waited for: 0 -> 0; matrix products, arithmetic and copies ran while one was open for 0% -> 0% of each run, Pallas kernels for 35% -> 26%
where the time goes in v5:
time: 126 us
  Pallas kernels  116 us (92%)
  starting transfers between devices  8.13 us (6%)
  local copies, waits for them, and re-layouts  1.67 us (1%)
    pallas_call x1, Pallas kernels, exchange(): pl.pallas_call(exchange_kernel, out_shape=(jax.ShapeDtypeStruct((10, GROU...  51.8 us
    pallas_call x1, Pallas kernels, attend(): pl.pallas_call(attend_kernel, out_shape=jax.ShapeDtypeStruct((GROUPS, 64,...  32.3 us
    pallas_call x1, Pallas kernels, finish(): pl.pallas_call(finish_kernel, out_shape=jax.ShapeDtypeStruct((TOK, D), BF...  31.9 us
    ppermute x3, starting transfers between devices, per_device(): weights.append(lax.ppermute(joined, 'head', pairs))  8.13 us
  transfers between devices with their start and end apart: 3, of which 0 were waited for; matrix products, arithmetic and copies ran while one was open for 0% of the time, Pallas kernels for 26%

profile of v5, /device:TPU:25, one launch (start us, length us, event | category | flops | bytes accessed | tf_op | source)
XLA Modules:
  0.0 125.8 jit_solution(5375167704463840957)
XLA Ops:
  0.0 51.8 %exchange.1 = (bf16[10,8,256,128]{3,2,1,0:T(8,128)(2,1)}, bf16[8,128,128]{2,1,0:T(8,128)(2,1)}, s32[1,128]{1,0:T(1,128)}, s32[1,128]{1,0:T(1,128)}, f32[8,128,25...) custom-call(bf16[256,512]{1,0:T(8,128)(2,1)} %points_ref.3, f32[1,512]{1,0:T(1,128)} %bitcast.5, ...), custom_call_target="tpu_custom_call" | custom-call | tf_op jit(solution)/shard_map/exchange/pallas_call | solution.py:720
  51.8 3.4 %collective-permute-start.2 = (bf16[1024,256]{1,0:T(8,128)(2,1)}, bf16[1024,256]{1,0:T(8,128)(2,1)S(1)}, u32[]{:S(2)}, u32[]{:S(2)}) collective-permute-start(bf16[1024,256]{1,0:T(8,128)(2,1)} %get-tuple-element.18.w0_ref), channel_id=1, source_target_pairs={{0,6},{1,7},{2,0},{3,1},{4,2},{5,3},{6,4},{7,5},{8,14},{9,15},{10,... | collective-permute-start | bytes 1572872 | tf_op jit(solution)/shard_map/ppermute | solution.py:772
  55.2 4.7 %collective-permute-start.1 = (bf16[1024,256]{1,0:T(8,128)(2,1)}, bf16[1024,256]{1,0:T(8,128)(2,1)S(1)}, u32[]{:S(2)}, u32[]{:S(2)}) collective-permute-start(bf16[1024,256]{1,0:T(8,128)(2,1)} %get-tuple-element.18.w0_ref), channel_id=1, source_target_pairs={{0,4},{1,5},{2,6},{3,7},{4,0},{5,1},{6,2},{7,3},{8,12},{9,13},{10,... | collective-permute-start | bytes 1572872 | tf_op jit(solution)/shard_map/ppermute | solution.py:772
  59.9 0.0 collective-permute-start
  59.9 0.0 copy-start
  60.0 0.0 copy-start.1
  60.0 0.0 copy-start.2
  60.0 0.0 copy-start.4
  60.0 32.3 %attend.1.packed_ref = bf16[8,64,256]{2,1,0:T(8,128)(2,1)} custom-call(s32[1,128]{1,0:T(1,128)} %get-tuple-element.12.routes_hbm, s32[1,128]{1,0:T(1,128)} %get-tuple-element.13.local_hbm, s32[256]{0:T(256)} %counts_hbm.1, bf16[8,128,128]{2,1,0:T(8,128)(2,1)} %get-tuple-element.14.q_hbm, bf16[20,1024,128]{2,1,0:T(8,128)(2,1)} %bitcast.7, ...), custom_call_target="tpu_custom_call" | custom-call | flops 20000000000 | bytes 6000000 | tf_op jit(solution)/shard_map/attend/pallas_call | solution.py:254
  92.2 0.0 collective-permute-done.2.w3_ref
  92.3 0.0 collective-permute-done.1.w2_ref
  92.3 0.0 collective-permute-done.w1_ref
  92.3 0.0 copy-done
  92.3 0.0 copy-done.1
  92.3 0.0 copy-done.2
  92.3 0.0 copy-done.4
  92.3 0.0 copy-start.3
  92.3 0.9 copy-done.3
  93.3 31.9 %finish.1 = bf16[256,512]{1,0:T(8,128)(2,1)S(1)} custom-call(bf16[256,512]{1,0:T(8,128)(2,1)S(1)} %copy-done, bf16[8,64,256]{2,1,0:T(8,128)(2,1)S(1)} %copy-done.3, bf16[512,512]{1,0:T(8,128)(2,1)S(1)} %copy-done.1, f32[1,512]{1,0:T(1,128)S(1)} %bitcast.4, bf16[1024,256]{1,0:T(8,128)(2,1)S(1)} %copy-done.2, ...), custom_call_target="tpu_custom_call" | custom-call | tf_op jit(solution)/shard_map/finish/pallas_call | solution.py:401
  125.1 0.7 copy.14
Async XLA Ops:
  51.8 40.4 %collective-permute-start.2 = (bf16[1024,256]{1,0:T(8,128)(2,1)}, bf16[1024,256]{1,0:T(8,128)(2,1)S(1)}, u32[]{:S(2)}, u32[]{:S(2)}) collective-permute-start(bf16[1024,256]{1,0:T(8,128)(2,1)} %get-tuple-element.18.w0_ref), channel_id=1, source_target_pairs={{0,6},{1,7},{2,0},{3,1},{4,2},{5,3},{6,4},{7,5},{8,14},{9,15},{10,... | collective-permute-start | bytes 1572872 | tf_op jit(solution)/shard_map/ppermute | solution.py:772
  55.2 37.0 %collective-permute-start.1 = (bf16[1024,256]{1,0:T(8,128)(2,1)}, bf16[1024,256]{1,0:T(8,128)(2,1)S(1)}, u32[]{:S(2)}, u32[]{:S(2)}) collective-permute-start(bf16[1024,256]{1,0:T(8,128)(2,1)} %get-tuple-element.18.w0_ref), channel_id=1, source_target_pairs={{0,4},{1,5},{2,6},{3,7},{4,0},{5,1},{6,2},{7,3},{8,12},{9,13},{10,... | collective-permute-start | bytes 1572872 | tf_op jit(solution)/shard_map/ppermute | solution.py:772
  59.9 32.3 %collective-permute-start = (bf16[1024,256]{1,0:T(8,128)(2,1)}, bf16[1024,256]{1,0:T(8,128)(2,1)S(1)}, u32[]{:S(2)}, u32[]{:S(2)}) collective-permute-start(bf16[1024,256]{1,0:T(8,128)(2,1)} %get-tuple-element.18.w0_ref), channel_id=1, source_target_pairs={{0,2},{1,3},{2,4},{3,5},{4,6},{5,7},{6,0},{7,1},{8,10},{9,11},{10,... | collective-permute-start | bytes 1572872 | tf_op jit(solution)/shard_map/ppermute | solution.py:772
  59.9 32.3 %copy-start = (bf16[256,512]{1,0:T(8,128)(2,1)S(1)}, bf16[256,512]{1,0:T(8,128)(2,1)}, u32[]{:S(2)}) copy-start(bf16[256,512]{1,0:T(8,128)(2,1)} %points_ref.3) | copy-start | bytes 786436
  60.0 32.3 %copy-start.1 = (bf16[512,512]{1,0:T(8,128)(2,1)S(1)}, bf16[512,512]{1,0:T(8,128)(2,1)}, u32[]{:S(2)}) copy-start(bf16[512,512]{1,0:T(8,128)(2,1)} %w_out_ref.1) | copy-start | bytes 1572868
  60.0 32.3 %copy-start.2 = (bf16[1024,256]{1,0:T(8,128)(2,1)S(1)}, bf16[1024,256]{1,0:T(8,128)(2,1)}, u32[]{:S(2)}) copy-start(bf16[1024,256]{1,0:T(8,128)(2,1)} %get-tuple-element.18.w0_ref) | copy-start | bytes 1572868
  60.0 32.4 %copy-start.4 = (f32[512]{0:T(512)S(1)}, f32[512]{0:T(512)}, u32[]{:S(2)}) copy-start(f32[512]{0:T(512)} %param.16) | copy-start | bytes 6148
  92.3 1.0 copy-start.3

commit v6 on v5

--- a/solution.py
+++ b/solution.py
@@ -78,6 +78,14 @@
     return keyed, jnp.where(lane < 64, keyed, flag)
 
 
+def norms(values):
+    row, lane = iotas(LANES)
+    sum_of = ((lane == row // 16) & (lane < 4)).astype(F32).astype(BF16)
+    size = jnp.minimum(jnp.abs(values), jnp.full_like(values, 1e15))
+    size = jnp.where(lax.broadcasted_iota(jnp.int32, values.shape, 1) < 64, size, jnp.zeros_like(size))
+    return jnp.max(jnp.dot(size * size, sum_of, preferred_element_type=F32), axis=0, keepdims=True)
+
+
 def turn_values(vals, turned, at, size):
     ones_row = lax.broadcasted_iota(jnp.int32, (LANES, size), 0) % 32 >= 16
     picked = lax.dot_general(value_picker(), vals, (((1,), (1,)), ((), ())), preferred_element_type=F32)
@@ -107,8 +115,8 @@
 
 
 def attend_kernel(
-    routes_hbm, local_hbm, counts_hbm, q_hbm, kv_ref, own_hbm, own_top_hbm, out_ref,
-    routes_ref, local_ref, counts_ref, q_ref, own_ref, own_top_ref,
+    routes_hbm, local_hbm, counts_hbm, q_hbm, kv_ref, own_hbm, own_top_hbm, own_size_hbm, own_query_hbm, out_ref,
+    routes_ref, local_ref, counts_ref, q_ref, own_ref, own_top_ref, own_size_ref, own_query_ref,
     raw, keys, vals, turned, lhs, acc, top, done, sems, small_sems, out_sems,
 ):
     column, _, head_index = swap_ids()
@@ -119,6 +127,7 @@
         for index, (source, target) in enumerate((
             (routes_hbm, routes_ref), (local_hbm, local_ref), (counts_hbm, counts_ref),
             (q_hbm, q_ref), (own_hbm, own_ref), (own_top_hbm, own_top_ref),
+            (own_size_hbm, own_size_ref), (own_query_hbm, own_query_ref),
         ))
     ]
     for load in loads:
@@ -141,10 +150,8 @@
     for load in loads[3:]:
         load.wait()
 
-    row_q, lane_q = iotas(LANES)
     _, lane_kv = iotas(TOK)
     zero = jnp.zeros((TOK, LANES), BF16)
-    sum_of = ((lane_q == row_q // 16) & (lane_q < 4)).astype(F32).astype(BF16)
 
     def patch_body(patch, _):
         for which in range(CB):
@@ -162,8 +169,7 @@
                 at = pl.ds(pl.multiple_of(first, 16), TOK)
                 keys[at, :] = marked
                 vals[at, :] = block
-                squares = jnp.dot(keyed * keyed, sum_of, preferred_element_type=F32)
-                key_top = jnp.maximum(key_top, jnp.max(squares, axis=0, keepdims=True))
+                key_top = jnp.maximum(key_top, norms(keyed))
                 size = jnp.max(jnp.where(lane_kv < 64, zero, jnp.abs(block)).astype(F32), axis=0, keepdims=True)
                 val_top = jnp.maximum(val_top, size)
                 first = first + (count + 15) // 16 * 16
@@ -181,20 +187,17 @@
 
         lax.fori_loop(0, pieces, turn, 0)
 
-        query_top = jnp.zeros((1, LANES), F32)
-        for part in range(4):
-            packed = q_ref[patch * 4 + part]
-            for half in range(2):
-                q = half_of(packed, half)
-                q = jnp.where(lane_q < 64, q, jnp.zeros_like(q))
-                squares = jnp.dot(q * q, sum_of, preferred_element_type=F32)
-                query_top = jnp.maximum(query_top, jnp.max(squares, axis=0, keepdims=True))
-        small = (jnp.max(query_top * key_top) < 3000.0) & (jnp.max(val_top) < 1e9)
-
-        def shard_body(part, _):
-            shard = patch * 4 + part
-            spread_heads(q_ref[shard], lhs)
-            own_top = own_top_ref[shard]
+        query_top, own_size = own_query_ref[patch * 4], own_size_ref[patch * 4]
+        for part in range(1, 4):
+            query_top = jnp.maximum(query_top, own_query_ref[patch * 4 + part])
+            own_size = jnp.maximum(own_size, own_size_ref[patch * 4 + part])
+        sizes = jnp.maximum(query_top * key_top * (1.0 / 3000.0), val_top * 1e-9)
+        fits = jnp.maximum(jnp.max(sizes), jnp.max(own_size)) < 1.0
+
+        def shards_body(couple, _):
+            shards = [patch * 4 + couple * 2 + side for side in range(2)]
+            for side in range(2):
+                spread_heads(q_ref[shards[side]], lhs.at[pl.ds(side * ROWS, ROWS)])
 
             def over_chunks(body):
                 def chunk_body(chunk, _):
@@ -207,40 +210,48 @@
                 def _():
                     body(pl.ds(pl.multiple_of(chunks * CHUNK, CHUNK), TOK))
 
-            def begin(scale):
+            def begin(side, scale):
                 for head in range(4):
                     rows = slice(32 * head, 32 * head + 32)
-                    acc[rows] = own_ref[shard, rows] * head_columns(scale, head)
+                    acc[side, rows] = own_ref[shards[side], rows] * head_columns(scale, head)
 
             def gather(at, weights):
-                for head in range(4):
-                    rows = slice(32 * head, 32 * head + 32)
-                    acc[rows] += jnp.dot(turned[rows, at], head_columns(weights, head), preferred_element_type=F32)
-
-            fits = small & (jnp.max(jnp.abs(own_top)) < 55.0) & (jnp.max(jnp.abs(own_ref[shard])) < 1e12)
+                for side in range(2):
+                    for head in range(4):
+                        rows = slice(32 * head, 32 * head + 32)
+                        acc[side, rows] += jnp.dot(
+                            turned[rows, at], head_columns(weights, side * 4 + head), preferred_element_type=F32
+                        )
 
             @pl.when(fits)
             def _():
-                begin(jnp.exp2(own_top))
+                for side in range(2):
+                    begin(side, jnp.exp2(own_top_ref[shards[side]]))
                 over_chunks(lambda at: gather(at, jnp.exp2(scores_of(keys[at, :], lhs)).astype(BF16)))
 
             @pl.when(jnp.logical_not(fits))
             def _():
-                top[...] = own_top
+                for side in range(2):
+                    top[:, pl.ds(side * ROWS, ROWS)] = own_top_ref[shards[side]]
 
                 def raise_top(at):
                     top[...] = jnp.maximum(top[...], jnp.max(scores_of(keys[at, :], lhs), axis=0, keepdims=True))
 
                 over_chunks(raise_top)
-                begin(jnp.exp2(own_top - top[...]))
+                for side in range(2):
+                    begin(side, jnp.exp2(own_top_ref[shards[side]] - top[:, pl.ds(side * ROWS, ROWS)]))
                 over_chunks(lambda at: gather(at, jnp.exp2(scores_of(keys[at, :], lhs) - top[...]).astype(BF16)))
 
-            joined = [acc[32 * head:32 * head + 16] / acc[32 * head + 16:32 * head + 32] for head in range(4)]
-            done[shard] = jnp.concatenate(joined, axis=0).astype(BF16)
-            pltpu.make_async_copy(done.at[shard], out_ref.at[shard], out_sems.at[shard]).start()
+            for side in range(2):
+                joined = [
+                    acc[side, 32 * head:32 * head + 16] / acc[side, 32 * head + 16:32 * head + 32] for head in range(4)
+                ]
+                shard = shards[side]
+                done[shard] = jnp.concatenate(joined, axis=0).astype(BF16)
+                pltpu.make_async_copy(done.at[shard], out_ref.at[shard], out_sems.at[shard]).start()
             return 0
 
-        lax.fori_loop(0, 4, shard_body, 0)
+        lax.fori_loop(0, 2, shards_body, 0)
         return 0
 
     lax.fori_loop(0, NPL, patch_body, 0)
@@ -248,13 +259,13 @@
         pltpu.make_async_copy(done.at[shard], out_ref.at[shard], out_sems.at[shard]).wait()
 
 
-def attend(routes, local, counts, q, kv, own, own_top):
+def attend(routes, local, counts, q, kv, own, own_top, own_size, own_query):
     hbm = pl.BlockSpec(memory_space=pltpu.HBM)
     most = CB * PATCH + TOK
     return pl.pallas_call(
         attend_kernel,
         out_shape=jax.ShapeDtypeStruct((GROUPS, 64, TOK), BF16),
-        in_specs=[hbm] * 7,
+        in_specs=[hbm] * 9,
         out_specs=hbm,
         scratch_shapes=[
             pltpu.SMEM((1, LANES), jnp.int32),
@@ -263,22 +274,24 @@
             pltpu.VMEM((GROUPS, LANES, LANES), BF16),
             pltpu.VMEM((GROUPS, LANES, TOK), F32),
             pltpu.VMEM((GROUPS, 1, ROWS), F32),
+            pltpu.VMEM((GROUPS, 1, ROWS), F32),
+            pltpu.VMEM((GROUPS, 1, LANES), F32),
             pltpu.VMEM((NPL * CB, PATCH, LANES), BF16),
             pltpu.VMEM((most, LANES), BF16),
             pltpu.VMEM((most, LANES), BF16),
             pltpu.VMEM((LANES, most), BF16),
-            pltpu.VMEM((ROWS, LANES), BF16),
-            pltpu.VMEM((LANES, TOK), F32),
-            pltpu.VMEM((1, ROWS), F32),
+            pltpu.VMEM((2 * ROWS, LANES), BF16),
+            pltpu.VMEM((2, LANES, TOK), F32),
+            pltpu.VMEM((1, 2 * ROWS), F32),
             pltpu.VMEM((GROUPS, 64, TOK), BF16),
             pltpu.SemaphoreType.DMA((NPL * CB,)),
-            pltpu.SemaphoreType.DMA((6,)),
+            pltpu.SemaphoreType.DMA((8,)),
             pltpu.SemaphoreType.DMA((8,)),
         ],
         compiler_params=pltpu.CompilerParams(vmem_limit_bytes=60 << 20),
         cost_estimate=pl.CostEstimate(flops=20_000_000_000, bytes_accessed=6_000_000, transcendentals=17_000_000),
         name="attend",
-    )(routes, local, counts, q, kv, own, own_top)
+    )(routes, local, counts, q, kv, own, own_top, own_size, own_query)
 
 
 def each(body):
@@ -426,9 +439,9 @@
 
 def exchange_kernel(
     points_ref, gain_ref, w_ref, scale_ref, place_ref, counts_ref, route_ref, local_ref, w1_ref, w2_ref,
-    kv_out, q_out, route_out, local_out, own_out, own_top_out, weights_out,
-    kv_ref, q_ref, raw, queries, keys, turned, lhs, scores, own, own_top,
-    all_send, all_recv, ring_send, ring_recv, pair_send, pair_recv, route_sem, local_sem, load_sem, own_sem,
+    kv_out, q_out, route_out, local_out, own_out, own_top_out, own_size_out, own_query_out, weights_out,
+    kv_ref, q_ref, raw, queries, keys, turned, lhs, scores, own, own_top, own_size, own_query,
+    all_send, all_recv, ring_send, ring_recv, pair_send, pair_recv, route_sem, local_sem, load_sem, own_sem, over_send, over_recv,
 ):
     column, plane, head = swap_ids()
     core = lax.rem(head, 2)
@@ -450,17 +463,19 @@
         return 0
 
     lax.fori_loop(0, 8, greet, 0)
-    for other in (right, left, pair):
+    over_right = (lax.rem(column + 1, 4) * 8 + plane, head)
+    over_left = (lax.rem(column + 3, 4) * 8 + plane, head)
+    for other in (right, left, pair, over_right, over_left):
         pl.semaphore_signal(barrier, inc=1, device_id=other, device_id_type=MESH)
 
     def enter():
         @pl.when(diagonal)
         def _():
-            pl.semaphore_wait(barrier, 10)
+            pl.semaphore_wait(barrier, 12)
 
         @pl.when(across)
         def _():
-            pl.semaphore_wait(barrier, 11)
+            pl.semaphore_wait(barrier, 13)
 
     def rows(half):
         return pl.ds(half * LANES, LANES)
@@ -631,49 +646,73 @@
         return (
             pltpu.make_async_copy(own.at[shard], own_out.at[shard], own_sem.at[0, shard]),
             pltpu.make_async_copy(own_top.at[shard], own_top_out.at[shard], own_sem.at[1, shard]),
+            pltpu.make_async_copy(own_size.at[shard], own_size_out.at[shard], own_sem.at[2, shard]),
+            pltpu.make_async_copy(own_query.at[shard], own_query_out.at[shard], own_sem.at[3, shard]),
         )
 
-    def own_patch(patch):
-        def own_shard(part, _):
-            shard = patch * 4 + part
-            spread_heads(queries[shard], lhs)
+    def own_run(begin, end):
+        def own_shard(shard, _):
+            patch = shard // 4
+            packed = queries[shard]
+            spread_heads(packed, lhs)
             most = None
+            spots = [pl.ds(pl.multiple_of(patch * PATCH + piece * CHUNK, CHUNK), CHUNK) for piece in range(2)]
             for piece in range(2):
-                at = slice(patch * PATCH + piece * CHUNK, patch * PATCH + piece * CHUNK + CHUNK)
-                found = scores_of(keys[at, :], lhs)
+                found = scores_of(keys[spots[piece], :], lhs)
                 scores[piece] = found
                 found = jnp.max(found, axis=0, keepdims=True)
                 most = found if piece == 0 else jnp.maximum(most, found)
             own_top[shard] = most
             total = [None] * 4
             for piece in range(2):
-                at = slice(patch * PATCH + piece * CHUNK, patch * PATCH + piece * CHUNK + CHUNK)
                 weights = jnp.exp2(scores[piece] - most).astype(BF16)
                 for index in range(4):
                     rows_of = slice(32 * index, 32 * index + 32)
-                    term = jnp.dot(turned[rows_of, at], head_columns(weights, index), preferred_element_type=F32)
+                    term = jnp.dot(
+                        turned[rows_of, spots[piece]], head_columns(weights, index), preferred_element_type=F32
+                    )
                     total[index] = term if piece == 0 else total[index] + term
             for index in range(4):
                 own[shard, 32 * index:32 * index + 32] = total[index]
+                columns = slice(TOK * index, TOK * index + TOK)
+                size = jnp.max(jnp.abs(total[index]), axis=0, keepdims=True) * 1e-12
+                own_size[shard, :, columns] = jnp.maximum(size, jnp.abs(most[:, columns]) * (1.0 / 55.0))
+            own_query[shard] = jnp.maximum(norms(half_of(packed, 0)), norms(half_of(packed, 1)))
             for save in own_saved(shard):
                 save.start()
             return 0
 
-        lax.fori_loop(0, 4, own_shard, 0)
-
-    for half in range(2):
-        own_patch(half)
-        hop(0, 0, half).wait_recv()
-        hop(0, 1, half).start()
-        hop(1, 0, half).wait_recv()
-        hop(1, 1, half).start()
-        shared(1, half).start()
-        shared(3, half).start()
-    for half in range(2):
-        hop(0, 1, half).wait_recv()
-        shared(0, half).start()
-        hop(1, 1, half).wait_recv()
-        shared(4, half).start()
+        lax.fori_loop(begin, end, own_shard, 0)
+
+    def swapped(way):
+        if way == 0:
+            source, target, half, to = 8 + core, core, 1, over_right
+        else:
+            source, target, half, to = core, 8 + core, 0, over_left
+        return moved(source, target, half, over_send.at[way], over_recv.at[way], to)
+
+    own_run(0, 5)
+    hop(0, 0, 0).wait_recv()
+    hop(0, 1, 0).start()
+    hop(1, 0, 1).wait_recv()
+    hop(1, 1, 1).start()
+    shared(1, 0).start()
+    shared(3, 1).start()
+    hop(0, 0, 1).wait_recv()
+    shared(1, 1).start()
+    hop(1, 0, 0).wait_recv()
+    shared(3, 0).start()
+    own_run(5, 8)
+    hop(0, 1, 0).wait_recv()
+    swapped(1).start()
+    hop(1, 1, 1).wait_recv()
+    swapped(0).start()
+    shared(0, 0).start()
+    shared(4, 1).start()
+    swapped(0).wait_recv()
+    shared(0, 1).start()
+    swapped(1).wait_recv()
+    shared(4, 0).start()
 
     def sent(group):
         @pl.when(across | (group != plane))
@@ -697,11 +736,14 @@
 
     for half in range(2):
         for way in range(2):
-            for step in range(2):
-                hop(way, step, half).wait_send()
+            hop(way, 0, half).wait_send()
         for place in range(5):
             shared(place, half).wait_send()
             taken(place, half).wait_recv()
+    hop(0, 1, 0).wait_send()
+    hop(1, 1, 1).wait_send()
+    swapped(0).wait_send()
+    swapped(1).wait_send()
     for join in joins:
         join.wait()
 
@@ -726,10 +768,12 @@
             jax.ShapeDtypeStruct((1, LANES), jnp.int32),
             jax.ShapeDtypeStruct((GROUPS, LANES, TOK), F32),
             jax.ShapeDtypeStruct((GROUPS, 1, ROWS), F32),
+            jax.ShapeDtypeStruct((GROUPS, 1, ROWS), F32),
+            jax.ShapeDtypeStruct((GROUPS, 1, LANES), F32),
             jax.ShapeDtypeStruct((2 * D, 256), BF16),
         ),
         in_specs=[vmem] * 5 + [pl.BlockSpec(memory_space=pltpu.SMEM)] + [anywhere] * 4,
-        out_specs=(anywhere,) * 7,
+        out_specs=(anywhere,) * 9,
         scratch_shapes=[
             pltpu.VMEM((GROUPS, TOK, LANES), BF16),
             pltpu.VMEM((GROUPS, LANES, LANES), BF16),
@@ -741,6 +785,8 @@
             pltpu.VMEM((2, CHUNK, ROWS), F32),
             pltpu.VMEM((GROUPS, LANES, TOK), F32),
             pltpu.VMEM((GROUPS, 1, ROWS), F32),
+            pltpu.VMEM((GROUPS, 1, ROWS), F32),
+            pltpu.VMEM((GROUPS, 1, LANES), F32),
             pltpu.SemaphoreType.DMA((3, 8)),
             pltpu.SemaphoreType.DMA((3, 8)),
             pltpu.SemaphoreType.DMA((2, 2, 2)),
@@ -750,7 +796,9 @@
             pltpu.SemaphoreType.DMA((2, 2)),
             pltpu.SemaphoreType.DMA((5,)),
             pltpu.SemaphoreType.DMA((5,)),
-            pltpu.SemaphoreType.DMA((2, 8)),
+            pltpu.SemaphoreType.DMA((4, 8)),
+            pltpu.SemaphoreType.DMA((2,)),
+            pltpu.SemaphoreType.DMA((2,)),
         ],
         compiler_params=pltpu.CompilerParams(collective_id=0, has_side_effects=True, vmem_limit_bytes=60 << 20),
         name="exchange",
@@ -763,14 +811,14 @@
 def per_device(
     points, gain_attn, w_qkv, w_out, gain_mlp, w_fc1, w_fc2, contact_route, contact_patch, counts
 ):
-    slots, q, routes, local, sums, tops, joined = exchange(
+    slots, q, routes, local, sums, tops, sizes, tallest, joined = exchange(
         points, gain_attn, w_qkv, counts, contact_route.reshape(1, -1), contact_patch, w_fc1, w_fc2
     )
     weights = [joined]
     for step in range(1, 4):
         pairs = [(head, (head + 2 * step) % GROUPS) for head in range(GROUPS)]
         weights.append(lax.ppermute(joined, "head", pairs))
-    packed = attend(routes, local, counts, q, slots.reshape(20, PATCH, LANES), sums, tops)
+    packed = attend(routes, local, counts, q, slots.reshape(20, PATCH, LANES), sums, tops, sizes, tallest)
     return finish(points, packed, w_out, gain_mlp, weights)
 
 

time: 126 us -> 124 us (0.984); the launches traced: 126 us -> 122 us
  starting transfers between devices: 8.13 us -> 3.67 us
    pallas_call x1, Pallas kernels: 51.8 us -> 58.1 us  [exchange(): pl.pallas_call(exchange_kernel, out_shape=(jax.ShapeDtypeStruct((10, GROU...]
    ppermute x3, starting transfers between devices: 8.13 us -> 3.67 us  [per_device(): weights.append(lax.ppermute(joined, 'head', pairs))]
    pallas_call x1, Pallas kernels: 32.3 us -> 29 us  [attend(): pl.pallas_call(attend_kernel, out_shape=jax.ShapeDtypeStruct((GROUPS, 64,...]
    pallas_call x1, Pallas kernels: 31.9 us -> 29.9 us  [finish(): pl.pallas_call(finish_kernel, out_shape=jax.ShapeDtypeStruct((TOK, D), BF...]
  transfers between devices with their start and end apart: 3 -> 3, of which waited for: 0 -> 0; matrix products, arithmetic and copies ran while one was open for 0% -> 0% of each run, Pallas kernels for 26% -> 24%
where the time goes in v6:
time: 124 us; the launch traced here: 122 us
  Pallas kernels  117 us (94%)
  starting transfers between devices  3.67 us (3%)
  local copies, waits for them, and re-layouts  1.67 us (1%)
    pallas_call x1, Pallas kernels, exchange(): pl.pallas_call(exchange_kernel, out_shape=(jax.ShapeDtypeStruct((10, GROU...  58.1 us
    pallas_call x1, Pallas kernels, finish(): pl.pallas_call(finish_kernel, out_shape=jax.ShapeDtypeStruct((TOK, D), BF...  29.9 us
    pallas_call x1, Pallas kernels, attend(): pl.pallas_call(attend_kernel, out_shape=jax.ShapeDtypeStruct((GROUPS, 64,...  29 us
    ppermute x3, starting transfers between devices, per_device(): weights.append(lax.ppermute(joined, 'head', pairs))  3.67 us
  transfers between devices with their start and end apart: 3, of which 0 were waited for; matrix products, arithmetic and copies ran while one was open for 0% of the time, Pallas kernels for 24%

profile of v6, /device:TPU:25, one launch (start us, length us, event | category | flops | bytes accessed | tf_op | source)
XLA Modules:
  0.0 122.5 jit_solution(7197284727730063759)
XLA Ops:
  0.0 58.1 %exchange.1 = (bf16[10,8,256,128]{3,2,1,0:T(8,128)(2,1)}, bf16[8,128,128]{2,1,0:T(8,128)(2,1)}, s32[1,128]{1,0:T(1,128)}, s32[1,128]{1,0:T(1,128)}, f32[8,128,25...) custom-call(bf16[256,512]{1,0:T(8,128)(2,1)} %points_ref.3, ...), custom_call_target="tpu_custom_call" | custom-call | tf_op jit(solution)/shard_map/exchange/pallas_call | solution.py:762
  58.1 1.1 collective-permute-start.2
  59.2 2.5 %collective-permute-start.1 = (bf16[1024,256]{1,0:T(8,128)(2,1)}, bf16[1024,256]{1,0:T(8,128)(2,1)S(1)}, u32[]{:S(2)}, u32[]{:S(2)}) collective-permute-start(bf16[1024,256]{1,0:T(8,128)(2,1)} %get-tuple-element.22.w0_ref), channel_id=1, source_target_pairs={{0,4},{1,5},{2,6},{3,7},{4,0},{5,1},{6,2},{7,3},{8,12},{9,13},{10,... | collective-permute-start | bytes 1572872 | tf_op jit(solution)/shard_map/ppermute | solution.py:820
  61.8 0.0 collective-permute-start
  61.8 0.0 copy-start
  61.8 0.0 copy-start.1
  61.8 0.0 copy-start.2
  61.8 0.0 copy-start.4
  61.8 29.0 %attend.1.packed_ref = bf16[8,64,256]{2,1,0:T(8,128)(2,1)} custom-call(s32[1,128]{1,0:T(1,128)} %get-tuple-element.14.routes_hbm, s32[1,128]{1,0:T(1,128)} %get-tuple-element.15.local_hbm, s32[256]{0:T(256)} %counts_hbm.1, bf16[8,128,128]{2,1,0:T(8,128)(2,1)} %get-tuple-element.16.q_hbm, bf16[20,1024,128]{2,1,0:T(8,128)(2,1)} %bitcast.7, ...), custom_call_target="tpu_custom_call" | custom-call | flops 20000000000 | bytes 6000000 | tf_op jit(solution)/shard_map/attend/pallas_call | solution.py:265
  90.8 0.0 collective-permute-done.2.w3_ref
  90.8 0.0 collective-permute-done.1.w2_ref
  90.8 0.0 collective-permute-done.w1_ref
  90.8 0.0 copy-done
  90.8 0.0 copy-done.1
  90.8 0.0 copy-done.2
  90.9 0.0 copy-done.4
  90.9 0.0 copy-start.3
  90.9 0.9 copy-done.3
  91.8 29.9 %finish.1 = bf16[256,512]{1,0:T(8,128)(2,1)S(1)} custom-call(bf16[256,512]{1,0:T(8,128)(2,1)S(1)} %copy-done, bf16[8,64,256]{2,1,0:T(8,128)(2,1)S(1)} %copy-done.3, bf16[512,512]{1,0:T(8,128)(2,1)S(1)} %copy-done.1, f32[1,512]{1,0:T(1,128)S(1)} %bitcast.4, bf16[1024,256]{1,0:T(8,128)(2,1)S(1)} %copy-done.2, ...), custom_call_target="tpu_custom_call" | custom-call | tf_op jit(solution)/shard_map/finish/pallas_call | solution.py:414
  121.8 0.7 copy.14
Async XLA Ops:
  58.1 32.7 %collective-permute-start.2 = (bf16[1024,256]{1,0:T(8,128)(2,1)}, bf16[1024,256]{1,0:T(8,128)(2,1)S(1)}, u32[]{:S(2)}, u32[]{:S(2)}) collective-permute-start(bf16[1024,256]{1,0:T(8,128)(2,1)} %get-tuple-element.22.w0_ref), channel_id=1, source_target_pairs={{0,6},{1,7},{2,0},{3,1},{4,2},{5,3},{6,4},{7,5},{8,14},{9,15},{10,... | collective-permute-start | bytes 1572872 | tf_op jit(solution)/shard_map/ppermute | solution.py:820
  59.2 31.6 %collective-permute-start.1 = (bf16[1024,256]{1,0:T(8,128)(2,1)}, bf16[1024,256]{1,0:T(8,128)(2,1)S(1)}, u32[]{:S(2)}, u32[]{:S(2)}) collective-permute-start(bf16[1024,256]{1,0:T(8,128)(2,1)} %get-tuple-element.22.w0_ref), channel_id=1, source_target_pairs={{0,4},{1,5},{2,6},{3,7},{4,0},{5,1},{6,2},{7,3},{8,12},{9,13},{10,... | collective-permute-start | bytes 1572872 | tf_op jit(solution)/shard_map/ppermute | solution.py:820
  61.8 29.1 %collective-permute-start = (bf16[1024,256]{1,0:T(8,128)(2,1)}, bf16[1024,256]{1,0:T(8,128)(2,1)S(1)}, u32[]{:S(2)}, u32[]{:S(2)}) collective-permute-start(bf16[1024,256]{1,0:T(8,128)(2,1)} %get-tuple-element.22.w0_ref), channel_id=1, source_target_pairs={{0,2},{1,3},{2,4},{3,5},{4,6},{5,7},{6,0},{7,1},{8,10},{9,11},{10,... | collective-permute-start | bytes 1572872 | tf_op jit(solution)/shard_map/ppermute | solution.py:820
  61.8 29.1 %copy-start = (bf16[256,512]{1,0:T(8,128)(2,1)S(1)}, bf16[256,512]{1,0:T(8,128)(2,1)}, u32[]{:S(2)}) copy-start(bf16[256,512]{1,0:T(8,128)(2,1)} %points_ref.3) | copy-start | bytes 786436
  61.8 29.1 %copy-start.1 = (bf16[512,512]{1,0:T(8,128)(2,1)S(1)}, bf16[512,512]{1,0:T(8,128)(2,1)}, u32[]{:S(2)}) copy-start(bf16[512,512]{1,0:T(8,128)(2,1)} %w_out_ref.1) | copy-start | bytes 1572868
  61.8 29.1 %copy-start.2 = (bf16[1024,256]{1,0:T(8,128)(2,1)S(1)}, bf16[1024,256]{1,0:T(8,128)(2,1)}, u32[]{:S(2)}) copy-start(bf16[1024,256]{1,0:T(8,128)(2,1)} %get-tuple-element.22.w0_ref) | copy-start | bytes 1572868
  61.8 29.1 %copy-start.4 = (f32[512]{0:T(512)S(1)}, f32[512]{0:T(512)}, u32[]{:S(2)}) copy-start(f32[512]{0:T(512)} %param.16) | copy-start | bytes 6148
  90.9 1.0 copy-start.3

commit v7 on v6

--- a/solution.py
+++ b/solution.py
@@ -441,7 +441,7 @@
     points_ref, gain_ref, w_ref, scale_ref, place_ref, counts_ref, route_ref, local_ref, w1_ref, w2_ref,
     kv_out, q_out, route_out, local_out, own_out, own_top_out, own_size_out, own_query_out, weights_out,
     kv_ref, q_ref, raw, queries, keys, turned, lhs, scores, own, own_top, own_size, own_query,
-    all_send, all_recv, ring_send, ring_recv, pair_send, pair_recv, route_sem, local_sem, load_sem, own_sem, over_send, over_recv,
+    all_send, all_recv, ring_send, ring_recv, pair_send, pair_recv, route_sem, local_sem, load_sem, own_sem,
 ):
     column, plane, head = swap_ids()
     core = lax.rem(head, 2)
@@ -463,19 +463,17 @@
         return 0
 
     lax.fori_loop(0, 8, greet, 0)
-    over_right = (lax.rem(column + 1, 4) * 8 + plane, head)
-    over_left = (lax.rem(column + 3, 4) * 8 + plane, head)
-    for other in (right, left, pair, over_right, over_left):
+    for other in (right, left, pair):
         pl.semaphore_signal(barrier, inc=1, device_id=other, device_id_type=MESH)
 
     def enter():
         @pl.when(diagonal)
         def _():
-            pl.semaphore_wait(barrier, 12)
+            pl.semaphore_wait(barrier, 10)
 
         @pl.when(across)
         def _():
-            pl.semaphore_wait(barrier, 13)
+            pl.semaphore_wait(barrier, 11)
 
     def rows(half):
         return pl.ds(half * LANES, LANES)
@@ -684,35 +682,19 @@
 
         lax.fori_loop(begin, end, own_shard, 0)
 
-    def swapped(way):
-        if way == 0:
-            source, target, half, to = 8 + core, core, 1, over_right
-        else:
-            source, target, half, to = core, 8 + core, 0, over_left
-        return moved(source, target, half, over_send.at[way], over_recv.at[way], to)
-
-    own_run(0, 5)
-    hop(0, 0, 0).wait_recv()
-    hop(0, 1, 0).start()
-    hop(1, 0, 1).wait_recv()
-    hop(1, 1, 1).start()
-    shared(1, 0).start()
-    shared(3, 1).start()
-    hop(0, 0, 1).wait_recv()
-    shared(1, 1).start()
-    hop(1, 0, 0).wait_recv()
-    shared(3, 0).start()
-    own_run(5, 8)
-    hop(0, 1, 0).wait_recv()
-    swapped(1).start()
-    hop(1, 1, 1).wait_recv()
-    swapped(0).start()
-    shared(0, 0).start()
-    shared(4, 1).start()
-    swapped(0).wait_recv()
-    shared(0, 1).start()
-    swapped(1).wait_recv()
-    shared(4, 0).start()
+    for half in range(2):
+        hop(0, 0, half).wait_recv()
+        hop(0, 1, half).start()
+        hop(1, 0, half).wait_recv()
+        hop(1, 1, half).start()
+        shared(1, half).start()
+        shared(3, half).start()
+        own_run(4 * half, 4 * half + 4)
+    for half in range(2):
+        hop(0, 1, half).wait_recv()
+        shared(0, half).start()
+        hop(1, 1, half).wait_recv()
+        shared(4, half).start()
 
     def sent(group):
         @pl.when(across | (group != plane))
@@ -736,14 +718,11 @@
 
     for half in range(2):
         for way in range(2):
-            hop(way, 0, half).wait_send()
+            for step in range(2):
+                hop(way, step, half).wait_send()
         for place in range(5):
             shared(place, half).wait_send()
             taken(place, half).wait_recv()
-    hop(0, 1, 0).wait_send()
-    hop(1, 1, 1).wait_send()
-    swapped(0).wait_send()
-    swapped(1).wait_send()
     for join in joins:
         join.wait()
 
@@ -797,8 +776,6 @@
             pltpu.SemaphoreType.DMA((5,)),
             pltpu.SemaphoreType.DMA((5,)),
             pltpu.SemaphoreType.DMA((4, 8)),
-            pltpu.SemaphoreType.DMA((2,)),
-            pltpu.SemaphoreType.DMA((2,)),
         ],
         compiler_params=pltpu.CompilerParams(collective_id=0, has_side_effects=True, vmem_limit_bytes=60 << 20),
         name="exchange",

time: 124 us -> 115 us (0.927)
  Pallas kernels: 117 us -> 105 us
  starting transfers between devices: 3.67 us -> 6.01 us
    pallas_call x1, Pallas kernels: 58.1 us -> 48.6 us  [exchange(): pl.pallas_call(exchange_kernel, out_shape=(jax.ShapeDtypeStruct((10, GROU...]
    ppermute x3, starting transfers between devices: 3.67 us -> 6.01 us  [per_device(): weights.append(lax.ppermute(joined, 'head', pairs))]
    pallas_call x1, Pallas kernels: 29 us -> 27.4 us  [attend(): pl.pallas_call(attend_kernel, out_shape=jax.ShapeDtypeStruct((GROUPS, 64,...]
where the time goes in v7:
time: 115 us; the launch traced here: 113 us
  Pallas kernels  105 us (91%)
  starting transfers between devices  6.01 us (5%)
  local copies, waits for them, and re-layouts  1.67 us (1%)
    pallas_call x1, Pallas kernels, exchange(): pl.pallas_call(exchange_kernel, out_shape=(jax.ShapeDtypeStruct((10, GROU...  48.6 us
    pallas_call x1, Pallas kernels, finish(): pl.pallas_call(finish_kernel, out_shape=jax.ShapeDtypeStruct((TOK, D), BF...  28.8 us
    pallas_call x1, Pallas kernels, attend(): pl.pallas_call(attend_kernel, out_shape=jax.ShapeDtypeStruct((GROUPS, 64,...  27.4 us
    ppermute x3, starting transfers between devices, per_device(): weights.append(lax.ppermute(joined, 'head', pairs))  6.01 us
  transfers between devices with their start and end apart: 3, of which 0 were waited for; matrix products, arithmetic and copies ran while one was open for 0% of the time, Pallas kernels for 24%

profile of v7, /device:TPU:25, one launch (start us, length us, event | category | flops | bytes accessed | tf_op | source)
XLA Modules:
  0.0 112.6 jit_solution(10220092553249095438)
XLA Ops:
  0.0 48.6 %exchange.1 = (bf16[10,8,256,128]{3,2,1,0:T(8,128)(2,1)}, bf16[8,128,128]{2,1,0:T(8,128)(2,1)}, s32[1,128]{1,0:T(1,128)}, s32[1,128]{1,0:T(1,128)}, f32[8,128,25...) custom-call(bf16[256,512]{1,0:T(8,128)(2,1)} %points_ref.3, ...), custom_call_target="tpu_custom_call" | custom-call | tf_op jit(solution)/shard_map/exchange/pallas_call | solution.py:741
  48.6 1.3 %collective-permute-start.2 = (bf16[1024,256]{1,0:T(8,128)(2,1)}, bf16[1024,256]{1,0:T(8,128)(2,1)S(1)}, u32[]{:S(2)}, u32[]{:S(2)}) collective-permute-start(bf16[1024,256]{1,0:T(8,128)(2,1)} %get-tuple-element.22.w0_ref), channel_id=1, source_target_pairs={{0,6},{1,7},{2,0},{3,1},{4,2},{5,3},{6,4},{7,5},{8,14},{9,15},{10,... | collective-permute-start | bytes 1572872 | tf_op jit(solution)/shard_map/ppermute | solution.py:797
  49.9 4.7 %collective-permute-start.1 = (bf16[1024,256]{1,0:T(8,128)(2,1)}, bf16[1024,256]{1,0:T(8,128)(2,1)S(1)}, u32[]{:S(2)}, u32[]{:S(2)}) collective-permute-start(bf16[1024,256]{1,0:T(8,128)(2,1)} %get-tuple-element.22.w0_ref), channel_id=1, source_target_pairs={{0,4},{1,5},{2,6},{3,7},{4,0},{5,1},{6,2},{7,3},{8,12},{9,13},{10,... | collective-permute-start | bytes 1572872 | tf_op jit(solution)/shard_map/ppermute | solution.py:797
  54.6 0.0 collective-permute-start
  54.6 0.0 copy-start
  54.7 0.0 copy-start.1
  54.7 0.0 copy-start.2
  54.7 0.0 copy-start.4
  54.7 27.4 %attend.1.packed_ref = bf16[8,64,256]{2,1,0:T(8,128)(2,1)} custom-call(s32[1,128]{1,0:T(1,128)} %get-tuple-element.14.routes_hbm, s32[1,128]{1,0:T(1,128)} %get-tuple-element.15.local_hbm, s32[256]{0:T(256)} %counts_hbm.1, bf16[8,128,128]{2,1,0:T(8,128)(2,1)} %get-tuple-element.16.q_hbm, bf16[20,1024,128]{2,1,0:T(8,128)(2,1)} %bitcast.7, ...), custom_call_target="tpu_custom_call" | custom-call | flops 20000000000 | bytes 6000000 | tf_op jit(solution)/shard_map/attend/pallas_call | solution.py:265
  82.1 0.0 collective-permute-done.2.w3_ref
  82.1 0.0 collective-permute-done.1.w2_ref
  82.1 0.0 collective-permute-done.w1_ref
  82.1 0.0 copy-done
  82.1 0.0 copy-done.1
  82.1 0.0 copy-done.2
  82.1 0.0 copy-done.4
  82.1 0.0 copy-start.3
  82.1 0.9 copy-done.3
  83.1 28.8 %finish.1 = bf16[256,512]{1,0:T(8,128)(2,1)S(1)} custom-call(bf16[256,512]{1,0:T(8,128)(2,1)S(1)} %copy-done, bf16[8,64,256]{2,1,0:T(8,128)(2,1)S(1)} %copy-done.3, bf16[512,512]{1,0:T(8,128)(2,1)S(1)} %copy-done.1, f32[1,512]{1,0:T(1,128)S(1)} %bitcast.4, bf16[1024,256]{1,0:T(8,128)(2,1)S(1)} %copy-done.2, ...), custom_call_target="tpu_custom_call" | custom-call | tf_op jit(solution)/shard_map/finish/pallas_call | solution.py:414
  111.9 0.7 copy.14
Async XLA Ops:
  48.6 33.4 %collective-permute-start.2 = (bf16[1024,256]{1,0:T(8,128)(2,1)}, bf16[1024,256]{1,0:T(8,128)(2,1)S(1)}, u32[]{:S(2)}, u32[]{:S(2)}) collective-permute-start(bf16[1024,256]{1,0:T(8,128)(2,1)} %get-tuple-element.22.w0_ref), channel_id=1, source_target_pairs={{0,6},{1,7},{2,0},{3,1},{4,2},{5,3},{6,4},{7,5},{8,14},{9,15},{10,... | collective-permute-start | bytes 1572872 | tf_op jit(solution)/shard_map/ppermute | solution.py:797
  49.9 32.1 %collective-permute-start.1 = (bf16[1024,256]{1,0:T(8,128)(2,1)}, bf16[1024,256]{1,0:T(8,128)(2,1)S(1)}, u32[]{:S(2)}, u32[]{:S(2)}) collective-permute-start(bf16[1024,256]{1,0:T(8,128)(2,1)} %get-tuple-element.22.w0_ref), channel_id=1, source_target_pairs={{0,4},{1,5},{2,6},{3,7},{4,0},{5,1},{6,2},{7,3},{8,12},{9,13},{10,... | collective-permute-start | bytes 1572872 | tf_op jit(solution)/shard_map/ppermute | solution.py:797
  54.6 27.4 %collective-permute-start = (bf16[1024,256]{1,0:T(8,128)(2,1)}, bf16[1024,256]{1,0:T(8,128)(2,1)S(1)}, u32[]{:S(2)}, u32[]{:S(2)}) collective-permute-start(bf16[1024,256]{1,0:T(8,128)(2,1)} %get-tuple-element.22.w0_ref), channel_id=1, source_target_pairs={{0,2},{1,3},{2,4},{3,5},{4,6},{5,7},{6,0},{7,1},{8,10},{9,11},{10,... | collective-permute-start | bytes 1572872 | tf_op jit(solution)/shard_map/ppermute | solution.py:797
  54.6 27.4 %copy-start = (bf16[256,512]{1,0:T(8,128)(2,1)S(1)}, bf16[256,512]{1,0:T(8,128)(2,1)}, u32[]{:S(2)}) copy-start(bf16[256,512]{1,0:T(8,128)(2,1)} %points_ref.3) | copy-start | bytes 786436
  54.7 27.4 %copy-start.1 = (bf16[512,512]{1,0:T(8,128)(2,1)S(1)}, bf16[512,512]{1,0:T(8,128)(2,1)}, u32[]{:S(2)}) copy-start(bf16[512,512]{1,0:T(8,128)(2,1)} %w_out_ref.1) | copy-start | bytes 1572868
  54.7 27.5 %copy-start.2 = (bf16[1024,256]{1,0:T(8,128)(2,1)S(1)}, bf16[1024,256]{1,0:T(8,128)(2,1)}, u32[]{:S(2)}) copy-start(bf16[1024,256]{1,0:T(8,128)(2,1)} %get-tuple-element.22.w0_ref) | copy-start | bytes 1572868
  54.7 27.5 %copy-start.4 = (f32[512]{0:T(512)S(1)}, f32[512]{0:T(512)}, u32[]{:S(2)}) copy-start(f32[512]{0:T(512)} %param.16) | copy-start | bytes 6148
  82.1 1.0 copy-start.3

commit v8 on v7

--- a/solution.py
+++ b/solution.py
@@ -304,21 +304,22 @@
 
 def finish_kernel(
     points_ref, packed_ref, w_out_ref, gain_ref, w0_ref, w1_ref, w2_ref, w3_ref, out_ref,
-    points, w_out, gain, slabs, back, send, recv, local_sem, load_sem, weight_sem, pair_send, pair_recv,
+    points, w_out, gain, slabs, mid, back, send, recv, local_sem, load_sem, weight_sem, pair_send, pair_recv,
 ):
     column, plane, head = swap_ids()
-    diagonal = plane == head
-    across = jnp.logical_not(diagonal)
     barrier = pltpu.get_barrier_semaphore()
 
-    def greet(group):
-        @pl.when(across | (group != plane))
-        def _():
-            pl.semaphore_signal(barrier, inc=1, device_id=(column * 8 + group, plane), device_id_type=MESH)
+    def greet(index):
+        @pl.when(index != head)
+        def _():
+            pl.semaphore_signal(barrier, inc=1, device_id=(column * 8 + plane, index), device_id_type=MESH)
+
+        @pl.when(index != plane)
+        def _():
+            pl.semaphore_signal(barrier, inc=1, device_id=(column * 8 + index, head), device_id_type=MESH)
 
     each(greet)
     pair = (column * 8 + plane, head + 1 - 2 * lax.rem(head, 2))
-    pl.semaphore_signal(barrier, inc=1, device_id=pair, device_id_type=MESH)
     loads = [
         pltpu.make_async_copy(points_ref, points, load_sem.at[0]),
         pltpu.make_async_copy(w_out_ref, w_out, load_sem.at[1]),
@@ -339,44 +340,68 @@
     for load in own:
         load.start()
 
-    @pl.when(diagonal)
-    def _():
-        pl.semaphore_wait(barrier, 8)
-
-    @pl.when(across)
-    def _():
-        pl.semaphore_wait(barrier, 9)
-
-    def copy(shard, group):
+    pl.semaphore_wait(barrier, 14)
+
+    def level_leg(shard, slot):
         return pltpu.make_async_remote_copy(
-            src_ref=packed_ref.at[shard], dst_ref=back.at[group],
-            send_sem=send.at[shard], recv_sem=recv.at[group],
-            device_id=(column * 8 + head, shard), device_id_type=MESH,
-        )
-
-    at_home = pltpu.make_async_copy(packed_ref.at[head], back.at[plane], local_sem.at[0])
-
-    def start(shard):
-        @pl.when(across | (shard != head))
-        def _():
-            copy(shard, plane).start()
+            src_ref=packed_ref.at[shard], dst_ref=mid.at[slot],
+            send_sem=send.at[0, shard], recv_sem=recv.at[0, slot],
+            device_id=(column * 8 + plane, shard), device_id_type=MESH,
+        )
+
+    def plane_leg(home, slot):
+        return pltpu.make_async_remote_copy(
+            src_ref=mid.at[home], dst_ref=back.at[slot],
+            send_sem=send.at[1, home], recv_sem=recv.at[1, slot],
+            device_id=(column * 8 + home, head), device_id_type=MESH,
+        )
+
+    level_stay = pltpu.make_async_copy(packed_ref.at[head], mid.at[head], local_sem.at[0])
+    plane_stay = pltpu.make_async_copy(mid.at[plane], back.at[plane], local_sem.at[1])
+    level_stay.start()
+
+    def start(step):
+        shard = lax.rem(head + step, 8)
+
+        @pl.when(shard != head)
+        def _():
+            level_leg(shard, head).start()
 
     each(start)
+
+    def forward(step):
+        home = lax.rem(plane + step, 8)
+
+        @pl.when(home == head)
+        def _():
+            level_stay.wait()
+
+        @pl.when(home != head)
+        def _():
+            level_leg(0, home).wait_recv()
+
+        @pl.when(home == plane)
+        def _():
+            plane_stay.start()
+
+        @pl.when(home != plane)
+        def _():
+            plane_leg(home, plane).start()
+
+    each(forward)
     for load in lent:
         load.start()
-
-    @pl.when(diagonal)
-    def _():
-        at_home.start()
-        at_home.wait()
-
     for load in loads:
         load.wait()
 
-    def wait(index):
-        @pl.when(across | (index != plane))
-        def _():
-            copy(0, index).wait_recv()
+    def wait(group):
+        @pl.when(group == plane)
+        def _():
+            plane_stay.wait()
+
+        @pl.when(group != plane)
+        def _():
+            plane_leg(0, group).wait_recv()
 
     each(wait)
 
@@ -400,9 +425,13 @@
     out_ref[:, 256:] = high.astype(BF16)
 
     def sent(index):
-        @pl.when(across | (index != head))
-        def _():
-            copy(index, plane).wait_send()
+        @pl.when(index != head)
+        def _():
+            level_leg(index, head).wait_send()
+
+        @pl.when(index != plane)
+        def _():
+            plane_leg(index, plane).wait_send()
 
     each(sent)
     for load in lent:
@@ -422,9 +451,10 @@
             pltpu.VMEM((1, D), F32),
             pltpu.VMEM((GROUPS, 2 * D, 256), BF16),
             pltpu.VMEM((GROUPS, 64, TOK), BF16),
-            pltpu.SemaphoreType.DMA((8,)),
-            pltpu.SemaphoreType.DMA((8,)),
-            pltpu.SemaphoreType.DMA((1,)),
+            pltpu.VMEM((GROUPS, 64, TOK), BF16),
+            pltpu.SemaphoreType.DMA((2, 8)),
+            pltpu.SemaphoreType.DMA((2, 8)),
+            pltpu.SemaphoreType.DMA((2,)),
             pltpu.SemaphoreType.DMA((3,)),
             pltpu.SemaphoreType.DMA((4,)),
             pltpu.SemaphoreType.DMA((4,)),

time: 115 us -> 116 us (level)
  the two profiles are of different devices: /device:TPU:25 before, /device:TPU:1 now
where the time goes in v8:
time: 116 us
  Pallas kernels  112 us (97%)
  local copies, waits for them, and re-layouts  1.67 us (1%)
  starting transfers between devices  1.53 us (1%)
    pallas_call x1, Pallas kernels, exchange(): pl.pallas_call(exchange_kernel, out_shape=(jax.ShapeDtypeStruct((10, GROU...  54.3 us
    pallas_call x1, Pallas kernels, finish(): pl.pallas_call(finish_kernel, out_shape=jax.ShapeDtypeStruct((TOK, D), BF...  29.2 us
    pallas_call x1, Pallas kernels, attend(): pl.pallas_call(attend_kernel, out_shape=jax.ShapeDtypeStruct((GROUPS, 64,...  29 us
  transfers between devices with their start and end apart: 3, of which 0 were waited for; matrix products, arithmetic and copies ran while one was open for 0% of the time, Pallas kernels for 25%

profile of v8, /device:TPU:1, one launch (start us, length us, event | category | flops | bytes accessed | tf_op | source)
XLA Modules:
  0.0 115.8 jit_solution(466373597562636607)
XLA Ops:
  0.0 54.3 %exchange.1 = (bf16[10,8,256,128]{3,2,1,0:T(8,128)(2,1)}, bf16[8,128,128]{2,1,0:T(8,128)(2,1)}, s32[1,128]{1,0:T(1,128)}, s32[1,128]{1,0:T(1,128)}, f32[8,128,25...) custom-call(bf16[256,512]{1,0:T(8,128)(2,1)} %points_ref.3, ...), custom_call_target="tpu_custom_call" | custom-call | tf_op jit(solution)/shard_map/exchange/pallas_call | solution.py:771
  54.3 0.1 collective-permute-start.2
  54.4 0.1 collective-permute-start.1
  54.5 1.4 %collective-permute-start = (bf16[1024,256]{1,0:T(8,128)(2,1)}, bf16[1024,256]{1,0:T(8,128)(2,1)S(1)}, u32[]{:S(2)}, u32[]{:S(2)}) collective-permute-start(bf16[1024,256]{1,0:T(8,128)(2,1)} %get-tuple-element.22.w0_ref), channel_id=1, source_target_pairs={{0,2},{1,3},{2,4},{3,5},{4,6},{5,7},{6,0},{7,1},{8,10},{9,11},{10,... | collective-permute-start | bytes 1572872 | tf_op jit(solution)/shard_map/ppermute | solution.py:827
  55.8 0.0 copy-start
  55.8 0.0 copy-start.1
  55.8 0.0 copy-start.2
  55.8 0.0 copy-start.4
  55.8 29.0 %attend.1.packed_ref = bf16[8,64,256]{2,1,0:T(8,128)(2,1)} custom-call(s32[1,128]{1,0:T(1,128)} %get-tuple-element.14.routes_hbm, s32[1,128]{1,0:T(1,128)} %get-tuple-element.15.local_hbm, s32[256]{0:T(256)} %counts_hbm.1, bf16[8,128,128]{2,1,0:T(8,128)(2,1)} %get-tuple-element.16.q_hbm, bf16[20,1024,128]{2,1,0:T(8,128)(2,1)} %bitcast.7, ...), custom_call_target="tpu_custom_call" | custom-call | flops 20000000000 | bytes 6000000 | tf_op jit(solution)/shard_map/attend/pallas_call | solution.py:265
  84.8 0.0 collective-permute-done.2.w3_ref
  84.9 0.0 collective-permute-done.1.w2_ref
  84.9 0.0 collective-permute-done.w1_ref
  84.9 0.0 copy-done
  84.9 0.0 copy-done.1
  84.9 0.0 copy-done.2
  84.9 0.0 copy-done.4
  84.9 0.0 copy-start.3
  84.9 0.9 copy-done.3
  85.9 29.2 %finish.1 = bf16[256,512]{1,0:T(8,128)(2,1)S(1)} custom-call(bf16[256,512]{1,0:T(8,128)(2,1)S(1)} %copy-done, bf16[8,64,256]{2,1,0:T(8,128)(2,1)S(1)} %copy-done.3, bf16[512,512]{1,0:T(8,128)(2,1)S(1)} %copy-done.1, f32[1,512]{1,0:T(1,128)S(1)} %bitcast.4, bf16[1024,256]{1,0:T(8,128)(2,1)S(1)} %copy-done.2, ...), custom_call_target="tpu_custom_call" | custom-call | tf_op jit(solution)/shard_map/finish/pallas_call | solution.py:443
  115.0 0.7 copy.14
Async XLA Ops:
  54.3 30.6 %collective-permute-start.2 = (bf16[1024,256]{1,0:T(8,128)(2,1)}, bf16[1024,256]{1,0:T(8,128)(2,1)S(1)}, u32[]{:S(2)}, u32[]{:S(2)}) collective-permute-start(bf16[1024,256]{1,0:T(8,128)(2,1)} %get-tuple-element.22.w0_ref), channel_id=1, source_target_pairs={{0,6},{1,7},{2,0},{3,1},{4,2},{5,3},{6,4},{7,5},{8,14},{9,15},{10,... | collective-permute-start | bytes 1572872 | tf_op jit(solution)/shard_map/ppermute | solution.py:827
  54.4 30.5 %collective-permute-start.1 = (bf16[1024,256]{1,0:T(8,128)(2,1)}, bf16[1024,256]{1,0:T(8,128)(2,1)S(1)}, u32[]{:S(2)}, u32[]{:S(2)}) collective-permute-start(bf16[1024,256]{1,0:T(8,128)(2,1)} %get-tuple-element.22.w0_ref), channel_id=1, source_target_pairs={{0,4},{1,5},{2,6},{3,7},{4,0},{5,1},{6,2},{7,3},{8,12},{9,13},{10,... | collective-permute-start | bytes 1572872 | tf_op jit(solution)/shard_map/ppermute | solution.py:827
  54.5 30.4 %collective-permute-start = (bf16[1024,256]{1,0:T(8,128)(2,1)}, bf16[1024,256]{1,0:T(8,128)(2,1)S(1)}, u32[]{:S(2)}, u32[]{:S(2)}) collective-permute-start(bf16[1024,256]{1,0:T(8,128)(2,1)} %get-tuple-element.22.w0_ref), channel_id=1, source_target_pairs={{0,2},{1,3},{2,4},{3,5},{4,6},{5,7},{6,0},{7,1},{8,10},{9,11},{10,... | collective-permute-start | bytes 1572872 | tf_op jit(solution)/shard_map/ppermute | solution.py:827
  55.8 29.1 %copy-start = (bf16[256,512]{1,0:T(8,128)(2,1)S(1)}, bf16[256,512]{1,0:T(8,128)(2,1)}, u32[]{:S(2)}) copy-start(bf16[256,512]{1,0:T(8,128)(2,1)} %points_ref.3) | copy-start | bytes 786436
  55.8 29.1 %copy-start.1 = (bf16[512,512]{1,0:T(8,128)(2,1)S(1)}, bf16[512,512]{1,0:T(8,128)(2,1)}, u32[]{:S(2)}) copy-start(bf16[512,512]{1,0:T(8,128)(2,1)} %w_out_ref.1) | copy-start | bytes 1572868
  55.8 29.1 %copy-start.2 = (bf16[1024,256]{1,0:T(8,128)(2,1)S(1)}, bf16[1024,256]{1,0:T(8,128)(2,1)}, u32[]{:S(2)}) copy-start(bf16[1024,256]{1,0:T(8,128)(2,1)} %get-tuple-element.22.w0_ref) | copy-start | bytes 1572868
  55.8 29.1 %copy-start.4 = (f32[512]{0:T(512)S(1)}, f32[512]{0:T(512)}, u32[]{:S(2)}) copy-start(f32[512]{0:T(512)} %param.16) | copy-start | bytes 6148
  84.9 1.0 copy-start.3

commit v9 on v8

--- a/solution.py
+++ b/solution.py
@@ -361,7 +361,7 @@
     level_stay.start()
 
     def start(step):
-        shard = lax.rem(head + step, 8)
+        shard = step
 
         @pl.when(shard != head)
         def _():
@@ -370,7 +370,7 @@
     each(start)
 
     def forward(step):
-        home = lax.rem(plane + step, 8)
+        home = step
 
         @pl.when(home == head)
         def _():
@@ -461,7 +461,7 @@
             pltpu.SemaphoreType.DMA((4,)),
         ],
         compiler_params=pltpu.CompilerParams(
-            collective_id=1, has_side_effects=True, vmem_limit_bytes=40 << 20
+            collective_id=1, has_side_effects=True, vmem_limit_bytes=60 << 20
         ),
         name="finish",
     )(points, packed, w_out, gain.reshape(1, D), *weights)
@@ -469,9 +469,9 @@
 
 def exchange_kernel(
     points_ref, gain_ref, w_ref, scale_ref, place_ref, counts_ref, route_ref, local_ref, w1_ref, w2_ref,
-    kv_out, q_out, route_out, local_out, own_out, own_top_out, own_size_out, own_query_out, weights_out,
+    kv_out, q_out, route_out, local_out, own_out, own_top_out, own_size_out, own_query_out, weights_out, weights_below, weights_above,
     kv_ref, q_ref, raw, queries, keys, turned, lhs, scores, own, own_top, own_size, own_query,
-    all_send, all_recv, ring_send, ring_recv, pair_send, pair_recv, route_sem, local_sem, load_sem, own_sem,
+    all_send, all_recv, ring_send, ring_recv, pair_send, pair_recv, route_sem, local_sem, load_sem, own_sem, near_send, near_recv,
 ):
     column, plane, head = swap_ids()
     core = lax.rem(head, 2)
@@ -493,17 +493,20 @@
         return 0
 
     lax.fori_loop(0, 8, greet, 0)
-    for other in (right, left, pair):
+    level = head // 2
+    above = (column * 8 + plane, lax.rem(level + 1, 4) * 2 + core)
+    below = (column * 8 + plane, lax.rem(level + 3, 4) * 2 + core)
+    for other in (right, left, pair, above, below):
         pl.semaphore_signal(barrier, inc=1, device_id=other, device_id_type=MESH)
 
     def enter():
         @pl.when(diagonal)
         def _():
-            pl.semaphore_wait(barrier, 10)
+            pl.semaphore_wait(barrier, 12)
 
         @pl.when(across)
         def _():
-            pl.semaphore_wait(barrier, 11)
+            pl.semaphore_wait(barrier, 13)
 
     def rows(half):
         return pl.ds(half * LANES, LANES)
@@ -567,11 +570,20 @@
         def _():
             spread_q(group, head).start()
 
+    parts = (
+        (w1_ref, pl.ds(0, D)), (w2_ref.at[:, pl.ds(0, 256)], pl.ds(D, 256)), (w2_ref.at[:, pl.ds(256, 256)], pl.ds(D + 256, 256)),
+    )
     joins = [
         pltpu.make_async_copy(source, weights_out.at[rows_at], load_sem.at[2 + index])
-        for index, (source, rows_at) in enumerate((
-            (w1_ref, pl.ds(0, D)), (w2_ref.at[:, pl.ds(0, 256)], pl.ds(D, 256)), (w2_ref.at[:, pl.ds(256, 256)], pl.ds(D + 256, 256)),
-        ))
+        for index, (source, rows_at) in enumerate(parts)
+    ]
+    nears = [
+        pltpu.make_async_remote_copy(
+            src_ref=source, dst_ref=target.at[rows_at], send_sem=near_send.at[way, index],
+            recv_sem=near_recv.at[way, index], device_id=to, device_id_type=MESH,
+        )
+        for way, (target, to) in enumerate(((weights_below, above), (weights_above, below)))
+        for index, (source, rows_at) in enumerate(parts)
     ]
     for join in joins:
         join.start()
@@ -592,6 +604,8 @@
         start(2 * couple)
         start(2 * couple + 1)
     each(start_q)
+    for near in nears:
+        near.start()
 
     @pl.when(diagonal)
     def _():
@@ -753,8 +767,8 @@
         for place in range(5):
             shared(place, half).wait_send()
             taken(place, half).wait_recv()
-    for join in joins:
-        join.wait()
+    for copy in (*joins, *nears):
+        copy.wait()
 
     def saved(shard):
         for save in own_saved(shard):
@@ -780,9 +794,11 @@
             jax.ShapeDtypeStruct((GROUPS, 1, ROWS), F32),
             jax.ShapeDtypeStruct((GROUPS, 1, LANES), F32),
             jax.ShapeDtypeStruct((2 * D, 256), BF16),
+            jax.ShapeDtypeStruct((2 * D, 256), BF16),
+            jax.ShapeDtypeStruct((2 * D, 256), BF16),
         ),
         in_specs=[vmem] * 5 + [pl.BlockSpec(memory_space=pltpu.SMEM)] + [anywhere] * 4,
-        out_specs=(anywhere,) * 9,
+        out_specs=(anywhere,) * 11,
         scratch_shapes=[
             pltpu.VMEM((GROUPS, TOK, LANES), BF16),
             pltpu.VMEM((GROUPS, LANES, LANES), BF16),
@@ -806,6 +822,8 @@
             pltpu.SemaphoreType.DMA((5,)),
             pltpu.SemaphoreType.DMA((5,)),
             pltpu.SemaphoreType.DMA((4, 8)),
+            pltpu.SemaphoreType.DMA((2, 3)),
+            pltpu.SemaphoreType.DMA((2, 3)),
         ],
         compiler_params=pltpu.CompilerParams(collective_id=0, has_side_effects=True, vmem_limit_bytes=60 << 20),
         name="exchange",
@@ -818,13 +836,11 @@
 def per_device(
     points, gain_attn, w_qkv, w_out, gain_mlp, w_fc1, w_fc2, contact_route, contact_patch, counts
 ):
-    slots, q, routes, local, sums, tops, sizes, tallest, joined = exchange(
+    slots, q, routes, local, sums, tops, sizes, tallest, joined, low, high = exchange(
         points, gain_attn, w_qkv, counts, contact_route.reshape(1, -1), contact_patch, w_fc1, w_fc2
     )
-    weights = [joined]
-    for step in range(1, 4):
-        pairs = [(head, (head + 2 * step) % GROUPS) for head in range(GROUPS)]
-        weights.append(lax.ppermute(joined, "head", pairs))
+    far = lax.ppermute(joined, "head", [(head, (head + 4) % GROUPS) for head in range(GROUPS)])
+    weights = [joined, low, high, far]
     packed = attend(routes, local, counts, q, slots.reshape(20, PATCH, LANES), sums, tops, sizes, tallest)
     return finish(points, packed, w_out, gain_mlp, weights)
 

time: 116 us -> 113 us (0.974)
  the two profiles are of different devices: /device:TPU:1 before, /device:TPU:54 now
where the time goes in v9:
time: 113 us
  Pallas kernels  110 us (97%)
  local copies, waits for them, and re-layouts  2.46 us (2%)
    pallas_call x1, Pallas kernels, exchange(): pl.pallas_call(exchange_kernel, out_shape=(jax.ShapeDtypeStruct((10, GROU...  56.3 us
    pallas_call x1, Pallas kernels, finish(): pl.pallas_call(finish_kernel, out_shape=jax.ShapeDtypeStruct((TOK, D), BF...  34.3 us
    pallas_call x1, Pallas kernels, attend(): pl.pallas_call(attend_kernel, out_shape=jax.ShapeDtypeStruct((GROUPS, 64,...  19.8 us
    unnamed x3, local copies, waits for them, and re-layouts  2.46 us
  transfers between devices with their start and end apart: 1, of which 0 were waited for; matrix products, arithmetic and copies ran while one was open for 0% of the time, Pallas kernels for 17%

profile of v9, /device:TPU:54, one launch (start us, length us, event | category | flops | bytes accessed | tf_op | source)
XLA Modules:
  0.0 113.2 jit_solution(13835928205052579211)
XLA Ops:
  0.0 56.3 %exchange.1 = (bf16[10,8,256,128]{3,2,1,0:T(8,128)(2,1)}, bf16[8,128,128]{2,1,0:T(8,128)(2,1)}, s32[1,128]{1,0:T(1,128)}, s32[1,128]{1,0:T(1,128)}, f32[8,128,25...) custom-call(bf16[256,512]{1,0:T(8,128)(2,1)} %points_ref.3, ...), custom_call_target="tpu_custom_call" | custom-call | tf_op jit(solution)/shard_map/exchange/pallas_call | solution.py:785
  56.3 0.3 collective-permute-start
  56.6 19.8 %attend.1.packed_ref = bf16[8,64,256]{2,1,0:T(8,128)(2,1)} custom-call(s32[1,128]{1,0:T(1,128)} %get-tuple-element.16.routes_hbm, s32[1,128]{1,0:T(1,128)} %get-tuple-element.17.local_hbm, s32[256]{0:T(256)} %counts_hbm.1, bf16[8,128,128]{2,1,0:T(8,128)(2,1)} %get-tuple-element.18.q_hbm, bf16[20,1024,128]{2,1,0:T(8,128)(2,1)} %bitcast.7, ...), custom_call_target="tpu_custom_call" | custom-call | flops 20000000000 | bytes 6000000 | tf_op jit(solution)/shard_map/attend/pallas_call | solution.py:265
  76.4 0.0 collective-permute-done.w3_ref
  76.4 0.0 copy-start
  76.4 0.8 copy-done
  77.2 34.3 %finish.1 = bf16[256,512]{1,0:T(8,128)(2,1)} custom-call(bf16[256,512]{1,0:T(8,128)(2,1)} %points_ref.3, bf16[8,64,256]{2,1,0:T(8,128)(2,1)} %attend.1.packed_ref, bf16[512,512]{1,0:T(8,128)(2,1)} %w_out_ref.1, f32[1,512]{1,0:T(1,128)} %bitcast.5, bf16[1024,256]{1,0:T(8,128)(2,1)} %get-tuple-element.24.w0_ref, bf16[1024,256]{1,0:T(8,128)(2,1)} %get-tuple-element.25.w1_ref, ...), custom_call_target="tpu_custom_call" | custom-call | tf_op jit(solution)/shard_map/finish/pallas_call | solution.py:443
  111.5 1.7 %copy.14 = bf16[256,512]{1,0:T(8,128)(2,1)} copy(bf16[256,512]{1,0:T(8,128)(2,1)} %finish.1) | data formatting | bytes 524288
Async XLA Ops:
  56.3 20.1 %collective-permute-start = (bf16[1024,256]{1,0:T(8,128)(2,1)}, bf16[1024,256]{1,0:T(8,128)(2,1)S(1)}, u32[]{:S(2)}, u32[]{:S(2)}) collective-permute-start(bf16[1024,256]{1,0:T(8,128)(2,1)} %get-tuple-element.24.w0_ref), channel_id=1, source_target_pairs={{0,4},{1,5},{2,6},{3,7},{4,0},{5,1},{6,2},{7,3},{8,12},{9,13},{10,... | collective-permute-start | bytes 1572872 | tf_op jit(solution)/shard_map/ppermute | solution.py:842
  76.4 0.8 copy-start

commit v10 on v9

--- a/solution.py
+++ b/solution.py
@@ -461,7 +461,7 @@
             pltpu.SemaphoreType.DMA((4,)),
         ],
         compiler_params=pltpu.CompilerParams(
-            collective_id=1, has_side_effects=True, vmem_limit_bytes=60 << 20
+            collective_id=1, has_side_effects=True, vmem_limit_bytes=50 << 20
         ),
         name="finish",
     )(points, packed, w_out, gain.reshape(1, D), *weights)

time: 113 us -> 112 us (level)
  the two profiles are of different devices: /device:TPU:54 before, /device:TPU:85 now
where the time goes in v10:
time: 112 us; the launch traced here: 111 us
  Pallas kernels  109 us (97%)
  local copies, waits for them, and re-layouts  1.68 us (2%)
    pallas_call x1, Pallas kernels, exchange(): pl.pallas_call(exchange_kernel, out_shape=(jax.ShapeDtypeStruct((10, GROU...  56.6 us
    pallas_call x1, Pallas kernels, finish(): pl.pallas_call(finish_kernel, out_shape=jax.ShapeDtypeStruct((TOK, D), BF...  33.4 us
    pallas_call x1, Pallas kernels, attend(): pl.pallas_call(attend_kernel, out_shape=jax.ShapeDtypeStruct((GROUPS, 64,...  19.1 us
  transfers between devices with their start and end apart: 1, of which 0 were waited for; matrix products, arithmetic and copies ran while one was open for 0% of the time, Pallas kernels for 17%

profile of v10, /device:TPU:85, one launch (start us, length us, event | category | flops | bytes accessed | tf_op | source)
XLA Modules:
  0.0 111.2 jit_solution(461936547174935677)
XLA Ops:
  0.0 56.6 %exchange.1 = (bf16[10,8,256,128]{3,2,1,0:T(8,128)(2,1)}, bf16[8,128,128]{2,1,0:T(8,128)(2,1)}, s32[1,128]{1,0:T(1,128)}, s32[1,128]{1,0:T(1,128)}, f32[8,128,25...) custom-call(bf16[256,512]{1,0:T(8,128)(2,1)} %points_ref.3, ...), custom_call_target="tpu_custom_call" | custom-call | tf_op jit(solution)/shard_map/exchange/pallas_call | solution.py:785
  56.6 0.3 collective-permute-start
  56.9 0.0 copy-start
  56.9 0.0 copy-start.1
  56.9 0.0 copy-start.2
  56.9 0.0 copy-start.3
  56.9 0.0 copy-start.4
  56.9 0.0 copy-start.6
  57.0 19.1 %attend.1.packed_ref = bf16[8,64,256]{2,1,0:T(8,128)(2,1)} custom-call(s32[1,128]{1,0:T(1,128)} %get-tuple-element.16.routes_hbm, s32[1,128]{1,0:T(1,128)} %get-tuple-element.17.local_hbm, s32[256]{0:T(256)} %counts_hbm.1, bf16[8,128,128]{2,1,0:T(8,128)(2,1)} %get-tuple-element.18.q_hbm, bf16[20,1024,128]{2,1,0:T(8,128)(2,1)} %bitcast.7, ...), custom_call_target="tpu_custom_call" | custom-call | flops 20000000000 | bytes 6000000 | tf_op jit(solution)/shard_map/attend/pallas_call | solution.py:265
  76.1 0.0 collective-permute-done.w3_ref
  76.1 0.0 copy-done
  76.1 0.0 copy-done.1
  76.1 0.0 copy-done.2
  76.1 0.0 copy-done.3
  76.1 0.0 copy-done.4
  76.1 0.0 copy-done.6
  76.2 0.0 copy-start.5
  76.2 0.9 copy-done.5
  77.1 33.4 %finish.1 = bf16[256,512]{1,0:T(8,128)(2,1)S(1)} custom-call(bf16[256,512]{1,0:T(8,128)(2,1)S(1)} %copy-done, bf16[8,64,256]{2,1,0:T(8,128)(2,1)S(1)} %copy-done.5, bf16[512,512]{1,0:T(8,128)(2,1)S(1)} %copy-done.1, f32[1,512]{1,0:T(1,128)S(1)} %bitcast.4, bf16[1024,256]{1,0:T(8,128)(2,1)S(1)} %copy-done.2, bf16[1024,256]{1,0:T(8,128)(2,1)S(1)} %copy-done.3, ...), custom_call_target="tpu_custom_call" | custom-call | tf_op jit(solution)/shard_map/finish/pallas_call | solution.py:443
  110.5 0.7 copy.14
Async XLA Ops:
  56.6 19.5 %collective-permute-start = (bf16[1024,256]{1,0:T(8,128)(2,1)}, bf16[1024,256]{1,0:T(8,128)(2,1)S(1)}, u32[]{:S(2)}, u32[]{:S(2)}) collective-permute-start(bf16[1024,256]{1,0:T(8,128)(2,1)} %get-tuple-element.24.w0_ref), channel_id=1, source_target_pairs={{0,4},{1,5},{2,6},{3,7},{4,0},{5,1},{6,2},{7,3},{8,12},{9,13},{10,... | collective-permute-start | bytes 1572872 | tf_op jit(solution)/shard_map/ppermute | solution.py:842
  56.9 19.2 %copy-start = (bf16[256,512]{1,0:T(8,128)(2,1)S(1)}, bf16[256,512]{1,0:T(8,128)(2,1)}, u32[]{:S(2)}) copy-start(bf16[256,512]{1,0:T(8,128)(2,1)} %points_ref.3) | copy-start | bytes 786436
  56.9 19.2 %copy-start.1 = (bf16[512,512]{1,0:T(8,128)(2,1)S(1)}, bf16[512,512]{1,0:T(8,128)(2,1)}, u32[]{:S(2)}) copy-start(bf16[512,512]{1,0:T(8,128)(2,1)} %w_out_ref.1) | copy-start | bytes 1572868
  56.9 19.2 %copy-start.2 = (bf16[1024,256]{1,0:T(8,128)(2,1)S(1)}, bf16[1024,256]{1,0:T(8,128)(2,1)}, u32[]{:S(2)}) copy-start(bf16[1024,256]{1,0:T(8,128)(2,1)} %get-tuple-element.24.w0_ref) | copy-start | bytes 1572868
  56.9 19.2 %copy-start.3 = (bf16[1024,256]{1,0:T(8,128)(2,1)S(1)}, bf16[1024,256]{1,0:T(8,128)(2,1)}, u32[]{:S(2)}) copy-start(bf16[1024,256]{1,0:T(8,128)(2,1)} %get-tuple-element.25.w1_ref) | copy-start | bytes 1572868
  56.9 19.2 %copy-start.4 = (bf16[1024,256]{1,0:T(8,128)(2,1)S(1)}, bf16[1024,256]{1,0:T(8,128)(2,1)}, u32[]{:S(2)}) copy-start(bf16[1024,256]{1,0:T(8,128)(2,1)} %get-tuple-element.26.w2_ref) | copy-start | bytes 1572868
  56.9 19.2 %copy-start.6 = (f32[512]{0:T(512)S(1)}, f32[512]{0:T(512)}, u32[]{:S(2)}) copy-start(f32[512]{0:T(512)} %param.16) | copy-start | bytes 6148
  76.2 1.0 copy-start.5
